TPU v7x, 768 devices: a whole 4x8x12 slice. The times are simulated.
768 devices in a mesh: seq: 48 (over y, z_lo), head: 16 (over z_hi, x, core).
Axes of the slice: x: 4, y: 8, z: 12 (z_hi: 2, z_lo: 6; z = z_hi * 6 + z_lo), core: 2. Of those that a mesh axis runs over, the one named last changes fastest.
Arguments:
- query_rows: bfloat16 [36864, 2048], P('seq', 'head'), may hold values from -6 to 6
- key_rows: bfloat16 [36864, 2048], P('seq', 'head'), may hold values from -6 to 6
- value_rows: bfloat16 [36864, 2048], P('seq', 'head'), may hold values from -6 to 6
- output_rows: bfloat16 [36864, 2048], P('seq', 'head'), may hold values from -6 to 6
- output_grad: bfloat16 [36864, 2048], P('seq', 'head'), may hold values from -6 to 6
- projection: bfloat16 [3, 2048, 3072], P(None, 'head'), may hold values from -0.078125 to 0.078125
- neighbours: int32 [96, 4], replicated, may hold values from 0 to 95, as said below
- counts: int32 [96], replicated, may hold values from 3 to 4, as said below
Outputs:
- input_grad: bfloat16 [36864, 3072], P('seq', 'head')
Inputs may be any that keep to these rules, and one draw needn't show every extreme that they name: `neighbours`: row t lists 4 different tiles: first t itself, then t - 1, then t + 1 (modulo 96); the others lie among tiles (t // 2 - 1) * 2 to (t // 2 + 2) * 2 - 1, taken modulo 96. `counts`: every tile uses at least its first three listed tiles; some tile uses all 4.
All inputs are finite; a program needn't handle non-finite values.
Results may differ from a plain program's by a relative error of at most 0.015.
Values may be sent and summed in bfloat16 or wider, within the bound.
No kernel may reach another device: no remote copies, remote signals or barrier semaphores. Data moves between devices by JAX's collectives and lax.ppermute only.
A program may use at most 32 MiB of HBM per device.

v0:
```python
import jax
import jax.numpy as jnp
from jax import lax
from jax.sharding import PartitionSpec as P

HD = 128
TILE = 384
NB = 4


def with_halo(cells, sides, width):
    for axis, dim in sides:
        count = lax.axis_size(axis)
        head = lax.slice_in_dim(cells, 0, width, axis=dim)
        tail = lax.slice_in_dim(cells, cells.shape[dim] - width, cells.shape[dim], axis=dim)
        cells = jnp.concatenate(
            [
                lax.ppermute(tail, axis, [(i, (i + 1) % count) for i in range(count)]),
                cells,
                lax.ppermute(head, axis, [((i + 1) % count, i) for i in range(count)]),
            ],
            axis=dim,
        )
    return cells


def passed_along(block, axis, distance):
    devices = range(lax.axis_size(axis))
    route = [((i - distance) % len(devices), i) for i in devices]
    return lax.ppermute(block, axis, route)


def head_split(rows, heads_dev):
    return rows.reshape(rows.shape[0] // TILE, TILE, heads_dev, HD)


def tile_scores(query_tile, near_keys, score_scale):
    return (
        jnp.einsum("ihd,jchd->hijc", query_tile, near_keys, preferred_element_type=jnp.float32)
        * score_scale
    )


def score_grads(softmax_weights, grad_tile, near_values, delta_tile, score_scale):
    prob_grad = jnp.einsum(
        "ihd,jchd->hijc", grad_tile, near_values, preferred_element_type=jnp.float32
    )
    return (
        softmax_weights.astype(jnp.float32)
        * (prob_grad - delta_tile[:, :, None, None])
        * score_scale
    ).astype(jnp.bfloat16)


def local(
    query_rows, key_rows, value_rows, output_rows, output_grad, projection, neighbours, counts
):
    seq_count = lax.axis_size("seq")
    place = lax.axis_index("seq")
    rows_dev = query_rows.shape[0]
    tiles_dev = rows_dev // TILE
    tiles_all = tiles_dev * seq_count
    heads_dev = query_rows.shape[1] // HD
    score_scale = HD ** (-0.5)
    first_tile = (place - 1) * tiles_dev
    window = with_halo(jnp.stack([key_rows, value_rows]), (("seq", 1),), rows_dev)
    key_window = window[0].reshape(3 * tiles_dev, TILE, heads_dev, HD)
    value_window = window[1].reshape(3 * tiles_dev, TILE, heads_dev, HD)
    queries = head_split(query_rows, heads_dev)
    grads_out = head_split(output_grad, heads_dev)
    outputs = head_split(output_rows, heads_dev)
    deltas = jnp.transpose(
        jnp.sum(grads_out.astype(jnp.float32) * outputs.astype(jnp.float32), axis=-1), (0, 2, 1)
    )
    slot_range = jnp.arange(NB)
    query_grads = []
    row_peaks = []
    row_totals = []
    key_acc = jnp.zeros((3 * tiles_dev, TILE, heads_dev, HD), jnp.float32)
    value_acc = jnp.zeros((3 * tiles_dev, TILE, heads_dev, HD), jnp.float32)
    for tile_at in range(tiles_dev):
        global_tile = place * tiles_dev + tile_at
        listed = neighbours[global_tile]
        is_live = slot_range < counts[global_tile]
        slots = (listed - first_tile) % tiles_all
        near_keys = key_window[slots]
        near_values = value_window[slots]
        live_mask = is_live[None, None, :, None]
        scores = jnp.where(
            live_mask, tile_scores(queries[tile_at], near_keys, score_scale), -jnp.inf
        )
        row_peak = jnp.max(scores, axis=(2, 3))
        raised = jnp.where(live_mask, jnp.exp(scores - row_peak[:, :, None, None]), 0.0)
        row_total = jnp.sum(raised, axis=(2, 3))
        softmax_weights = (raised / row_total[:, :, None, None]).astype(jnp.bfloat16)
        score_grad = score_grads(
            softmax_weights, grads_out[tile_at], near_values, deltas[tile_at], score_scale
        )
        query_grads.append(
            jnp.einsum(
                "hijc,jchd->ihd", score_grad, near_keys, preferred_element_type=jnp.float32
            ).astype(jnp.bfloat16)
        )
        row_peaks.append(row_peak)
        row_totals.append(row_total)
        key_acc = key_acc.at[slots].add(
            jnp.einsum(
                "hijc,ihd->jchd", score_grad, queries[tile_at], preferred_element_type=jnp.float32
            )
        )
        value_acc = value_acc.at[slots].add(
            jnp.einsum(
                "hijc,ihd->jchd",
                softmax_weights,
                grads_out[tile_at],
                preferred_element_type=jnp.float32,
            )
        )
    partials = jnp.stack([key_acc, value_acc])
    from_next = passed_along(partials[:, :tiles_dev].astype(jnp.bfloat16), "seq", -1).astype(
        jnp.float32
    )
    from_prev = passed_along(partials[:, 2 * tiles_dev :].astype(jnp.bfloat16), "seq", 1).astype(
        jnp.float32
    )
    owned = partials[:, tiles_dev : 2 * tiles_dev] + from_next + from_prev
    key_grads = owned[0].astype(jnp.bfloat16).reshape(rows_dev, heads_dev * HD)
    value_grads = owned[1].astype(jnp.bfloat16).reshape(rows_dev, heads_dev * HD)
    grad_stack = jnp.stack(
        [jnp.stack(query_grads).reshape(rows_dev, heads_dev * HD), key_grads, value_grads]
    )
    term = jnp.einsum("cik,ckm->im", grad_stack, projection, preferred_element_type=jnp.float32)
    return lax.psum_scatter(term.astype(jnp.bfloat16), "head", scatter_dimension=1, tiled=True)


def solution(mesh):
    in_specs = (
        P("seq", "head"),
        P("seq", "head"),
        P("seq", "head"),
        P("seq", "head"),
        P("seq", "head"),
        P(None, "head", None),
        P(),
        P(),
    )
    out_specs = P("seq", "head")
    return jax.shard_map(local, mesh=mesh, in_specs=in_specs, out_specs=out_specs, check_vma=False)
```

profile of v0, /device:TPU:6, one launch (start us, length us, event | category | flops | bytes accessed | tf_op | source)
XLA Modules:
  0.0 255.4 jit_solution(8709436877698455809)
XLA Ops:
  7.8 4.3 %collective-permute-start = (bf16[2,768,128]{2,1,0:T(8,128)(2,1)S(1)}, bf16[2,768,128]{2,1,0:T(8,128)(2,1)S(1)}, u32[]{:S(2)}, u32[]{:S(2)}) collective-permute-start(bf16[2,768,128]{2,1,0:T(8,128)(2,1)S(1)} %pad_maximum_fusion.2), channel_id=1, source_target_pairs={{0,16},{16,32},{32,48},{48,64},{64,80},{80,96},{96,112},{112,128},... | collective-permute-start | bytes 1179656 | tf_op jit(solution)/shard_map/ppermute | solution.py:18
  12.0 13.3 %collective-permute-start.1 = (bf16[2,768,128]{2,1,0:T(8,128)(2,1)S(1)}, bf16[2,768,128]{2,1,0:T(8,128)(2,1)S(1)}, u32[]{:S(2)}, u32[]{:S(2)}) collective-permute-start(bf16[2,768,128]{2,1,0:T(8,128)(2,1)S(1)} %pad_maximum_fusion.2), channel_id=1, source_target_pairs={{16,0},{32,16},{48,32},{64,48},{80,64},{96,80},{112,96},{128,112},... | collective-permute-start | bytes 1179656 | tf_op jit(solution)/shard_map/ppermute | solution.py:20
  26.3 1.4 fusion.53
  32.0 1.4 collective-permute-done
  35.7 1.9 gather_fusion.2
  37.6 1.4 gather_fusion.3
  39.0 1.7 gather_fusion
  40.7 2.6 %gather_fusion.1 = bf16[4,384,128]{2,1,0:T(8,128)(2,1)} fusion(bf16[6,384,128]{2,1,0:T(8,128)(2,1)} %bitcast.103, s32[1024]{0:T(1024)S(1)} %pad_clamp_fusion.1), kind=kCustom, calls=%fused_computation.1 | custom fusion | bytes 786448 | tf_op jit(solution)/shard_map/gather | solution.py:87
  48.2 1.4 fusion.11
  50.2 1.4 fusion.28
  52.1 1.4 fusion.34
  54.6 3.3 %scatter_fusion.2 = f32[6,384,128]{2,1,0:T(8,128)} fusion(f32[6,384,128]{2,1,0:T(8,128)} %broadcast.182.clone.1, s32[4]{0:T(128)S(1)} %get-tuple-element.21, f32[4,384,128]{2,1,0:T(8,128)} %fusion.11), kind=kCustom, calls=%fused_computation.6 | custom fusion | flops 196608 | bytes 2359312 | tf_op jit(solution)/shard_map/scatter-add | solution.py:111
  57.8 3.0 %scatter_fusion.3 = f32[6,384,128]{2,1,0:T(8,128)} fusion(f32[6,384,128]{2,1,0:T(8,128)} %scatter_fusion.2, s32[4]{0:T(128)S(1)} %get-tuple-element.22, f32[4,384,128]{2,1,0:T(8,128)S(1)} %fusion.9), kind=kCustom, calls=%fused_computation.7 | custom fusion | flops 196608 | bytes 2359312 | tf_op jit(solution)/shard_map/scatter-add | solution.py:111
  60.9 2.1 scatter_fusion
  63.0 2.1 scatter_fusion.1
  65.1 1.6 fusion
  67.7 11.3 %collective-permute-start.2 = (bf16[2,2,384,1,128]{4,2,1,3,0:T(8,128)(2,1)}, bf16[2,2,384,1,128]{4,2,1,3,0:T(8,128)(2,1)}, u32[]{:S(2)}, u32[]{:S(2)}) collective-permute-start(bf16[2,2,384,1,128]{4,2,1,3,0:T(8,128)(2,1)} %get-tuple-element.7), channel_id=1, source_target_pairs={{16,0},{32,16},{48,32},{64,48},{80,64},{96,80},{112,96},{128,112},... | collective-permute-start | bytes 1179656 | tf_op jit(solution)/shard_map/ppermute | solution.py:30
  78.9 1.9 collective-permute-start.3
  82.4 1.7 copy.18
  84.2 4.6 %collective-permute-done.2 = bf16[2,2,384,1,128]{4,2,1,3,0:T(8,128)(2,1)} collective-permute-done((bf16[2,2,384,1,128]{4,2,1,3,0:T(8,128)(2,1)}, bf16[2,2,384,1,128]{4,2,1,3,0:T(8,128)(2,1)}, u32[]{:S(2)}, u32[]{:S(2)}) %collective-permute-start.2) | collective-permute-done | bytes 393248 | tf_op jit(solution)/shard_map/ppermute | solution.py:30
  88.7 9.1 %collective-permute-done.3 = bf16[2,2,384,1,128]{4,2,1,3,0:T(8,128)(2,1)} collective-permute-done((bf16[2,2,384,1,128]{4,2,1,3,0:T(8,128)(2,1)}, bf16[2,2,384,1,128]{4,2,1,3,0:T(8,128)(2,1)}, u32[]{:S(2)}, u32[]{:S(2)}) %collective-permute-start.3) | collective-permute-done | bytes 393248 | tf_op jit(solution)/shard_map/ppermute | solution.py:30
  97.8 1.4 fusion.20
  99.2 4.3 %bitcast_convert_fusion = bf16[768,3072]{0,1:T(8,128)(2,1)} fusion(bf16[3,128,3072]{2,1,0:T(8,128)(2,1)S(1)} %copy-done, bf16[1,768,128]{2,1,0:T(8,128)(2,1)S(1)} %bitcast.112, bf16[1,768,128]{2,1,0:T(8,128)(2,1)S(1)} %bitcast.111, bf16[1,768,128]{2,1,0:T(8,128)(2,1)S(1)} %bitcast.110), kind=kOutput, calls=%fused_computation.8 | convolution fusion | flops 1814888448 | bytes 7667712 | tf_op jit(solution)/shard_map/cik,ckm->im/dot_general | solution.py:132
  103.6 145.0 %reduce-scatter.2.cloned.1.call-done = bf16[768,192]{0,1:T(8,128)(2,1)} async-done(((bf16[768,3072]{0,1:T(8,128)(2,1)}), bf16[768,192]{0,1:T(8,128)(2,1)}) %reduce-scatter.2.cloned.1.call-update) | async-done | bytes 294928 | tf_op jit(solution)/shard_map/reduce_scatter | solution.py:133
  (68 shorter events, 18.4 us)
Async XLA Ops:
  6.5 92.7 %copy-start = (bf16[3,128,3072]{2,1,0:T(8,128)(2,1)S(1)}, bf16[3,128,3072]{2,1,0:T(8,128)(2,1)}, u32[]{:S(2)}) copy-start(bf16[3,128,3072]{2,1,0:T(8,128)(2,1)} %param.13) | copy-start | bytes 7077892
  6.5 242.0 %reduce-scatter.2.cloned.1.call-start = ((), (), s32[]{:S(2)}) async-start(), calls=%async_computation.1 | async-start | bytes 5013504 | tf_op jit(solution)/shard_map/reduce_scatter | solution.py:133
  7.8 25.6 %collective-permute-start = (bf16[2,768,128]{2,1,0:T(8,128)(2,1)S(1)}, bf16[2,768,128]{2,1,0:T(8,128)(2,1)S(1)}, u32[]{:S(2)}, u32[]{:S(2)}) collective-permute-start(bf16[2,768,128]{2,1,0:T(8,128)(2,1)S(1)} %pad_maximum_fusion.2), channel_id=1, source_target_pairs={{0,16},{16,32},{32,48},{48,64},{64,80},{80,96},{96,112},{112,128},... | collective-permute-start | bytes 1179656 | tf_op jit(solution)/shard_map/ppermute | solution.py:18
  12.0 21.6 %collective-permute-start.1 = (bf16[2,768,128]{2,1,0:T(8,128)(2,1)S(1)}, bf16[2,768,128]{2,1,0:T(8,128)(2,1)S(1)}, u32[]{:S(2)}, u32[]{:S(2)}) collective-permute-start(bf16[2,768,128]{2,1,0:T(8,128)(2,1)S(1)} %pad_maximum_fusion.2), channel_id=1, source_target_pairs={{16,0},{32,16},{48,32},{64,48},{80,64},{96,80},{112,96},{128,112},... | collective-permute-start | bytes 1179656 | tf_op jit(solution)/shard_map/ppermute | solution.py:20
  34.8 8.5 %copy-start.10 = (bf16[768,128]{1,0:T(8,128)(2,1)S(1)}, bf16[768,128]{1,0:T(8,128)(2,1)}, u32[]{:S(2)}) copy-start(bf16[768,128]{1,0:T(8,128)(2,1)} %param.8) | copy-start | bytes 589828
  35.7 1.9 copy-start.9
  37.6 6.8 %copy-start.5 = (bf16[4,384,128]{2,1,0:T(8,128)(2,1)}, bf16[4,384,128]{2,1,0:T(8,128)(2,1)S(1)}, u32[]{:S(2)}) copy-start(bf16[4,384,128]{2,1,0:T(8,128)(2,1)S(1)} %gather_fusion.2) | copy-start | bytes 1179652
  39.0 5.4 %copy-start.16 = (pred[4]{0:T(512)(128)(4,1)S(1)}, pred[4]{0:T(512)(128)(4,1)}, u32[]{:S(2)}) copy-start(pred[4]{0:T(512)(128)(4,1)} %iota_compare_fusion) | copy-start | bytes 16
  40.7 5.0 %copy-start.7 = (bf16[4,384,128]{2,1,0:T(8,128)(2,1)}, bf16[4,384,128]{2,1,0:T(8,128)(2,1)S(1)}, u32[]{:S(2)}) copy-start(bf16[4,384,128]{2,1,0:T(8,128)(2,1)S(1)} %gather_fusion) | copy-start | bytes 1179652
  45.0 0.7 copy-start.15
  46.8 0.9 copy-start.11
  47.8 1.9 copy-start.13
  47.8 1.9 copy-start.18
  49.6 1.9 copy-start.12
  49.6 1.9 copy-start.17
  50.2 1.9 copy-start.1
  52.1 1.4 copy-start.3
  65.1 15.8 %copy-start.2 = (bf16[384,4,384]{0,2,1:T(8,128)(2,1)S(1)}, bf16[384,4,384]{0,2,1:T(8,128)(2,1)}, u32[]{:S(2)}) copy-start(bf16[384,4,384]{0,2,1:T(8,128)(2,1)} %copy-done.1) | copy-start | bytes 3538948
  65.1 15.8 %copy-start.6 = (bf16[4,384,128]{2,1,0:T(8,128)(2,1)S(1)}, bf16[4,384,128]{2,1,0:T(8,128)(2,1)}, u32[]{:S(2)}) copy-start(bf16[4,384,128]{2,1,0:T(8,128)(2,1)} %copy-done.5) | copy-start | bytes 1179652
  66.7 14.6 %copy-start.4 = (bf16[384,4,384]{0,2,1:T(8,128)(2,1)S(1)}, bf16[384,4,384]{0,2,1:T(8,128)(2,1)}, u32[]{:S(2)}) copy-start(bf16[384,4,384]{0,2,1:T(8,128)(2,1)} %copy-done.3) | copy-start | bytes 3538948
  66.7 14.6 %copy-start.8 = (bf16[4,384,128]{2,1,0:T(8,128)(2,1)S(1)}, bf16[4,384,128]{2,1,0:T(8,128)(2,1)}, u32[]{:S(2)}) copy-start(bf16[4,384,128]{2,1,0:T(8,128)(2,1)} %copy-done.7) | copy-start | bytes 1179652
  67.7 21.1 %collective-permute-start.2 = (bf16[2,2,384,1,128]{4,2,1,3,0:T(8,128)(2,1)}, bf16[2,2,384,1,128]{4,2,1,3,0:T(8,128)(2,1)}, u32[]{:S(2)}, u32[]{:S(2)}) collective-permute-start(bf16[2,2,384,1,128]{4,2,1,3,0:T(8,128)(2,1)} %get-tuple-element.7), channel_id=1, source_target_pairs={{16,0},{32,16},{48,32},{64,48},{80,64},{96,80},{112,96},{128,112},... | collective-permute-start | bytes 1179656 | tf_op jit(solution)/shard_map/ppermute | solution.py:30
  78.9 18.9 %collective-permute-start.3 = (bf16[2,2,384,1,128]{4,2,1,3,0:T(8,128)(2,1)}, bf16[2,2,384,1,128]{4,2,1,3,0:T(8,128)(2,1)}, u32[]{:S(2)}, u32[]{:S(2)}) collective-permute-start(bf16[2,2,384,1,128]{4,2,1,3,0:T(8,128)(2,1)} %get-tuple-element.8), channel_id=1, source_target_pairs={{752,0},{0,16},{16,32},{32,48},{48,64},{64,80},{80,96},{96,112},{1... | collective-permute-start | bytes 1179656 | tf_op jit(solution)/shard_map/ppermute | solution.py:30
  84.2 15.0 %copy-start.14 = (bf16[2,384,1,128]{3,1,0,2:T(8,128)(2,1)S(1)}, bf16[2,384,1,128]{3,1,0,2:T(8,128)(2,1)}, u32[]{:S(2)}) copy-start(bf16[2,384,1,128]{3,1,0,2:T(8,128)(2,1)} %copy.18) | copy-start | bytes 589828
Sparse Core Ops, SparseCore 0:
  103.7 144.8 reduce-scatter.1
where the time goes:
time: 256 us; the launch traced here: 255 us
  waiting for transfers between devices  160 us (62%)
  starting transfers between devices  30.7 us (12%)
  other arithmetic  23.6 us (9%)
  local copies, waits for them, and re-layouts  14.6 us (6%)
  between operations  13.7 us (5%)
  matrix products  12.3 us (5%)
    reduce_scatter x1, waiting for transfers between devices, local(): lax.psum_scatter(term.astype(jnp.bfloat16), 'head', scatter_dimension=1,...  145 us
    ppermute x2, waiting for transfers between devices, passed_along(): return lax.ppermute(block, axis, route)  13.6 us
    ppermute x1, starting transfers between devices, with_halo(): lax.ppermute(head, axis, [((i + 1) % count, i) for i in range(count)])  13.3 us
    ppermute x2, starting transfers between devices, passed_along(): return lax.ppermute(block, axis, route)  13.2 us
    scatter-add x2, other arithmetic, local(): value_acc.at[slots]  6.27 us
  transfers between devices with their start and end apart: 5, of which 5 were waited for; matrix products, arithmetic and copies ran while one was open for 4% of the time, Pallas kernels for 0%

commit v1 on v0

v1 whole, which is shorter than its diff:
```python
import jax
import jax.numpy as jnp
from jax import lax
from jax.sharding import Mesh
from jax.sharding import PartitionSpec as P

HD = 128
TILE = 384
NB = 4
HEAD_AXES = ("zh", "x", "c")


def with_halo(cells, axis, width):
    count = lax.axis_size(axis)
    head = lax.slice_in_dim(cells, 0, width, axis=1)
    tail = lax.slice_in_dim(cells, cells.shape[1] - width, cells.shape[1], axis=1)
    return jnp.concatenate(
        [
            lax.ppermute(tail, axis, [(i, (i + 1) % count) for i in range(count)]),
            cells,
            lax.ppermute(head, axis, [((i + 1) % count, i) for i in range(count)]),
        ],
        axis=1,
    )


def passed_along(block, axis, distance):
    devices = range(lax.axis_size(axis))
    route = [((i - distance) % len(devices), i) for i in devices]
    return lax.ppermute(block, axis, route)


def pick(array, axis, index):
    return lax.dynamic_index_in_dim(array, index, axis, keepdims=False)


def reduce_scatter(parts):
    c = lax.axis_index("c")
    x = lax.axis_index("x")
    zh = lax.axis_index("zh")
    n_c, n_x, n_zh = parts.shape[3], parts.shape[2], parts.shape[1]
    if n_c > 1:
        got = lax.ppermute(
            pick(parts, 3, 1 - c).astype(jnp.bfloat16), "c", [(0, 1), (1, 0)]
        )
        sums = pick(parts, 3, c) + got.astype(jnp.float32)
    else:
        sums = parts[:, :, :, 0]
    if n_x > 1:
        halves = [sums[:, z] for z in range(n_zh)]
        out = []
        for z, half in enumerate(halves):
            step = 1 if z % 2 == 0 else -1
            route = [(i, (i + step) % n_x) for i in range(n_x)]
            acc = pick(half, 1, (x - step) % n_x)
            for k in range(1, n_x):
                got = lax.ppermute(acc.astype(jnp.bfloat16), "x", route)
                acc = got.astype(jnp.float32) + pick(half, 1, (x - step * (1 + k)) % n_x)
            out.append(acc)
        sums = jnp.stack(out, axis=1)
    else:
        sums = sums[:, :, 0]
    if n_zh > 1:
        route = [(i, (i + 1) % n_zh) for i in range(n_zh)]
        acc = pick(sums, 1, (zh - 1) % n_zh)
        for k in range(1, n_zh):
            got = lax.ppermute(acc.astype(jnp.bfloat16), "zh", route)
            acc = got.astype(jnp.float32) + pick(sums, 1, (zh - 1 - k) % n_zh)
        return acc
    return sums[:, 0]


def local(
    query_rows, key_rows, value_rows, output_rows, output_grad, projection, neighbours, counts
):
    seq_count = lax.axis_size("seq")
    place = lax.axis_index("seq")
    rows_dev = query_rows.shape[0]
    tiles_dev = rows_dev // TILE
    tiles_all = tiles_dev * seq_count
    heads_dev = query_rows.shape[1] // HD
    win = 3 * tiles_dev
    score_scale = HD ** (-0.5)
    first_tile = (place - 1) * tiles_dev
    window = with_halo(jnp.stack([key_rows, value_rows]), "seq", rows_dev)
    key_window = window[0].reshape(win * TILE, heads_dev, HD)
    value_window = window[1].reshape(win * TILE, heads_dev, HD)
    queries = query_rows.reshape(tiles_dev, TILE, heads_dev, HD)
    grads_out = output_grad.reshape(tiles_dev, TILE, heads_dev, HD)
    outputs = output_rows.reshape(tiles_dev, TILE, heads_dev, HD)
    deltas = jnp.sum(grads_out.astype(jnp.float32) * outputs.astype(jnp.float32), axis=-1)
    slot_range = jnp.arange(NB)
    window_ids = jnp.arange(win)
    query_grads = []
    key_acc = jnp.zeros((win * TILE, heads_dev, HD), jnp.float32)
    value_acc = jnp.zeros((win * TILE, heads_dev, HD), jnp.float32)
    for tile_at in range(tiles_dev):
        global_tile = place * tiles_dev + tile_at
        listed = neighbours[global_tile]
        is_live = slot_range < counts[global_tile]
        slots = (listed - first_tile) % tiles_all
        used = jnp.any((slots[:, None] == window_ids[None, :]) & is_live[:, None], axis=0)
        live_mask = jnp.repeat(used, TILE)[None, None, :]
        scores = (
            jnp.einsum(
                "ihd,jhd->hij", queries[tile_at], key_window, preferred_element_type=jnp.float32
            )
            * score_scale
        )
        scores = jnp.where(live_mask, scores, -jnp.inf)
        row_peak = jnp.max(scores, axis=2)
        raised = jnp.where(live_mask, jnp.exp(scores - row_peak[:, :, None]), 0.0)
        row_total = jnp.sum(raised, axis=2)
        softmax_weights = (raised / row_total[:, :, None]).astype(jnp.bfloat16)
        prob_grad = jnp.einsum(
            "ihd,jhd->hij", grads_out[tile_at], value_window, preferred_element_type=jnp.float32
        )
        delta_tile = jnp.transpose(deltas[tile_at], (1, 0))
        score_grad = (
            softmax_weights.astype(jnp.float32)
            * (prob_grad - delta_tile[:, :, None])
            * score_scale
        ).astype(jnp.bfloat16)
        query_grads.append(
            jnp.einsum(
                "hij,jhd->ihd", score_grad, key_window, preferred_element_type=jnp.float32
            ).astype(jnp.bfloat16)
        )
        key_acc = key_acc + jnp.einsum(
            "hij,ihd->jhd", score_grad, queries[tile_at], preferred_element_type=jnp.float32
        )
        value_acc = value_acc + jnp.einsum(
            "hij,ihd->jhd", softmax_weights, grads_out[tile_at], preferred_element_type=jnp.float32
        )
    partials = jnp.stack([key_acc, value_acc])
    from_next = passed_along(partials[:, :rows_dev].astype(jnp.bfloat16), "seq", -1).astype(
        jnp.float32
    )
    from_prev = passed_along(
        partials[:, 2 * rows_dev :].astype(jnp.bfloat16), "seq", 1
    ).astype(jnp.float32)
    owned = partials[:, rows_dev : 2 * rows_dev] + from_next + from_prev
    key_grads = owned[0].astype(jnp.bfloat16).reshape(rows_dev, heads_dev * HD)
    value_grads = owned[1].astype(jnp.bfloat16).reshape(rows_dev, heads_dev * HD)
    grad_stack = jnp.stack(
        [jnp.stack(query_grads).reshape(rows_dev, heads_dev * HD), key_grads, value_grads]
    )
    n_zh, n_x, n_c = (lax.axis_size(a) for a in HEAD_AXES)
    width = projection.shape[2] // (n_zh * n_x * n_c)
    weight = projection.reshape(3, heads_dev * HD, n_zh, n_x, n_c, width)
    parts = jnp.einsum(
        "cik,ckzxym->izxym", grad_stack, weight, preferred_element_type=jnp.float32
    )
    return reduce_scatter(parts).astype(jnp.bfloat16)


def head_shape(n_head):
    n_c = 2 if n_head % 2 == 0 else 1
    n_x = 4 if (n_head // n_c) % 4 == 0 else n_head // n_c
    return n_head // (n_c * n_x), n_x, n_c


def solution(mesh):
    n_seq, n_head = mesh.devices.shape
    split = Mesh(mesh.devices.reshape((n_seq,) + head_shape(n_head)), ("seq",) + HEAD_AXES)
    rows = P("seq", HEAD_AXES)
    in_specs = (rows, rows, rows, rows, rows, P(None, HEAD_AXES, None), P(), P())
    return jax.shard_map(local, mesh=split, in_specs=in_specs, out_specs=rows, check_vma=False)
```

time: 256 us -> 158 us (0.62)
  the two profiles are of different devices: /device:TPU:6 before, /device:TPU:64 now
where the time goes in v1:
time: 158 us; the launch traced here: 157 us
  starting transfers between devices  57.6 us (36%)
  waiting for transfers between devices  56.8 us (36%)
  other arithmetic  19.5 us (12%)
  local copies, waits for them, and re-layouts  12.9 us (8%)
  matrix products  9.34 us (6%)
    ppermute x6, starting transfers between devices, reduce_scatter(): got = lax.ppermute(acc.astype(jnp.bfloat16), 'x', route)  25.2 us
    ppermute x1, waiting for transfers between devices, reduce_scatter(): got = lax.ppermute(acc.astype(jnp.bfloat16), 'zh', route)  18 us
    ppermute x6, waiting for transfers between devices, reduce_scatter(): got = lax.ppermute(acc.astype(jnp.bfloat16), 'x', route)  15.4 us
    ppermute x2, waiting for transfers between devices, passed_along(): return lax.ppermute(block, axis, route)  14.2 us
    unnamed x17, local copies, waits for them, and re-layouts  9.42 us
    ppermute x1, starting transfers between devices, reduce_scatter(): got = lax.ppermute(acc.astype(jnp.bfloat16), 'zh', route)  9.19 us
    ppermute x2, starting transfers between devices, passed_along(): return lax.ppermute(block, axis, route)  8.89 us
    ppermute x1, starting transfers between devices, with_halo(): lax.ppermute(head, axis, [((i + 1) % count, i) for i in range(count)])  8.19 us
  transfers between devices with their start and end apart: 12, of which 9 were waited for; matrix products, arithmetic and copies ran while one was open for 9% of the time, Pallas kernels for 0%

profile of v1, /device:TPU:64, one launch (start us, length us, event | category | flops | bytes accessed | tf_op | source)
XLA Modules:
  0.0 156.8 jit_solution(12778662814098922647)
XLA Ops:
  1.1 4.3 %collective-permute-start = (bf16[2,768,128]{2,1,0:T(8,128)(2,1)S(1)}, bf16[2,768,128]{2,1,0:T(8,128)(2,1)S(1)}, u32[]{:S(2)}, u32[]{:S(2)}) collective-permute-start(bf16[2,768,128]{2,1,0:T(8,128)(2,1)S(1)} %pad_maximum_fusion.2), channel_id=1, source_target_pairs={{0,16},{16,32},{32,48},{48,64},{64,80},{80,96},{96,112},{112,128},... | collective-permute-start | bytes 1179656 | tf_op jit(solution)/shard_map/ppermute | solution.py:19
  5.3 8.2 %collective-permute-start.1 = (bf16[2,768,128]{2,1,0:T(8,128)(2,1)S(1)}, bf16[2,768,128]{2,1,0:T(8,128)(2,1)S(1)}, u32[]{:S(2)}, u32[]{:S(2)}) collective-permute-start(bf16[2,768,128]{2,1,0:T(8,128)(2,1)S(1)} %pad_maximum_fusion.2), channel_id=1, source_target_pairs={{16,0},{32,16},{48,32},{64,48},{80,64},{96,80},{112,96},{128,112},... | collective-permute-start | bytes 1179656 | tf_op jit(solution)/shard_map/ppermute | solution.py:21
  17.7 4.4 %copy.14 = bf16[3,128,3072]{1,2,0:T(8,128)(2,1)} copy(bf16[3,128,3072]{2,1,0:T(8,128)(2,1)} %param.13) | data formatting | bytes 4718592 | tf_op args[5]
  22.2 4.6 %collective-permute-done.1 = bf16[2,768,128]{2,1,0:T(8,128)(2,1)S(1)} collective-permute-done((bf16[2,768,128]{2,1,0:T(8,128)(2,1)S(1)}, bf16[2,768,128]{2,1,0:T(8,128)(2,1)S(1)}, u32[]{:S(2)}, u32[]{:S(2)}) %collective-permute-start.1) | collective-permute-done | bytes 393248 | tf_op jit(solution)/shard_map/ppermute | solution.py:21
  39.1 6.8 %collective-permute-start.2 = (bf16[2,768,1,128]{3,1,2,0:T(8,128)(2,1)}, bf16[2,768,1,128]{3,1,2,0:T(8,128)(2,1)S(1)}, u32[]{:S(2)}, u32[]{:S(2)}) collective-permute-start(bf16[2,768,1,128]{3,1,2,0:T(8,128)(2,1)} %get-tuple-element.9), channel_id=1, source_target_pairs={{16,0},{32,16},{48,32},{64,48},{80,64},{96,80},{112,96},{128,112},... | collective-permute-start | bytes 1179656 | tf_op jit(solution)/shard_map/ppermute | solution.py:30
  45.9 2.1 %collective-permute-start.3 = (bf16[2,768,1,128]{3,1,2,0:T(8,128)(2,1)}, bf16[2,768,1,128]{3,1,2,0:T(8,128)(2,1)S(1)}, u32[]{:S(2)}, u32[]{:S(2)}) collective-permute-start(bf16[2,768,1,128]{3,1,2,0:T(8,128)(2,1)} %get-tuple-element.10), channel_id=1, source_target_pairs={{752,0},{0,16},{16,32},{32,48},{48,64},{64,80},{80,96},{96,112},{1... | collective-permute-start | bytes 1179656 | tf_op jit(solution)/shard_map/ppermute | solution.py:30
  49.2 4.4 %collective-permute-done.2 = bf16[2,768,1,128]{3,1,2,0:T(8,128)(2,1)S(1)} collective-permute-done((bf16[2,768,1,128]{3,1,2,0:T(8,128)(2,1)}, bf16[2,768,1,128]{3,1,2,0:T(8,128)(2,1)S(1)}, u32[]{:S(2)}, u32[]{:S(2)}) %collective-permute-start.2) | collective-permute-done | bytes 393248 | tf_op jit(solution)/shard_map/ppermute | solution.py:30
  53.6 9.8 %collective-permute-done.3 = bf16[2,768,1,128]{3,1,2,0:T(8,128)(2,1)S(1)} collective-permute-done((bf16[2,768,1,128]{3,1,2,0:T(8,128)(2,1)}, bf16[2,768,1,128]{3,1,2,0:T(8,128)(2,1)S(1)}, u32[]{:S(2)}, u32[]{:S(2)}) %collective-permute-start.3) | collective-permute-done | bytes 393248 | tf_op jit(solution)/shard_map/ppermute | solution.py:30
  63.6 2.7 %convolution_bitcast_fusion = f32[768,2,4,2,192]{0,4,3,2,1:T(8,128)S(1)} fusion(bf16[3,128,2,4,2,192]{1,5,4,3,2,0:T(8,128)(2,1)S(1)} %bitcast.115, bf16[1,768,128]{2,1,0:T(8,128)(2,1)S(1)} %get-tuple-element.12, bf16[1,768,128]{2,1,0:T(8,128)(2,1)S(1)} %get-tuple-element.11, bf16[1,768,128]{2,1,0:T(8,128)(2,1)S(1)} %bitcast.120), kind=kOutput, calls=%fused_computation.22 | convolution fusion | flops 1813708800 | bytes 12386304 | tf_op jit(solution)/shard_map/cik,ckzxym->izxym/dot_general | solution.py:151
  66.3 3.6 %copy-done.1 = f32[768,2,4,2,192]{0,4,3,2,1:T(8,128)} copy-done((f32[768,2,4,2,192]{0,4,3,2,1:T(8,128)}, f32[768,2,4,2,192]{0,4,3,2,1:T(8,128)S(1)}, u32[]{:S(2)}) %copy-start.1) | copy-done | bytes 9437208
  70.1 1.9 %collective-permute-start.4 = (bf16[768,2,4,192]{0,3,2,1:T(8,128)(2,1)S(1)}, bf16[768,2,4,192]{0,3,2,1:T(8,128)(2,1)}, u32[]{:S(2)}, u32[]{:S(2)}) collective-permute-start(bf16[768,2,4,192]{0,3,2,1:T(8,128)(2,1)S(1)} %fusion.13), channel_id=1, source_target_pairs={{0,1},{1,0},{2,3},{3,2},{4,5},{5,4},{6,7},{7,6},{8,9},{9,8},{10,11... | collective-permute-start | bytes 7077896 | tf_op jit(solution)/shard_map/ppermute | solution.py:43
  72.1 4.6 %collective-permute-done.4 = bf16[768,2,4,192]{0,3,2,1:T(8,128)(2,1)} collective-permute-done((bf16[768,2,4,192]{0,3,2,1:T(8,128)(2,1)S(1)}, bf16[768,2,4,192]{0,3,2,1:T(8,128)(2,1)}, u32[]{:S(2)}, u32[]{:S(2)}) %collective-permute-start.4) | collective-permute-done | bytes 2359328 | tf_op jit(solution)/shard_map/ppermute | solution.py:43
  76.7 3.7 %bitcast_add_fusion = f32[768,2,4,192]{0,3,2,1:T(8,128)S(1)} fusion(bf16[768,2,4,192]{0,3,2,1:T(8,128)(2,1)} %collective-permute-done.4, f32[768,2,4,2,192]{0,4,3,2,1:T(8,128)} %copy-done.1, s32[]{:T(128)S(6)} %select_n.135), kind=kLoop, calls=%fused_computation | loop fusion | flops 2359296 | bytes 11796484 | tf_op jit(solution)/shard_map/add | solution.py:46
  82.2 8.0 %collective-permute-start.8 = (bf16[768,192]{0,1:T(8,128)(2,1)S(1)}, bf16[768,192]{0,1:T(8,128)(2,1)}, u32[]{:S(2)}, u32[]{:S(2)}) collective-permute-start(bf16[768,192]{0,1:T(8,128)(2,1)S(1)} %fusion.39), channel_id=1, source_target_pairs={{0,6},{2,0},{4,2},{6,4},{1,7},{3,1},{5,3},{7,5},{8,14},{10,8},{12,... | collective-permute-start | bytes 884744 | tf_op jit(solution)/shard_map/ppermute | solution.py:57
  90.3 1.9 %collective-permute-start.5 = (bf16[768,192]{0,1:T(8,128)(2,1)S(1)}, bf16[768,192]{0,1:T(8,128)(2,1)S(1)}, u32[]{:S(2)}, u32[]{:S(2)}) collective-permute-start(bf16[768,192]{0,1:T(8,128)(2,1)S(1)} %fusion.38), channel_id=1, source_target_pairs={{0,2},{2,4},{4,6},{6,0},{1,3},{3,5},{5,7},{7,1},{8,10},{10,12},{12... | collective-permute-start | bytes 884744 | tf_op jit(solution)/shard_map/ppermute | solution.py:57
  92.3 4.5 %collective-permute-done.8 = bf16[768,192]{0,1:T(8,128)(2,1)} collective-permute-done((bf16[768,192]{0,1:T(8,128)(2,1)S(1)}, bf16[768,192]{0,1:T(8,128)(2,1)}, u32[]{:S(2)}, u32[]{:S(2)}) %collective-permute-start.8) | collective-permute-done | bytes 294944 | tf_op jit(solution)/shard_map/ppermute | solution.py:57
  98.0 5.7 %collective-permute-start.9 = (bf16[768,192]{0,1:T(8,128)(2,1)S(1)}, bf16[768,192]{0,1:T(8,128)(2,1)}, u32[]{:S(2)}, u32[]{:S(2)}) collective-permute-start(bf16[768,192]{0,1:T(8,128)(2,1)S(1)} %fusion.34), channel_id=1, source_target_pairs={{0,6},{2,0},{4,2},{6,4},{1,7},{3,1},{5,3},{7,5},{8,14},{10,8},{12,... | collective-permute-start | bytes 884744 | tf_op jit(solution)/shard_map/ppermute | solution.py:57
  103.8 1.9 %collective-permute-start.6 = (bf16[768,192]{0,1:T(8,128)(2,1)S(1)}, bf16[768,192]{0,1:T(8,128)(2,1)}, u32[]{:S(2)}, u32[]{:S(2)}) collective-permute-start(bf16[768,192]{0,1:T(8,128)(2,1)S(1)} %fusion.37), channel_id=1, source_target_pairs={{0,2},{2,4},{4,6},{6,0},{1,3},{3,5},{5,7},{7,1},{8,10},{10,12},{12... | collective-permute-start | bytes 884744 | tf_op jit(solution)/shard_map/ppermute | solution.py:57
  105.7 3.6 %collective-permute-done.9 = bf16[768,192]{0,1:T(8,128)(2,1)} collective-permute-done((bf16[768,192]{0,1:T(8,128)(2,1)S(1)}, bf16[768,192]{0,1:T(8,128)(2,1)}, u32[]{:S(2)}, u32[]{:S(2)}) %collective-permute-start.9) | collective-permute-done | bytes 294944 | tf_op jit(solution)/shard_map/ppermute | solution.py:57
  110.6 5.7 %collective-permute-start.10 = (bf16[768,192]{0,1:T(8,128)(2,1)S(1)}, bf16[768,192]{0,1:T(8,128)(2,1)S(1)}, u32[]{:S(2)}, u32[]{:S(2)}) collective-permute-start(bf16[768,192]{0,1:T(8,128)(2,1)S(1)} %fusion.33), channel_id=1, source_target_pairs={{0,6},{2,0},{4,2},{6,4},{1,7},{3,1},{5,3},{7,5},{8,14},{10,8},{12,... | collective-permute-start | bytes 884744 | tf_op jit(solution)/shard_map/ppermute | solution.py:57
  117.3 1.9 %collective-permute-start.7 = (bf16[768,192]{0,1:T(8,128)(2,1)S(1)}, bf16[768,192]{0,1:T(8,128)(2,1)}, u32[]{:S(2)}, u32[]{:S(2)}) collective-permute-start(bf16[768,192]{0,1:T(8,128)(2,1)S(1)} %fusion.36), channel_id=1, source_target_pairs={{0,2},{2,4},{4,6},{6,0},{1,3},{3,5},{5,7},{7,1},{8,10},{10,12},{12... | collective-permute-start | bytes 884744 | tf_op jit(solution)/shard_map/ppermute | solution.py:57
  122.2 5.4 %collective-permute-done.7 = bf16[768,192]{0,1:T(8,128)(2,1)} collective-permute-done((bf16[768,192]{0,1:T(8,128)(2,1)S(1)}, bf16[768,192]{0,1:T(8,128)(2,1)}, u32[]{:S(2)}, u32[]{:S(2)}) %collective-permute-start.7) | collective-permute-done | bytes 294944 | tf_op jit(solution)/shard_map/ppermute | solution.py:57
  128.7 9.2 %collective-permute-start.11 = (bf16[768,192]{0,1:T(8,128)(2,1)S(1)}, bf16[768,192]{0,1:T(8,128)(2,1)S(1)}, u32[]{:S(2)}, u32[]{:S(2)}) collective-permute-start(bf16[768,192]{0,1:T(8,128)(2,1)S(1)} %fusion.40), channel_id=1, source_target_pairs={{0,8},{8,0},{1,9},{9,1},{2,10},{10,2},{3,11},{11,3},{4,12},{12,4},... | collective-permute-start | bytes 884744 | tf_op jit(solution)/shard_map/ppermute | solution.py:67
  138.0 18.0 %collective-permute-done.11 = bf16[768,192]{0,1:T(8,128)(2,1)S(1)} collective-permute-done((bf16[768,192]{0,1:T(8,128)(2,1)S(1)}, bf16[768,192]{0,1:T(8,128)(2,1)S(1)}, u32[]{:S(2)}, u32[]{:S(2)}) %collective-permute-start.11) | collective-permute-done | bytes 294944 | tf_op jit(solution)/shard_map/ppermute | solution.py:67
  (66 shorter events, 29.2 us)
Async XLA Ops:
  1.1 21.2 %collective-permute-start = (bf16[2,768,128]{2,1,0:T(8,128)(2,1)S(1)}, bf16[2,768,128]{2,1,0:T(8,128)(2,1)S(1)}, u32[]{:S(2)}, u32[]{:S(2)}) collective-permute-start(bf16[2,768,128]{2,1,0:T(8,128)(2,1)S(1)} %pad_maximum_fusion.2), channel_id=1, source_target_pairs={{0,16},{16,32},{32,48},{48,64},{64,80},{80,96},{96,112},{112,128},... | collective-permute-start | bytes 1179656 | tf_op jit(solution)/shard_map/ppermute | solution.py:19
  5.3 21.5 %collective-permute-start.1 = (bf16[2,768,128]{2,1,0:T(8,128)(2,1)S(1)}, bf16[2,768,128]{2,1,0:T(8,128)(2,1)S(1)}, u32[]{:S(2)}, u32[]{:S(2)}) collective-permute-start(bf16[2,768,128]{2,1,0:T(8,128)(2,1)S(1)} %pad_maximum_fusion.2), channel_id=1, source_target_pairs={{16,0},{32,16},{48,32},{64,48},{80,64},{96,80},{112,96},{128,112},... | collective-permute-start | bytes 1179656 | tf_op jit(solution)/shard_map/ppermute | solution.py:21
  17.6 4.4 %copy-start.3 = (bf16[768,128]{1,0:T(8,128)(2,1)S(1)}, bf16[768,128]{1,0:T(8,128)(2,1)}, u32[]{:S(2)}) copy-start(bf16[768,128]{1,0:T(8,128)(2,1)} %param.12) | copy-start | bytes 589828
  17.6 4.4 %copy-start.7 = (bf16[768,128]{1,0:T(8,128)(2,1)S(1)}, bf16[768,128]{1,0:T(8,128)(2,1)}, u32[]{:S(2)}) copy-start(bf16[768,128]{1,0:T(8,128)(2,1)} %param.11) | copy-start | bytes 589828
  17.6 9.2 %copy-start.4 = (bf16[768,128]{1,0:T(8,128)(2,1)S(1)}, bf16[768,128]{1,0:T(8,128)(2,1)}, u32[]{:S(2)}) copy-start(bf16[768,128]{1,0:T(8,128)(2,1)} %param.10) | copy-start | bytes 589828
  17.7 9.2 %copy-start.5 = (bf16[768,128]{1,0:T(8,128)(2,1)S(1)}, bf16[768,128]{1,0:T(8,128)(2,1)}, u32[]{:S(2)}) copy-start(bf16[768,128]{1,0:T(8,128)(2,1)} %param.9) | copy-start | bytes 589828
  22.0 5.0 %copy-start.6 = (bf16[768,128]{1,0:T(8,128)(2,1)S(1)}, bf16[768,128]{1,0:T(8,128)(2,1)}, u32[]{:S(2)}) copy-start(bf16[768,128]{1,0:T(8,128)(2,1)} %param.8) | copy-start | bytes 589828
  39.1 14.6 %collective-permute-start.2 = (bf16[2,768,1,128]{3,1,2,0:T(8,128)(2,1)}, bf16[2,768,1,128]{3,1,2,0:T(8,128)(2,1)S(1)}, u32[]{:S(2)}, u32[]{:S(2)}) collective-permute-start(bf16[2,768,1,128]{3,1,2,0:T(8,128)(2,1)} %get-tuple-element.9), channel_id=1, source_target_pairs={{16,0},{32,16},{48,32},{64,48},{80,64},{96,80},{112,96},{128,112},... | collective-permute-start | bytes 1179656 | tf_op jit(solution)/shard_map/ppermute | solution.py:30
  45.9 17.5 %collective-permute-start.3 = (bf16[2,768,1,128]{3,1,2,0:T(8,128)(2,1)}, bf16[2,768,1,128]{3,1,2,0:T(8,128)(2,1)S(1)}, u32[]{:S(2)}, u32[]{:S(2)}) collective-permute-start(bf16[2,768,1,128]{3,1,2,0:T(8,128)(2,1)} %get-tuple-element.10), channel_id=1, source_target_pairs={{752,0},{0,16},{16,32},{32,48},{48,64},{64,80},{80,96},{96,112},{1... | collective-permute-start | bytes 1179656 | tf_op jit(solution)/shard_map/ppermute | solution.py:30
  49.2 14.4 %copy-start.2 = (bf16[3,128,3072]{1,2,0:T(8,128)(2,1)S(1)}, bf16[3,128,3072]{1,2,0:T(8,128)(2,1)}, u32[]{:S(2)}) copy-start(bf16[3,128,3072]{1,2,0:T(8,128)(2,1)} %copy.14) | copy-start | bytes 7077892
  66.2 3.6 %copy-start.1 = (f32[768,2,4,2,192]{0,4,3,2,1:T(8,128)}, f32[768,2,4,2,192]{0,4,3,2,1:T(8,128)S(1)}, u32[]{:S(2)}) copy-start(f32[768,2,4,2,192]{0,4,3,2,1:T(8,128)S(1)} %convolution_bitcast_fusion) | copy-start | bytes 28311556
  70.1 6.6 %collective-permute-start.4 = (bf16[768,2,4,192]{0,3,2,1:T(8,128)(2,1)S(1)}, bf16[768,2,4,192]{0,3,2,1:T(8,128)(2,1)}, u32[]{:S(2)}, u32[]{:S(2)}) collective-permute-start(bf16[768,2,4,192]{0,3,2,1:T(8,128)(2,1)S(1)} %fusion.13), channel_id=1, source_target_pairs={{0,1},{1,0},{2,3},{3,2},{4,5},{5,4},{6,7},{7,6},{8,9},{9,8},{10,11... | collective-permute-start | bytes 7077896 | tf_op jit(solution)/shard_map/ppermute | solution.py:43
  80.8 1.4 copy-start
  82.2 14.5 %collective-permute-start.8 = (bf16[768,192]{0,1:T(8,128)(2,1)S(1)}, bf16[768,192]{0,1:T(8,128)(2,1)}, u32[]{:S(2)}, u32[]{:S(2)}) collective-permute-start(bf16[768,192]{0,1:T(8,128)(2,1)S(1)} %fusion.39), channel_id=1, source_target_pairs={{0,6},{2,0},{4,2},{6,4},{1,7},{3,1},{5,3},{7,5},{8,14},{10,8},{12,... | collective-permute-start | bytes 884744 | tf_op jit(solution)/shard_map/ppermute | solution.py:57
  90.3 13.4 %collective-permute-start.5 = (bf16[768,192]{0,1:T(8,128)(2,1)S(1)}, bf16[768,192]{0,1:T(8,128)(2,1)S(1)}, u32[]{:S(2)}, u32[]{:S(2)}) collective-permute-start(bf16[768,192]{0,1:T(8,128)(2,1)S(1)} %fusion.38), channel_id=1, source_target_pairs={{0,2},{2,4},{4,6},{6,0},{1,3},{3,5},{5,7},{7,1},{8,10},{10,12},{12... | collective-permute-start | bytes 884744 | tf_op jit(solution)/shard_map/ppermute | solution.py:57
  98.0 11.4 %collective-permute-start.9 = (bf16[768,192]{0,1:T(8,128)(2,1)S(1)}, bf16[768,192]{0,1:T(8,128)(2,1)}, u32[]{:S(2)}, u32[]{:S(2)}) collective-permute-start(bf16[768,192]{0,1:T(8,128)(2,1)S(1)} %fusion.34), channel_id=1, source_target_pairs={{0,6},{2,0},{4,2},{6,4},{1,7},{3,1},{5,3},{7,5},{8,14},{10,8},{12,... | collective-permute-start | bytes 884744 | tf_op jit(solution)/shard_map/ppermute | solution.py:57
  103.8 12.5 %collective-permute-start.6 = (bf16[768,192]{0,1:T(8,128)(2,1)S(1)}, bf16[768,192]{0,1:T(8,128)(2,1)}, u32[]{:S(2)}, u32[]{:S(2)}) collective-permute-start(bf16[768,192]{0,1:T(8,128)(2,1)S(1)} %fusion.37), channel_id=1, source_target_pairs={{0,2},{2,4},{4,6},{6,0},{1,3},{3,5},{5,7},{7,1},{8,10},{10,12},{12... | collective-permute-start | bytes 884744 | tf_op jit(solution)/shard_map/ppermute | solution.py:57
  110.6 10.5 %collective-permute-start.10 = (bf16[768,192]{0,1:T(8,128)(2,1)S(1)}, bf16[768,192]{0,1:T(8,128)(2,1)S(1)}, u32[]{:S(2)}, u32[]{:S(2)}) collective-permute-start(bf16[768,192]{0,1:T(8,128)(2,1)S(1)} %fusion.33), channel_id=1, source_target_pairs={{0,6},{2,0},{4,2},{6,4},{1,7},{3,1},{5,3},{7,5},{8,14},{10,8},{12,... | collective-permute-start | bytes 884744 | tf_op jit(solution)/shard_map/ppermute | solution.py:57
  117.3 10.3 %collective-permute-start.7 = (bf16[768,192]{0,1:T(8,128)(2,1)S(1)}, bf16[768,192]{0,1:T(8,128)(2,1)}, u32[]{:S(2)}, u32[]{:S(2)}) collective-permute-start(bf16[768,192]{0,1:T(8,128)(2,1)S(1)} %fusion.36), channel_id=1, source_target_pairs={{0,2},{2,4},{4,6},{6,0},{1,3},{3,5},{5,7},{7,1},{8,10},{10,12},{12... | collective-permute-start | bytes 884744 | tf_op jit(solution)/shard_map/ppermute | solution.py:57
  128.7 27.2 %collective-permute-start.11 = (bf16[768,192]{0,1:T(8,128)(2,1)S(1)}, bf16[768,192]{0,1:T(8,128)(2,1)S(1)}, u32[]{:S(2)}, u32[]{:S(2)}) collective-permute-start(bf16[768,192]{0,1:T(8,128)(2,1)S(1)} %fusion.40), channel_id=1, source_target_pairs={{0,8},{8,0},{1,9},{9,1},{2,10},{10,2},{3,11},{11,3},{4,12},{12,4},... | collective-permute-start | bytes 884744 | tf_op jit(solution)/shard_map/ppermute | solution.py:67

commit v2 on v1

v2 whole, which is shorter than its diff:
```python
import jax
import jax.numpy as jnp
from jax import lax
from jax.experimental import pallas as pl
from jax.experimental.pallas import tpu as pltpu
from jax.sharding import Mesh
from jax.sharding import PartitionSpec as P

HD = 128
TILE = 384
NB = 4
HEAD_AXES = ("zh", "x", "c")


def with_halo(cells, axis, width):
    count = lax.axis_size(axis)
    head = lax.slice_in_dim(cells, 0, width, axis=1)
    tail = lax.slice_in_dim(cells, cells.shape[1] - width, cells.shape[1], axis=1)
    return jnp.concatenate(
        [
            lax.ppermute(tail, axis, [(i, (i + 1) % count) for i in range(count)]),
            cells,
            lax.ppermute(head, axis, [((i + 1) % count, i) for i in range(count)]),
        ],
        axis=1,
    )


def passed_along(block, axis, distance):
    devices = range(lax.axis_size(axis))
    route = [((i - distance) % len(devices), i) for i in devices]
    return lax.ppermute(block, axis, route)


def pick(array, axis, index):
    return lax.dynamic_index_in_dim(array, index, axis, keepdims=False)


def ring_scatter(block, route_sign, n_x):
    x = lax.axis_index("x")
    rows = block.shape[0]
    halves = [block[: rows // 2], block[rows // 2 :]]
    out = []
    for h, half in enumerate(halves):
        step = route_sign if h == 0 else -route_sign
        route = [(i, (i + step) % n_x) for i in range(n_x)]
        acc = pick(half, 1, (x - step) % n_x)
        for k in range(1, n_x):
            got = lax.ppermute(acc.astype(jnp.bfloat16), "x", route)
            acc = got.astype(jnp.float32) + pick(half, 1, (x - step * (1 + k)) % n_x)
        out.append(acc)
    return jnp.concatenate(out, axis=0)


def reduce_scatter(parts):
    c = lax.axis_index("c")
    zh = lax.axis_index("zh")
    n_c, n_x, n_zh = parts.shape[3], parts.shape[2], parts.shape[1]
    if n_c > 1:
        got = lax.ppermute(
            pick(parts, 3, 1 - c).astype(jnp.bfloat16), "c", [(0, 1), (1, 0)]
        )
        sums = pick(parts, 3, c) + got.astype(jnp.float32)
    else:
        sums = parts[:, :, :, 0]
    if n_zh == 2 and n_x > 1:
        sent = ring_scatter(pick(sums, 1, 1 - zh), 1, n_x).astype(jnp.bfloat16)
        sent, later = lax.optimization_barrier((sent, pick(sums, 1, zh)))
        got = lax.ppermute(sent, "zh", [(0, 1), (1, 0)])
        kept = ring_scatter(later, -1, n_x)
        return kept + got.astype(jnp.float32)
    if n_x > 1:
        sums = jnp.stack([ring_scatter(sums[:, z], 1, n_x) for z in range(n_zh)], axis=1)
    else:
        sums = sums[:, :, 0]
    if n_zh > 1:
        route = [(i, (i + 1) % n_zh) for i in range(n_zh)]
        acc = pick(sums, 1, (zh - 1) % n_zh)
        for k in range(1, n_zh):
            got = lax.ppermute(acc.astype(jnp.bfloat16), "zh", route)
            acc = got.astype(jnp.float32) + pick(sums, 1, (zh - 1 - k) % n_zh)
        return acc
    return sums[:, 0]


def attention_kernel(q_ref, do_ref, o_ref, k_ref, v_ref, mask_ref, dq_ref, dk_ref, dv_ref):
    tile_at = pl.program_id(0)
    score_scale = HD ** (-0.5)
    queries = q_ref[...]
    grads = do_ref[...]
    keys = k_ref[...]
    values = v_ref[...]
    live = mask_ref[0] > 0.0
    contract_last = (((1,), (1,)), ((), ()))
    contract_first = (((0,), (0,)), ((), ()))
    scores = lax.dot_general(queries, keys, contract_last, preferred_element_type=jnp.float32)
    scores = jnp.where(live, scores * score_scale, -jnp.inf)
    row_peak = jnp.max(scores, axis=1, keepdims=True)
    raised = jnp.where(live, jnp.exp(scores - row_peak), 0.0)
    row_total = jnp.sum(raised, axis=1, keepdims=True)
    weights = (raised / row_total).astype(jnp.bfloat16)
    delta = jnp.sum(
        grads.astype(jnp.float32) * o_ref[...].astype(jnp.float32), axis=1, keepdims=True
    )
    prob_grad = lax.dot_general(grads, values, contract_last, preferred_element_type=jnp.float32)
    score_grad = (weights.astype(jnp.float32) * (prob_grad - delta) * score_scale).astype(
        jnp.bfloat16
    )
    dq_ref[...] = jnp.dot(score_grad, keys, preferred_element_type=jnp.float32).astype(
        dq_ref.dtype
    )
    key_part = lax.dot_general(score_grad, queries, contract_first, preferred_element_type=jnp.float32)
    value_part = lax.dot_general(weights, grads, contract_first, preferred_element_type=jnp.float32)

    @pl.when(tile_at == 0)
    def _():
        dk_ref[...] = key_part
        dv_ref[...] = value_part

    @pl.when(tile_at > 0)
    def _():
        dk_ref[...] += key_part
        dv_ref[...] += value_part


def attention(queries, grads, outputs, keys, values, mask):
    rows = queries.shape[0]
    keys_n = keys.shape[0]
    tiles = rows // TILE
    row_spec = pl.BlockSpec((TILE, HD), lambda t: (t, 0))
    whole = pl.BlockSpec((keys_n, HD), lambda t: (0, 0))
    flops = 10 * rows * keys_n * HD
    return pl.pallas_call(
        attention_kernel,
        grid=(tiles,),
        in_specs=[
            row_spec,
            row_spec,
            row_spec,
            whole,
            whole,
            pl.BlockSpec((1, 1, keys_n), lambda t: (t, 0, 0)),
        ],
        out_specs=[row_spec, whole, whole],
        out_shape=[
            jax.ShapeDtypeStruct((rows, HD), jnp.bfloat16),
            jax.ShapeDtypeStruct((keys_n, HD), jnp.float32),
            jax.ShapeDtypeStruct((keys_n, HD), jnp.float32),
        ],
        compiler_params=pltpu.CompilerParams(
            dimension_semantics=("arbitrary",), vmem_limit_bytes=48 * 1024 * 1024
        ),
        cost_estimate=pl.CostEstimate(
            flops=flops,
            transcendentals=rows * keys_n,
            bytes_accessed=2 * (3 * rows * HD + 2 * keys_n * HD) + 8 * keys_n * HD,
        ),
    )(queries, grads, outputs, keys, values, mask)


def local(
    query_rows, key_rows, value_rows, output_rows, output_grad, projection, neighbours, counts
):
    seq_count = lax.axis_size("seq")
    place = lax.axis_index("seq")
    rows_dev = query_rows.shape[0]
    tiles_dev = rows_dev // TILE
    tiles_all = tiles_dev * seq_count
    heads_dev = query_rows.shape[1] // HD
    win = 3 * tiles_dev
    score_scale = HD ** (-0.5)
    first_tile = (place - 1) * tiles_dev
    window = with_halo(jnp.stack([key_rows, value_rows]), "seq", rows_dev)
    key_window = window[0].reshape(win * TILE, heads_dev, HD)
    value_window = window[1].reshape(win * TILE, heads_dev, HD)
    slot_range = jnp.arange(NB)
    window_ids = jnp.arange(win)
    masks = []
    for tile_at in range(tiles_dev):
        global_tile = place * tiles_dev + tile_at
        listed = neighbours[global_tile]
        is_live = slot_range < counts[global_tile]
        slots = (listed - first_tile) % tiles_all
        used = jnp.any((slots[:, None] == window_ids[None, :]) & is_live[:, None], axis=0)
        masks.append(jnp.repeat(used, TILE).astype(jnp.float32))
    mask = jnp.stack(masks)[:, None, :]
    query_grads, key_accs, value_accs = [], [], []
    for head_at in range(heads_dev):
        cols = slice(head_at * HD, (head_at + 1) * HD)
        dq, dk, dv = attention(
            query_rows[:, cols],
            output_grad[:, cols],
            output_rows[:, cols],
            key_window[:, head_at],
            value_window[:, head_at],
            mask,
        )
        query_grads.append(dq)
        key_accs.append(dk)
        value_accs.append(dv)
    key_acc = jnp.stack(key_accs, axis=1)
    value_acc = jnp.stack(value_accs, axis=1)
    partials = jnp.stack([key_acc, value_acc])
    from_next = passed_along(partials[:, :rows_dev].astype(jnp.bfloat16), "seq", -1).astype(
        jnp.float32
    )
    from_prev = passed_along(
        partials[:, 2 * rows_dev :].astype(jnp.bfloat16), "seq", 1
    ).astype(jnp.float32)
    owned = partials[:, rows_dev : 2 * rows_dev] + from_next + from_prev
    key_grads = owned[0].astype(jnp.bfloat16).reshape(rows_dev, heads_dev * HD)
    value_grads = owned[1].astype(jnp.bfloat16).reshape(rows_dev, heads_dev * HD)
    grad_stack = jnp.stack(
        [jnp.concatenate(query_grads, axis=1), key_grads, value_grads]
    )
    n_zh, n_x, n_c = (lax.axis_size(a) for a in HEAD_AXES)
    width = projection.shape[2] // (n_zh * n_x * n_c)
    weight = projection.reshape(3, heads_dev * HD, n_zh, n_x, n_c, width)
    parts = jnp.einsum(
        "cik,ckzxym->izxym", grad_stack, weight, preferred_element_type=jnp.float32
    )
    return reduce_scatter(parts).astype(jnp.bfloat16)


def head_shape(n_head):
    n_c = 2 if n_head % 2 == 0 else 1
    n_x = 4 if (n_head // n_c) % 4 == 0 else n_head // n_c
    return n_head // (n_c * n_x), n_x, n_c


def solution(mesh):
    n_seq, n_head = mesh.devices.shape
    split = Mesh(mesh.devices.reshape((n_seq,) + head_shape(n_head)), ("seq",) + HEAD_AXES)
    rows = P("seq", HEAD_AXES)
    in_specs = (rows, rows, rows, rows, rows, P(None, HEAD_AXES, None), P(), P())
    return jax.shard_map(local, mesh=split, in_specs=in_specs, out_specs=rows, check_vma=False)
```

time: 158 us -> 167 us (1.057)
  the two profiles are of different devices: /device:TPU:64 before, /device:TPU:32 now
where the time goes in v2:
time: 167 us; the launch traced here: 166 us
  starting transfers between devices  83.6 us (50%)
  waiting for transfers between devices  43.1 us (26%)
  local copies, waits for them, and re-layouts  15 us (9%)
  other arithmetic  13.8 us (8%)
  Pallas kernels  7.5 us (4%)
  matrix products  2.65 us (2%)
    ppermute x12, starting transfers between devices, ring_scatter(): got = lax.ppermute(acc.astype(jnp.bfloat16), 'x', route)  44 us
    ppermute x12, waiting for transfers between devices, ring_scatter(): got = lax.ppermute(acc.astype(jnp.bfloat16), 'x', route)  19 us
    ppermute x1, starting transfers between devices, reduce_scatter(): got = lax.ppermute(sent, 'zh', [(0, 1), (1, 0)])  12.8 us
    ppermute x2, waiting for transfers between devices, passed_along(): return lax.ppermute(block, axis, route)  12.4 us
    ppermute x2, starting transfers between devices, passed_along(): return lax.ppermute(block, axis, route)  10.4 us
    unnamed x17, local copies, waits for them, and re-layouts  10.3 us
    ppermute x1, starting transfers between devices, with_halo(): lax.ppermute(head, axis, [((i + 1) % count, i) for i in range(count)])  10.3 us
    pallas_call x1, Pallas kernels, attention(): pl.pallas_call(attention_kernel, grid=(tiles,), in_specs=[row_spec, row_s...  7.5 us
  transfers between devices with their start and end apart: 18, of which 13 were waited for; matrix products, arithmetic and copies ran while one was open for 7% of the time, Pallas kernels for 0%

profile of v2, /device:TPU:32, one launch (start us, length us, event | category | flops | bytes accessed | tf_op | source)
XLA Modules:
  0.0 166.4 jit_solution(2579741063813627443)
XLA Ops:
  1.1 4.3 %collective-permute-start = (bf16[2,768,128]{2,1,0:T(8,128)(2,1)S(1)}, bf16[2,768,128]{2,1,0:T(8,128)(2,1)S(1)}, u32[]{:S(2)}, u32[]{:S(2)}) collective-permute-start(bf16[2,768,128]{2,1,0:T(8,128)(2,1)S(1)} %pad_maximum_fusion.2), channel_id=1, source_target_pairs={{0,16},{16,32},{32,48},{48,64},{64,80},{80,96},{96,112},{112,128},... | collective-permute-start | bytes 1179656 | tf_op jit(solution)/shard_map/ppermute | solution.py:21
  5.3 10.3 %collective-permute-start.1 = (bf16[2,768,128]{2,1,0:T(8,128)(2,1)S(1)}, bf16[2,768,128]{2,1,0:T(8,128)(2,1)S(1)}, u32[]{:S(2)}, u32[]{:S(2)}) collective-permute-start(bf16[2,768,128]{2,1,0:T(8,128)(2,1)S(1)} %pad_maximum_fusion.2), channel_id=1, source_target_pairs={{16,0},{32,16},{48,32},{64,48},{80,64},{96,80},{112,96},{128,112},... | collective-permute-start | bytes 1179656 | tf_op jit(solution)/shard_map/ppermute | solution.py:23
  19.8 3.9 %collective-permute-done = bf16[2,768,128]{2,1,0:T(8,128)(2,1)S(1)} collective-permute-done((bf16[2,768,128]{2,1,0:T(8,128)(2,1)S(1)}, bf16[2,768,128]{2,1,0:T(8,128)(2,1)S(1)}, u32[]{:S(2)}, u32[]{:S(2)}) %collective-permute-start) | collective-permute-done | bytes 393248 | tf_op jit(solution)/shard_map/ppermute | solution.py:21
  23.7 3.2 %collective-permute-done.1 = bf16[2,768,128]{2,1,0:T(8,128)(2,1)S(1)} collective-permute-done((bf16[2,768,128]{2,1,0:T(8,128)(2,1)S(1)}, bf16[2,768,128]{2,1,0:T(8,128)(2,1)S(1)}, u32[]{:S(2)}, u32[]{:S(2)}) %collective-permute-start.1) | collective-permute-done | bytes 393248 | tf_op jit(solution)/shard_map/ppermute | solution.py:23
  28.1 7.5 %shard_map.82 = (bf16[768,128]{1,0:T(8,128)(2,1)S(1)}, f32[2304,128]{1,0:T(8,128)S(1)}, f32[2304,128]{1,0:T(8,128)S(1)}) custom-call(bf16[768,128]{1,0:T(8,128)(2,1)S(1)} %copy-done, bf16[768,128]{1,0:T(8,128)(2,1)S(1)} %copy-done.1, bf16[768,128]{1,0:T(8,128)(2,1)S(1)} %copy-done.2, bf16[2304,128]{1,0:T(8,128)(2,1)S(1)} %get-tuple-element.28.k_ref, ...), custom_call_target="tpu_custom_call" | custom-call | flops 2264924160 | bytes 4128768 | tf_op jit(solution)/shard_map/pallas_call | solution.py:133
  36.7 8.5 %collective-permute-start.2 = (bf16[2,768,1,128]{3,1,2,0:T(8,128)(2,1)}, bf16[2,768,1,128]{3,1,2,0:T(8,128)(2,1)S(1)}, u32[]{:S(2)}, u32[]{:S(2)}) collective-permute-start(bf16[2,768,1,128]{3,1,2,0:T(8,128)(2,1)} %get-tuple-element.25), channel_id=1, source_target_pairs={{16,0},{32,16},{48,32},{64,48},{80,64},{96,80},{112,96},{128,112},... | collective-permute-start | bytes 1179656 | tf_op jit(solution)/shard_map/ppermute | solution.py:32
  47.2 4.3 %copy.12 = bf16[3,128,3072]{1,2,0:T(8,128)(2,1)} copy(bf16[3,128,3072]{2,1,0:T(8,128)(2,1)} %param.13) | data formatting | bytes 4718592 | tf_op args[5]
  51.4 3.7 %collective-permute-done.2 = bf16[2,768,1,128]{3,1,2,0:T(8,128)(2,1)S(1)} collective-permute-done((bf16[2,768,1,128]{3,1,2,0:T(8,128)(2,1)}, bf16[2,768,1,128]{3,1,2,0:T(8,128)(2,1)S(1)}, u32[]{:S(2)}, u32[]{:S(2)}) %collective-permute-start.2) | collective-permute-done | bytes 393248 | tf_op jit(solution)/shard_map/ppermute | solution.py:32
  55.1 8.8 %collective-permute-done.3 = bf16[2,768,1,128]{3,1,2,0:T(8,128)(2,1)S(1)} collective-permute-done((bf16[2,768,1,128]{3,1,2,0:T(8,128)(2,1)}, bf16[2,768,1,128]{3,1,2,0:T(8,128)(2,1)S(1)}, u32[]{:S(2)}, u32[]{:S(2)}) %collective-permute-start.3) | collective-permute-done | bytes 393248 | tf_op jit(solution)/shard_map/ppermute | solution.py:32
  64.0 2.6 %convolution_bitcast_fusion = f32[768,2,4,2,192]{0,4,3,2,1:T(8,128)S(1)} fusion(bf16[3,128,2,4,2,192]{1,5,4,3,2,0:T(8,128)(2,1)S(1)} %bitcast.112, bf16[1,768,128]{2,1,0:T(8,128)(2,1)S(1)} %get-tuple-element.30, bf16[1,768,128]{2,1,0:T(8,128)(2,1)S(1)} %get-tuple-element.29, bf16[1,768,128]{2,1,0:T(8,128)(2,1)S(1)} %bitcast.111), kind=kOutput, calls=%fused_computation.2 | convolution fusion | flops 1813708800 | bytes 12386304 | tf_op jit(solution)/shard_map/cik,ckzxym->izxym/dot_general | solution.py:219
  66.7 3.7 %copy-done.4 = f32[768,2,4,2,192]{0,4,3,2,1:T(8,128)} copy-done((f32[768,2,4,2,192]{0,4,3,2,1:T(8,128)}, f32[768,2,4,2,192]{0,4,3,2,1:T(8,128)S(1)}, u32[]{:S(2)}) %copy-start.4) | copy-done | bytes 9437208
  72.6 4.6 %collective-permute-done.4 = bf16[768,2,4,192]{0,3,2,1:T(8,128)(2,1)} collective-permute-done((bf16[768,2,4,192]{0,3,2,1:T(8,128)(2,1)S(1)}, bf16[768,2,4,192]{0,3,2,1:T(8,128)(2,1)}, u32[]{:S(2)}, u32[]{:S(2)}) %collective-permute-start.4) | collective-permute-done | bytes 2359328 | tf_op jit(solution)/shard_map/ppermute | solution.py:60
  77.2 3.7 %bitcast_add_fusion = f32[768,2,4,192]{0,3,2,1:T(8,128)S(1)} fusion(bf16[768,2,4,192]{0,3,2,1:T(8,128)(2,1)} %collective-permute-done.4, f32[768,2,4,2,192]{0,4,3,2,1:T(8,128)} %copy-done.4, s32[]{:T(128)S(6)} %select_n.128), kind=kLoop, calls=%fused_computation | loop fusion | flops 2359296 | bytes 11796484 | tf_op jit(solution)/shard_map/add | solution.py:63
  83.0 3.4 %collective-permute-start.5 = (bf16[384,192]{0,1:T(8,128)(2,1)S(1)}, bf16[384,192]{0,1:T(8,128)(2,1)S(1)}, u32[]{:S(2)}, u32[]{:S(2)}) collective-permute-start(bf16[384,192]{0,1:T(8,128)(2,1)S(1)} %get-tuple-element.21), channel_id=1, source_target_pairs={{0,2},{2,4},{4,6},{6,0},{1,3},{3,5},{5,7},{7,1},{8,10},{10,12},{12... | collective-permute-start | bytes 442376 | tf_op jit(solution)/shard_map/ppermute | solution.py:49
  86.5 3.7 %collective-permute-start.8 = (bf16[384,192]{0,1:T(8,128)(2,1)S(1)}, bf16[384,192]{0,1:T(8,128)(2,1)S(1)}, u32[]{:S(2)}, u32[]{:S(2)}) collective-permute-start(bf16[384,192]{0,1:T(8,128)(2,1)S(1)} %get-tuple-element.22), channel_id=1, source_target_pairs={{0,6},{2,0},{4,2},{6,4},{1,7},{3,1},{5,3},{7,5},{8,14},{10,8},{12,... | collective-permute-start | bytes 442376 | tf_op jit(solution)/shard_map/ppermute | solution.py:49
  93.0 2.2 %collective-permute-start.6 = (bf16[384,192]{0,1:T(8,128)(2,1)S(1)}, bf16[384,192]{0,1:T(8,128)(2,1)S(1)}, u32[]{:S(2)}, u32[]{:S(2)}) collective-permute-start(bf16[384,192]{0,1:T(8,128)(2,1)S(1)} %fusion.24), channel_id=1, source_target_pairs={{0,2},{2,4},{4,6},{6,0},{1,3},{3,5},{5,7},{7,1},{8,10},{10,12},{12... | collective-permute-start | bytes 442376 | tf_op jit(solution)/shard_map/ppermute | solution.py:49
  95.3 6.0 %collective-permute-done.6 = bf16[384,192]{0,1:T(8,128)(2,1)S(1)} collective-permute-done((bf16[384,192]{0,1:T(8,128)(2,1)S(1)}, bf16[384,192]{0,1:T(8,128)(2,1)S(1)}, u32[]{:S(2)}, u32[]{:S(2)}) %collective-permute-start.6) | collective-permute-done | bytes 147488 | tf_op jit(solution)/shard_map/ppermute | solution.py:49
  104.3 5.1 %collective-permute-start.9 = (bf16[384,192]{0,1:T(8,128)(2,1)S(1)}, bf16[384,192]{0,1:T(8,128)(2,1)S(1)}, u32[]{:S(2)}, u32[]{:S(2)}) collective-permute-start(bf16[384,192]{0,1:T(8,128)(2,1)S(1)} %get-tuple-element.20), channel_id=1, source_target_pairs={{0,6},{2,0},{4,2},{6,4},{1,7},{3,1},{5,3},{7,5},{8,14},{10,8},{12,... | collective-permute-start | bytes 442376 | tf_op jit(solution)/shard_map/ppermute | solution.py:49
  113.2 5.6 %collective-permute-start.10 = (bf16[384,192]{0,1:T(8,128)(2,1)S(1)}, bf16[384,192]{0,1:T(8,128)(2,1)S(1)}, u32[]{:S(2)}, u32[]{:S(2)}) collective-permute-start(bf16[384,192]{0,1:T(8,128)(2,1)S(1)} %get-tuple-element.18), channel_id=1, source_target_pairs={{0,6},{2,0},{4,2},{6,4},{1,7},{3,1},{5,3},{7,5},{8,14},{10,8},{12,... | collective-permute-start | bytes 442376 | tf_op jit(solution)/shard_map/ppermute | solution.py:49
  122.7 5.6 %collective-permute-start.11 = (bf16[384,192]{0,1:T(8,128)(2,1)S(1)}, bf16[384,192]{0,1:T(8,128)(2,1)S(1)}, u32[]{:S(2)}, u32[]{:S(2)}) collective-permute-start(bf16[384,192]{0,1:T(8,128)(2,1)S(1)} %fusion.29), channel_id=1, source_target_pairs={{0,6},{2,0},{4,2},{6,4},{1,7},{3,1},{5,3},{7,5},{8,14},{10,8},{12,... | collective-permute-start | bytes 442376 | tf_op jit(solution)/shard_map/ppermute | solution.py:49
  130.3 12.8 %collective-permute-start.17 = (bf16[768,192]{0,1:T(8,128)(2,1)S(1)}, bf16[768,192]{0,1:T(8,128)(2,1)S(1)}, u32[]{:S(2)}, u32[]{:S(2)}) collective-permute-start(bf16[768,192]{0,1:T(8,128)(2,1)S(1)} %pad_maximum_fusion.3), channel_id=1, source_target_pairs={{0,8},{8,0},{1,9},{9,1},{2,10},{10,2},{3,11},{11,3},{4,12},{12,4},... | collective-permute-start | bytes 884744 | tf_op jit(solution)/shard_map/ppermute | solution.py:69
  143.1 5.1 %collective-permute-start.12 = (bf16[384,192]{0,1:T(8,128)(2,1)S(1)}, bf16[384,192]{0,1:T(8,128)(2,1)S(1)}, u32[]{:S(2)}, u32[]{:S(2)}) collective-permute-start(bf16[384,192]{0,1:T(8,128)(2,1)S(1)} %fusion.28), channel_id=1, source_target_pairs={{0,6},{2,0},{4,2},{6,4},{1,7},{3,1},{5,3},{7,5},{8,14},{10,8},{12,... | collective-permute-start | bytes 442376 | tf_op jit(solution)/shard_map/ppermute | solution.py:49
  151.6 5.6 %collective-permute-start.13 = (bf16[384,192]{0,1:T(8,128)(2,1)S(1)}, bf16[384,192]{0,1:T(8,128)(2,1)S(1)}, u32[]{:S(2)}, u32[]{:S(2)}) collective-permute-start(bf16[384,192]{0,1:T(8,128)(2,1)S(1)} %fusion.27), channel_id=1, source_target_pairs={{0,6},{2,0},{4,2},{6,4},{1,7},{3,1},{5,3},{7,5},{8,14},{10,8},{12,... | collective-permute-start | bytes 442376 | tf_op jit(solution)/shard_map/ppermute | solution.py:49
  159.9 5.6 %collective-permute-done.16 = bf16[384,192]{0,1:T(8,128)(2,1)S(1)} collective-permute-done((bf16[384,192]{0,1:T(8,128)(2,1)S(1)}, bf16[384,192]{0,1:T(8,128)(2,1)S(1)}, u32[]{:S(2)}, u32[]{:S(2)}) %collective-permute-start.16) | collective-permute-done | bytes 147488 | tf_op jit(solution)/shard_map/ppermute | solution.py:49
  (68 shorter events, 36.2 us)
Async XLA Ops:
  1.1 22.6 %collective-permute-start = (bf16[2,768,128]{2,1,0:T(8,128)(2,1)S(1)}, bf16[2,768,128]{2,1,0:T(8,128)(2,1)S(1)}, u32[]{:S(2)}, u32[]{:S(2)}) collective-permute-start(bf16[2,768,128]{2,1,0:T(8,128)(2,1)S(1)} %pad_maximum_fusion.2), channel_id=1, source_target_pairs={{0,16},{16,32},{32,48},{48,64},{64,80},{80,96},{96,112},{112,128},... | collective-permute-start | bytes 1179656 | tf_op jit(solution)/shard_map/ppermute | solution.py:21
  5.3 21.5 %collective-permute-start.1 = (bf16[2,768,128]{2,1,0:T(8,128)(2,1)S(1)}, bf16[2,768,128]{2,1,0:T(8,128)(2,1)S(1)}, u32[]{:S(2)}, u32[]{:S(2)}) collective-permute-start(bf16[2,768,128]{2,1,0:T(8,128)(2,1)S(1)} %pad_maximum_fusion.2), channel_id=1, source_target_pairs={{16,0},{32,16},{48,32},{64,48},{80,64},{96,80},{112,96},{128,112},... | collective-permute-start | bytes 1179656 | tf_op jit(solution)/shard_map/ppermute | solution.py:23
  19.7 8.3 %copy-start = (bf16[768,128]{1,0:T(8,128)(2,1)S(1)}, bf16[768,128]{1,0:T(8,128)(2,1)}, u32[]{:S(2)}) copy-start(bf16[768,128]{1,0:T(8,128)(2,1)} %q_ref.1) | copy-start | bytes 589828
  19.7 8.3 %copy-start.1 = (bf16[768,128]{1,0:T(8,128)(2,1)S(1)}, bf16[768,128]{1,0:T(8,128)(2,1)}, u32[]{:S(2)}) copy-start(bf16[768,128]{1,0:T(8,128)(2,1)} %do_ref.1) | copy-start | bytes 589828
  19.8 8.3 %copy-start.2 = (bf16[768,128]{1,0:T(8,128)(2,1)S(1)}, bf16[768,128]{1,0:T(8,128)(2,1)}, u32[]{:S(2)}) copy-start(bf16[768,128]{1,0:T(8,128)(2,1)} %o_ref.1) | copy-start | bytes 589828
  36.7 18.3 %collective-permute-start.2 = (bf16[2,768,1,128]{3,1,2,0:T(8,128)(2,1)}, bf16[2,768,1,128]{3,1,2,0:T(8,128)(2,1)S(1)}, u32[]{:S(2)}, u32[]{:S(2)}) collective-permute-start(bf16[2,768,1,128]{3,1,2,0:T(8,128)(2,1)} %get-tuple-element.25), channel_id=1, source_target_pairs={{16,0},{32,16},{48,32},{64,48},{80,64},{96,80},{112,96},{128,112},... | collective-permute-start | bytes 1179656 | tf_op jit(solution)/shard_map/ppermute | solution.py:32
  45.2 18.6 %collective-permute-start.3 = (bf16[2,768,1,128]{3,1,2,0:T(8,128)(2,1)}, bf16[2,768,1,128]{3,1,2,0:T(8,128)(2,1)S(1)}, u32[]{:S(2)}, u32[]{:S(2)}) collective-permute-start(bf16[2,768,1,128]{3,1,2,0:T(8,128)(2,1)} %get-tuple-element.26), channel_id=1, source_target_pairs={{752,0},{0,16},{16,32},{32,48},{48,64},{64,80},{80,96},{96,112},{1... | collective-permute-start | bytes 1179656 | tf_op jit(solution)/shard_map/ppermute | solution.py:32
  51.4 12.6 %copy-start.5 = (bf16[3,128,3072]{1,2,0:T(8,128)(2,1)S(1)}, bf16[3,128,3072]{1,2,0:T(8,128)(2,1)}, u32[]{:S(2)}) copy-start(bf16[3,128,3072]{1,2,0:T(8,128)(2,1)} %copy.12) | copy-start | bytes 7077892
  66.7 3.7 %copy-start.4 = (f32[768,2,4,2,192]{0,4,3,2,1:T(8,128)}, f32[768,2,4,2,192]{0,4,3,2,1:T(8,128)S(1)}, u32[]{:S(2)}) copy-start(f32[768,2,4,2,192]{0,4,3,2,1:T(8,128)S(1)} %convolution_bitcast_fusion) | copy-start | bytes 28311556
  70.6 6.6 %collective-permute-start.4 = (bf16[768,2,4,192]{0,3,2,1:T(8,128)(2,1)S(1)}, bf16[768,2,4,192]{0,3,2,1:T(8,128)(2,1)}, u32[]{:S(2)}, u32[]{:S(2)}) collective-permute-start(bf16[768,2,4,192]{0,3,2,1:T(8,128)(2,1)S(1)} %fusion.1), channel_id=1, source_target_pairs={{0,1},{1,0},{2,3},{3,2},{4,5},{5,4},{6,7},{7,6},{8,9},{9,8},{10,11... | collective-permute-start | bytes 7077896 | tf_op jit(solution)/shard_map/ppermute | solution.py:60
  80.8 2.1 %copy-start.3 = (f32[768,2,4,192]{0,3,2,1:T(8,128)}, f32[768,2,4,192]{0,3,2,1:T(8,128)S(1)}, u32[]{:S(2)}) copy-start(f32[768,2,4,192]{0,3,2,1:T(8,128)S(1)} %bitcast_add_fusion) | copy-start | bytes 14155780
  83.0 9.0 %collective-permute-start.5 = (bf16[384,192]{0,1:T(8,128)(2,1)S(1)}, bf16[384,192]{0,1:T(8,128)(2,1)S(1)}, u32[]{:S(2)}, u32[]{:S(2)}) collective-permute-start(bf16[384,192]{0,1:T(8,128)(2,1)S(1)} %get-tuple-element.21), channel_id=1, source_target_pairs={{0,2},{2,4},{4,6},{6,0},{1,3},{3,5},{5,7},{7,1},{8,10},{10,12},{12... | collective-permute-start | bytes 442376 | tf_op jit(solution)/shard_map/ppermute | solution.py:49
  86.5 8.8 %collective-permute-start.8 = (bf16[384,192]{0,1:T(8,128)(2,1)S(1)}, bf16[384,192]{0,1:T(8,128)(2,1)S(1)}, u32[]{:S(2)}, u32[]{:S(2)}) collective-permute-start(bf16[384,192]{0,1:T(8,128)(2,1)S(1)} %get-tuple-element.22), channel_id=1, source_target_pairs={{0,6},{2,0},{4,2},{6,4},{1,7},{3,1},{5,3},{7,5},{8,14},{10,8},{12,... | collective-permute-start | bytes 442376 | tf_op jit(solution)/shard_map/ppermute | solution.py:49
  93.0 8.2 %collective-permute-start.6 = (bf16[384,192]{0,1:T(8,128)(2,1)S(1)}, bf16[384,192]{0,1:T(8,128)(2,1)S(1)}, u32[]{:S(2)}, u32[]{:S(2)}) collective-permute-start(bf16[384,192]{0,1:T(8,128)(2,1)S(1)} %fusion.24), channel_id=1, source_target_pairs={{0,2},{2,4},{4,6},{6,0},{1,3},{3,5},{5,7},{7,1},{8,10},{10,12},{12... | collective-permute-start | bytes 442376 | tf_op jit(solution)/shard_map/ppermute | solution.py:49
  102.4 8.2 %collective-permute-start.7 = (bf16[384,192]{0,1:T(8,128)(2,1)S(1)}, bf16[384,192]{0,1:T(8,128)(2,1)S(1)}, u32[]{:S(2)}, u32[]{:S(2)}) collective-permute-start(bf16[384,192]{0,1:T(8,128)(2,1)S(1)} %get-tuple-element.19), channel_id=1, source_target_pairs={{0,2},{2,4},{4,6},{6,0},{1,3},{3,5},{5,7},{7,1},{8,10},{10,12},{12... | collective-permute-start | bytes 442376 | tf_op jit(solution)/shard_map/ppermute | solution.py:49
  104.3 7.8 %collective-permute-start.9 = (bf16[384,192]{0,1:T(8,128)(2,1)S(1)}, bf16[384,192]{0,1:T(8,128)(2,1)S(1)}, u32[]{:S(2)}, u32[]{:S(2)}) collective-permute-start(bf16[384,192]{0,1:T(8,128)(2,1)S(1)} %get-tuple-element.20), channel_id=1, source_target_pairs={{0,6},{2,0},{4,2},{6,4},{1,7},{3,1},{5,3},{7,5},{8,14},{10,8},{12,... | collective-permute-start | bytes 442376 | tf_op jit(solution)/shard_map/ppermute | solution.py:49
  113.2 8.2 %collective-permute-start.10 = (bf16[384,192]{0,1:T(8,128)(2,1)S(1)}, bf16[384,192]{0,1:T(8,128)(2,1)S(1)}, u32[]{:S(2)}, u32[]{:S(2)}) collective-permute-start(bf16[384,192]{0,1:T(8,128)(2,1)S(1)} %get-tuple-element.18), channel_id=1, source_target_pairs={{0,6},{2,0},{4,2},{6,4},{1,7},{3,1},{5,3},{7,5},{8,14},{10,8},{12,... | collective-permute-start | bytes 442376 | tf_op jit(solution)/shard_map/ppermute | solution.py:49
  122.7 20.4 %collective-permute-start.11 = (bf16[384,192]{0,1:T(8,128)(2,1)S(1)}, bf16[384,192]{0,1:T(8,128)(2,1)S(1)}, u32[]{:S(2)}, u32[]{:S(2)}) collective-permute-start(bf16[384,192]{0,1:T(8,128)(2,1)S(1)} %fusion.29), channel_id=1, source_target_pairs={{0,6},{2,0},{4,2},{6,4},{1,7},{3,1},{5,3},{7,5},{8,14},{10,8},{12,... | collective-permute-start | bytes 442376 | tf_op jit(solution)/shard_map/ppermute | solution.py:49
  128.3 19.9 %collective-permute-start.14 = (bf16[384,192]{0,1:T(8,128)(2,1)S(1)}, bf16[384,192]{0,1:T(8,128)(2,1)S(1)}, u32[]{:S(2)}, u32[]{:S(2)}) collective-permute-start(bf16[384,192]{0,1:T(8,128)(2,1)S(1)} %fusion.30), channel_id=1, source_target_pairs={{0,2},{2,4},{4,6},{6,0},{1,3},{3,5},{5,7},{7,1},{8,10},{10,12},{12... | collective-permute-start | bytes 442376 | tf_op jit(solution)/shard_map/ppermute | solution.py:49
  130.3 35.3 %collective-permute-start.17 = (bf16[768,192]{0,1:T(8,128)(2,1)S(1)}, bf16[768,192]{0,1:T(8,128)(2,1)S(1)}, u32[]{:S(2)}, u32[]{:S(2)}) collective-permute-start(bf16[768,192]{0,1:T(8,128)(2,1)S(1)} %pad_maximum_fusion.3), channel_id=1, source_target_pairs={{0,8},{8,0},{1,9},{9,1},{2,10},{10,2},{3,11},{11,3},{4,12},{12,4},... | collective-permute-start | bytes 884744 | tf_op jit(solution)/shard_map/ppermute | solution.py:69
  143.1 8.5 %collective-permute-start.12 = (bf16[384,192]{0,1:T(8,128)(2,1)S(1)}, bf16[384,192]{0,1:T(8,128)(2,1)S(1)}, u32[]{:S(2)}, u32[]{:S(2)}) collective-permute-start(bf16[384,192]{0,1:T(8,128)(2,1)S(1)} %fusion.28), channel_id=1, source_target_pairs={{0,6},{2,0},{4,2},{6,4},{1,7},{3,1},{5,3},{7,5},{8,14},{10,8},{12,... | collective-permute-start | bytes 442376 | tf_op jit(solution)/shard_map/ppermute | solution.py:49
  148.3 8.9 %collective-permute-start.15 = (bf16[384,192]{0,1:T(8,128)(2,1)S(1)}, bf16[384,192]{0,1:T(8,128)(2,1)S(1)}, u32[]{:S(2)}, u32[]{:S(2)}) collective-permute-start(bf16[384,192]{0,1:T(8,128)(2,1)S(1)} %fusion.26), channel_id=1, source_target_pairs={{0,2},{2,4},{4,6},{6,0},{1,3},{3,5},{5,7},{7,1},{8,10},{10,12},{12... | collective-permute-start | bytes 442376 | tf_op jit(solution)/shard_map/ppermute | solution.py:49
  151.6 8.3 %collective-permute-start.13 = (bf16[384,192]{0,1:T(8,128)(2,1)S(1)}, bf16[384,192]{0,1:T(8,128)(2,1)S(1)}, u32[]{:S(2)}, u32[]{:S(2)}) collective-permute-start(bf16[384,192]{0,1:T(8,128)(2,1)S(1)} %fusion.27), channel_id=1, source_target_pairs={{0,6},{2,0},{4,2},{6,4},{1,7},{3,1},{5,3},{7,5},{8,14},{10,8},{12,... | collective-permute-start | bytes 442376 | tf_op jit(solution)/shard_map/ppermute | solution.py:49
  157.3 8.2 %collective-permute-start.16 = (bf16[384,192]{0,1:T(8,128)(2,1)S(1)}, bf16[384,192]{0,1:T(8,128)(2,1)S(1)}, u32[]{:S(2)}, u32[]{:S(2)}) collective-permute-start(bf16[384,192]{0,1:T(8,128)(2,1)S(1)} %fusion.25), channel_id=1, source_target_pairs={{0,2},{2,4},{4,6},{6,0},{1,3},{3,5},{5,7},{7,1},{8,10},{10,12},{12... | collective-permute-start | bytes 442376 | tf_op jit(solution)/shard_map/ppermute | solution.py:49

commit v3 on v2

--- a/solution.py
+++ b/solution.py
@@ -52,6 +52,25 @@
     return jnp.concatenate(out, axis=0)
 
 
+def four_scatter(block):
+    x = lax.axis_index("x")
+    rows = block.shape[0]
+    top = slice(0, rows // 2)
+    bottom = slice(rows // 2, rows)
+    cw = [(i, (i + 1) % 4) for i in range(4)]
+    ccw = [(i, (i - 1) % 4) for i in range(4)]
+    opposite = pick(block, 1, (x + 2) % 4)
+    from_left = lax.ppermute(opposite[top].astype(jnp.bfloat16), "x", cw)
+    from_right = lax.ppermute(opposite[bottom].astype(jnp.bfloat16), "x", ccw)
+    right = pick(block, 1, (x + 1) % 4)
+    left = pick(block, 1, (x - 1) % 4)
+    to_right = jnp.concatenate([right[top] + from_left.astype(jnp.float32), right[bottom]])
+    to_left = jnp.concatenate([left[top], left[bottom] + from_right.astype(jnp.float32)])
+    got_left = lax.ppermute(to_right.astype(jnp.bfloat16), "x", cw)
+    got_right = lax.ppermute(to_left.astype(jnp.bfloat16), "x", ccw)
+    return pick(block, 1, x) + got_left.astype(jnp.float32) + got_right.astype(jnp.float32)
+
+
 def reduce_scatter(parts):
     c = lax.axis_index("c")
     zh = lax.axis_index("zh")
@@ -63,13 +82,9 @@
         sums = pick(parts, 3, c) + got.astype(jnp.float32)
     else:
         sums = parts[:, :, :, 0]
-    if n_zh == 2 and n_x > 1:
-        sent = ring_scatter(pick(sums, 1, 1 - zh), 1, n_x).astype(jnp.bfloat16)
-        sent, later = lax.optimization_barrier((sent, pick(sums, 1, zh)))
-        got = lax.ppermute(sent, "zh", [(0, 1), (1, 0)])
-        kept = ring_scatter(later, -1, n_x)
-        return kept + got.astype(jnp.float32)
-    if n_x > 1:
+    if n_x == 4:
+        sums = four_scatter(jnp.swapaxes(sums, 1, 2))
+    elif n_x > 1:
         sums = jnp.stack([ring_scatter(sums[:, z], 1, n_x) for z in range(n_zh)], axis=1)
     else:
         sums = sums[:, :, 0]

time: 167 us -> 146 us (0.87)
  the two profiles are of different devices: /device:TPU:32 before, /device:TPU:70 now
where the time goes in v3:
time: 146 us; the launch traced here: 145 us
  waiting for transfers between devices  75.8 us (52%)
  starting transfers between devices  35.9 us (25%)
  local copies, waits for them, and re-layouts  12.1 us (8%)
  other arithmetic  11 us (8%)
  Pallas kernels  7.49 us (5%)
  matrix products  2.65 us (2%)
    ppermute x1, waiting for transfers between devices, reduce_scatter(): got = lax.ppermute(acc.astype(jnp.bfloat16), 'zh', route)  19.2 us
    ppermute x2, waiting for transfers between devices, passed_along(): return lax.ppermute(block, axis, route)  16.4 us
    ppermute x1, waiting for transfers between devices, with_halo(): lax.ppermute(head, axis, [((i + 1) % count, i) for i in range(count)])  13.1 us
    ppermute x1, waiting for transfers between devices, four_scatter(): got_left = lax.ppermute(to_right.astype(jnp.bfloat16), 'x', cw)  10.4 us
    unnamed x18, local copies, waits for them, and re-layouts  9.18 us
    ppermute x1, starting transfers between devices, reduce_scatter(): got = lax.ppermute(acc.astype(jnp.bfloat16), 'zh', route)  9.08 us
    pallas_call x1, Pallas kernels, attention(): pl.pallas_call(attention_kernel, grid=(tiles,), in_specs=[row_spec, row_s...  7.49 us
    ppermute x2, starting transfers between devices, passed_along(): return lax.ppermute(block, axis, route)  7 us
  transfers between devices with their start and end apart: 10, of which 9 were waited for; matrix products, arithmetic and copies ran while one was open for 6% of the time, Pallas kernels for 0%

profile of v3, /device:TPU:70, one launch (start us, length us, event | category | flops | bytes accessed | tf_op | source)
XLA Modules:
  0.0 145.4 jit_solution(10342357436012378305)
XLA Ops:
  1.1 4.3 %collective-permute-start = (bf16[2,768,128]{2,1,0:T(8,128)(2,1)S(1)}, bf16[2,768,128]{2,1,0:T(8,128)(2,1)S(1)}, u32[]{:S(2)}, u32[]{:S(2)}) collective-permute-start(bf16[2,768,128]{2,1,0:T(8,128)(2,1)S(1)} %pad_maximum_fusion.4), channel_id=1, source_target_pairs={{0,16},{16,32},{32,48},{48,64},{64,80},{80,96},{96,112},{112,128},... | collective-permute-start | bytes 1179656 | tf_op jit(solution)/shard_map/ppermute | solution.py:21
  5.3 1.9 %collective-permute-start.1 = (bf16[2,768,128]{2,1,0:T(8,128)(2,1)S(1)}, bf16[2,768,128]{2,1,0:T(8,128)(2,1)S(1)}, u32[]{:S(2)}, u32[]{:S(2)}) collective-permute-start(bf16[2,768,128]{2,1,0:T(8,128)(2,1)S(1)} %pad_maximum_fusion.4), channel_id=1, source_target_pairs={{16,0},{32,16},{48,32},{64,48},{80,64},{96,80},{112,96},{128,112},... | collective-permute-start | bytes 1179656 | tf_op jit(solution)/shard_map/ppermute | solution.py:23
  11.3 2.5 %collective-permute-done = bf16[2,768,128]{2,1,0:T(8,128)(2,1)S(1)} collective-permute-done((bf16[2,768,128]{2,1,0:T(8,128)(2,1)S(1)}, bf16[2,768,128]{2,1,0:T(8,128)(2,1)S(1)}, u32[]{:S(2)}, u32[]{:S(2)}) %collective-permute-start) | collective-permute-done | bytes 393248 | tf_op jit(solution)/shard_map/ppermute | solution.py:21
  13.8 13.1 %collective-permute-done.1 = bf16[2,768,128]{2,1,0:T(8,128)(2,1)S(1)} collective-permute-done((bf16[2,768,128]{2,1,0:T(8,128)(2,1)S(1)}, bf16[2,768,128]{2,1,0:T(8,128)(2,1)S(1)}, u32[]{:S(2)}, u32[]{:S(2)}) %collective-permute-start.1) | collective-permute-done | bytes 393248 | tf_op jit(solution)/shard_map/ppermute | solution.py:23
  29.1 7.5 %shard_map.82 = (bf16[768,128]{1,0:T(8,128)(2,1)S(1)}, f32[2304,128]{1,0:T(8,128)S(1)}, f32[2304,128]{1,0:T(8,128)S(1)}) custom-call(bf16[768,128]{1,0:T(8,128)(2,1)S(1)} %copy-done, bf16[768,128]{1,0:T(8,128)(2,1)S(1)} %copy-done.1, bf16[768,128]{1,0:T(8,128)(2,1)S(1)} %copy-done.2, bf16[2304,128]{1,0:T(8,128)(2,1)S(1)} %get-tuple-element.18.k_ref, ...), custom_call_target="tpu_custom_call" | custom-call | flops 2264924160 | bytes 4128768 | tf_op jit(solution)/shard_map/pallas_call | solution.py:148
  37.7 1.9 %collective-permute-start.2 = (bf16[2,768,1,128]{3,1,2,0:T(8,128)(2,1)}, bf16[2,768,1,128]{3,1,2,0:T(8,128)(2,1)S(1)}, u32[]{:S(2)}, u32[]{:S(2)}) collective-permute-start(bf16[2,768,1,128]{3,1,2,0:T(8,128)(2,1)} %get-tuple-element.15), channel_id=1, source_target_pairs={{16,0},{32,16},{48,32},{64,48},{80,64},{96,80},{112,96},{128,112},... | collective-permute-start | bytes 1179656 | tf_op jit(solution)/shard_map/ppermute | solution.py:32
  39.6 5.1 %collective-permute-start.3 = (bf16[2,768,1,128]{3,1,2,0:T(8,128)(2,1)}, bf16[2,768,1,128]{3,1,2,0:T(8,128)(2,1)S(1)}, u32[]{:S(2)}, u32[]{:S(2)}) collective-permute-start(bf16[2,768,1,128]{3,1,2,0:T(8,128)(2,1)} %get-tuple-element.16), channel_id=1, source_target_pairs={{752,0},{0,16},{16,32},{32,48},{48,64},{64,80},{80,96},{96,112},{1... | collective-permute-start | bytes 1179656 | tf_op jit(solution)/shard_map/ppermute | solution.py:32
  44.7 4.3 %copy.18 = bf16[3,128,3072]{1,2,0:T(8,128)(2,1)} copy(bf16[3,128,3072]{2,1,0:T(8,128)(2,1)} %param.13) | data formatting | bytes 4718592 | tf_op args[5]
  49.0 3.3 %collective-permute-done.2 = bf16[2,768,1,128]{3,1,2,0:T(8,128)(2,1)S(1)} collective-permute-done((bf16[2,768,1,128]{3,1,2,0:T(8,128)(2,1)}, bf16[2,768,1,128]{3,1,2,0:T(8,128)(2,1)S(1)}, u32[]{:S(2)}, u32[]{:S(2)}) %collective-permute-start.2) | collective-permute-done | bytes 393248 | tf_op jit(solution)/shard_map/ppermute | solution.py:32
  52.3 13.1 %collective-permute-done.3 = bf16[2,768,1,128]{3,1,2,0:T(8,128)(2,1)S(1)} collective-permute-done((bf16[2,768,1,128]{3,1,2,0:T(8,128)(2,1)}, bf16[2,768,1,128]{3,1,2,0:T(8,128)(2,1)S(1)}, u32[]{:S(2)}, u32[]{:S(2)}) %collective-permute-start.3) | collective-permute-done | bytes 393248 | tf_op jit(solution)/shard_map/ppermute | solution.py:32
  65.6 2.7 %convolution_bitcast_fusion = f32[768,2,4,2,192]{0,4,3,2,1:T(8,128)S(1)} fusion(bf16[3,128,2,4,2,192]{1,5,4,3,2,0:T(8,128)(2,1)S(1)} %bitcast.82, bf16[1,768,128]{2,1,0:T(8,128)(2,1)S(1)} %get-tuple-element.22, bf16[1,768,128]{2,1,0:T(8,128)(2,1)S(1)} %get-tuple-element.21, bf16[1,768,128]{2,1,0:T(8,128)(2,1)S(1)} %bitcast.81), kind=kOutput, calls=%fused_computation.2 | convolution fusion | flops 1813708800 | bytes 12386304 | tf_op jit(solution)/shard_map/cik,ckzxym->izxym/dot_general | solution.py:234
  68.3 3.6 %copy-done.4 = f32[768,2,4,2,192]{0,4,3,2,1:T(8,128)} copy-done((f32[768,2,4,2,192]{0,4,3,2,1:T(8,128)}, f32[768,2,4,2,192]{0,4,3,2,1:T(8,128)S(1)}, u32[]{:S(2)}) %copy-start.4) | copy-done | bytes 9437208
  72.1 1.9 %collective-permute-start.4 = (bf16[768,2,4,192]{0,3,2,1:T(8,128)(2,1)S(1)}, bf16[768,2,4,192]{0,3,2,1:T(8,128)(2,1)}, u32[]{:S(2)}, u32[]{:S(2)}) collective-permute-start(bf16[768,2,4,192]{0,3,2,1:T(8,128)(2,1)S(1)} %fusion.1), channel_id=1, source_target_pairs={{0,1},{1,0},{2,3},{3,2},{4,5},{5,4},{6,7},{7,6},{8,9},{9,8},{10,11... | collective-permute-start | bytes 7077896 | tf_op jit(solution)/shard_map/ppermute | solution.py:79
  74.1 4.6 %collective-permute-done.4 = bf16[768,2,4,192]{0,3,2,1:T(8,128)(2,1)} collective-permute-done((bf16[768,2,4,192]{0,3,2,1:T(8,128)(2,1)S(1)}, bf16[768,2,4,192]{0,3,2,1:T(8,128)(2,1)}, u32[]{:S(2)}, u32[]{:S(2)}) %collective-permute-start.4) | collective-permute-done | bytes 2359328 | tf_op jit(solution)/shard_map/ppermute | solution.py:79
  78.7 3.7 %bitcast_add_fusion = f32[768,2,4,192]{0,3,2,1:T(8,128)S(1)} fusion(bf16[768,2,4,192]{0,3,2,1:T(8,128)(2,1)} %collective-permute-done.4, f32[768,2,4,2,192]{0,4,3,2,1:T(8,128)} %copy-done.4, s32[]{:T(128)S(6)} %select_n.80), kind=kLoop, calls=%fused_computation | loop fusion | flops 2359296 | bytes 11796484 | tf_op jit(solution)/shard_map/add | solution.py:82
  82.6 1.9 %collective-permute-start.5 = (bf16[384,2,192]{0,2,1:T(8,128)(2,1)S(1)}, bf16[384,2,192]{0,2,1:T(8,128)(2,1)S(1)}, u32[]{:S(2)}, u32[]{:S(2)}) collective-permute-start(bf16[384,2,192]{0,2,1:T(8,128)(2,1)S(1)} %get-tuple-element.19), channel_id=1, source_target_pairs={{0,2},{2,4},{4,6},{6,0},{1,3},{3,5},{5,7},{7,1},{8,10},{10,12},{12... | collective-permute-start | bytes 884744 | tf_op jit(solution)/shard_map/ppermute | solution.py:63
  84.5 3.9 %collective-permute-start.7 = (bf16[384,2,192]{0,2,1:T(8,128)(2,1)S(1)}, bf16[384,2,192]{0,2,1:T(8,128)(2,1)S(1)}, u32[]{:S(2)}, u32[]{:S(2)}) collective-permute-start(bf16[384,2,192]{0,2,1:T(8,128)(2,1)S(1)} %get-tuple-element.20), channel_id=1, source_target_pairs={{0,6},{2,0},{4,2},{6,4},{1,7},{3,1},{5,3},{7,5},{8,14},{10,8},{12,... | collective-permute-start | bytes 884744 | tf_op jit(solution)/shard_map/ppermute | solution.py:64
  88.6 4.9 %collective-permute-done.5 = bf16[384,2,192]{0,2,1:T(8,128)(2,1)S(1)} collective-permute-done((bf16[384,2,192]{0,2,1:T(8,128)(2,1)S(1)}, bf16[384,2,192]{0,2,1:T(8,128)(2,1)S(1)}, u32[]{:S(2)}, u32[]{:S(2)}) %collective-permute-start.5) | collective-permute-done | bytes 294944 | tf_op jit(solution)/shard_map/ppermute | solution.py:63
  93.7 3.4 %collective-permute-start.6 = (bf16[768,2,192]{0,2,1:T(8,128)(2,1)S(1)}, bf16[768,2,192]{0,2,1:T(8,128)(2,1)S(1)}, u32[]{:S(2)}, u32[]{:S(2)}) collective-permute-start(bf16[768,2,192]{0,2,1:T(8,128)(2,1)S(1)} %pad_maximum_fusion.2), channel_id=1, source_target_pairs={{0,2},{2,4},{4,6},{6,0},{1,3},{3,5},{5,7},{7,1},{8,10},{10,12},{12... | collective-permute-start | bytes 1769480 | tf_op jit(solution)/shard_map/ppermute | solution.py:69
  97.2 2.4 %collective-permute-start.8 = (bf16[768,2,192]{0,2,1:T(8,128)(2,1)S(1)}, bf16[768,2,192]{0,2,1:T(8,128)(2,1)S(1)}, u32[]{:S(2)}, u32[]{:S(2)}) collective-permute-start(bf16[768,2,192]{0,2,1:T(8,128)(2,1)S(1)} %pad_maximum_fusion.3), channel_id=1, source_target_pairs={{0,6},{2,0},{4,2},{6,4},{1,7},{3,1},{5,3},{7,5},{8,14},{10,8},{12,... | collective-permute-start | bytes 1769480 | tf_op jit(solution)/shard_map/ppermute | solution.py:70
  99.7 10.4 %collective-permute-done.6 = bf16[768,2,192]{0,2,1:T(8,128)(2,1)S(1)} collective-permute-done((bf16[768,2,192]{0,2,1:T(8,128)(2,1)S(1)}, bf16[768,2,192]{0,2,1:T(8,128)(2,1)S(1)}, u32[]{:S(2)}, u32[]{:S(2)}) %collective-permute-start.6) | collective-permute-done | bytes 589856 | tf_op jit(solution)/shard_map/ppermute | solution.py:69
  110.1 4.8 %collective-permute-done.8 = bf16[768,2,192]{0,2,1:T(8,128)(2,1)S(1)} collective-permute-done((bf16[768,2,192]{0,2,1:T(8,128)(2,1)S(1)}, bf16[768,2,192]{0,2,1:T(8,128)(2,1)S(1)}, u32[]{:S(2)}, u32[]{:S(2)}) %collective-permute-start.8) | collective-permute-done | bytes 589856 | tf_op jit(solution)/shard_map/ppermute | solution.py:70
  116.3 9.1 %collective-permute-start.9 = (bf16[768,192]{0,1:T(8,128)(2,1)S(1)}, bf16[768,192]{0,1:T(8,128)(2,1)S(1)}, u32[]{:S(2)}, u32[]{:S(2)}) collective-permute-start(bf16[768,192]{0,1:T(8,128)(2,1)S(1)} %fusion.18), channel_id=1, source_target_pairs={{0,8},{8,0},{1,9},{9,1},{2,10},{10,2},{3,11},{11,3},{4,12},{12,4},... | collective-permute-start | bytes 884744 | tf_op jit(solution)/shard_map/ppermute | solution.py:95
  125.4 19.2 %collective-permute-done.9 = bf16[768,192]{0,1:T(8,128)(2,1)S(1)} collective-permute-done((bf16[768,192]{0,1:T(8,128)(2,1)S(1)}, bf16[768,192]{0,1:T(8,128)(2,1)S(1)}, u32[]{:S(2)}, u32[]{:S(2)}) %collective-permute-start.9) | collective-permute-done | bytes 294944 | tf_op jit(solution)/shard_map/ppermute | solution.py:95
  (47 shorter events, 11.5 us)
Async XLA Ops:
  1.1 12.7 %collective-permute-start = (bf16[2,768,128]{2,1,0:T(8,128)(2,1)S(1)}, bf16[2,768,128]{2,1,0:T(8,128)(2,1)S(1)}, u32[]{:S(2)}, u32[]{:S(2)}) collective-permute-start(bf16[2,768,128]{2,1,0:T(8,128)(2,1)S(1)} %pad_maximum_fusion.4), channel_id=1, source_target_pairs={{0,16},{16,32},{32,48},{48,64},{64,80},{80,96},{96,112},{112,128},... | collective-permute-start | bytes 1179656 | tf_op jit(solution)/shard_map/ppermute | solution.py:21
  5.3 21.5 %collective-permute-start.1 = (bf16[2,768,128]{2,1,0:T(8,128)(2,1)S(1)}, bf16[2,768,128]{2,1,0:T(8,128)(2,1)S(1)}, u32[]{:S(2)}, u32[]{:S(2)}) collective-permute-start(bf16[2,768,128]{2,1,0:T(8,128)(2,1)S(1)} %pad_maximum_fusion.4), channel_id=1, source_target_pairs={{16,0},{32,16},{48,32},{64,48},{80,64},{96,80},{112,96},{128,112},... | collective-permute-start | bytes 1179656 | tf_op jit(solution)/shard_map/ppermute | solution.py:23
  28.0 0.9 copy-start
  28.0 1.0 copy-start.1
  28.0 1.1 copy-start.2
  37.7 14.6 %collective-permute-start.2 = (bf16[2,768,1,128]{3,1,2,0:T(8,128)(2,1)}, bf16[2,768,1,128]{3,1,2,0:T(8,128)(2,1)S(1)}, u32[]{:S(2)}, u32[]{:S(2)}) collective-permute-start(bf16[2,768,1,128]{3,1,2,0:T(8,128)(2,1)} %get-tuple-element.15), channel_id=1, source_target_pairs={{16,0},{32,16},{48,32},{64,48},{80,64},{96,80},{112,96},{128,112},... | collective-permute-start | bytes 1179656 | tf_op jit(solution)/shard_map/ppermute | solution.py:32
  39.6 25.8 %collective-permute-start.3 = (bf16[2,768,1,128]{3,1,2,0:T(8,128)(2,1)}, bf16[2,768,1,128]{3,1,2,0:T(8,128)(2,1)S(1)}, u32[]{:S(2)}, u32[]{:S(2)}) collective-permute-start(bf16[2,768,1,128]{3,1,2,0:T(8,128)(2,1)} %get-tuple-element.16), channel_id=1, source_target_pairs={{752,0},{0,16},{16,32},{32,48},{48,64},{64,80},{80,96},{96,112},{1... | collective-permute-start | bytes 1179656 | tf_op jit(solution)/shard_map/ppermute | solution.py:32
  49.0 16.6 %copy-start.5 = (bf16[3,128,3072]{1,2,0:T(8,128)(2,1)S(1)}, bf16[3,128,3072]{1,2,0:T(8,128)(2,1)}, u32[]{:S(2)}) copy-start(bf16[3,128,3072]{1,2,0:T(8,128)(2,1)} %copy.18) | copy-start | bytes 7077892
  68.2 3.6 %copy-start.4 = (f32[768,2,4,2,192]{0,4,3,2,1:T(8,128)}, f32[768,2,4,2,192]{0,4,3,2,1:T(8,128)S(1)}, u32[]{:S(2)}) copy-start(f32[768,2,4,2,192]{0,4,3,2,1:T(8,128)S(1)} %convolution_bitcast_fusion) | copy-start | bytes 28311556
  72.1 6.6 %collective-permute-start.4 = (bf16[768,2,4,192]{0,3,2,1:T(8,128)(2,1)S(1)}, bf16[768,2,4,192]{0,3,2,1:T(8,128)(2,1)}, u32[]{:S(2)}, u32[]{:S(2)}) collective-permute-start(bf16[768,2,4,192]{0,3,2,1:T(8,128)(2,1)S(1)} %fusion.1), channel_id=1, source_target_pairs={{0,1},{1,0},{2,3},{3,2},{4,5},{5,4},{6,7},{7,6},{8,9},{9,8},{10,11... | collective-permute-start | bytes 7077896 | tf_op jit(solution)/shard_map/ppermute | solution.py:79
  82.4 14.7 %copy-start.3 = (f32[768,2,4,192]{0,3,2,1:T(8,128)}, f32[768,2,4,192]{0,3,2,1:T(8,128)S(1)}, u32[]{:S(2)}) copy-start(f32[768,2,4,192]{0,3,2,1:T(8,128)S(1)} %bitcast_add_fusion) | copy-start | bytes 14155780
  82.6 10.9 %collective-permute-start.5 = (bf16[384,2,192]{0,2,1:T(8,128)(2,1)S(1)}, bf16[384,2,192]{0,2,1:T(8,128)(2,1)S(1)}, u32[]{:S(2)}, u32[]{:S(2)}) collective-permute-start(bf16[384,2,192]{0,2,1:T(8,128)(2,1)S(1)} %get-tuple-element.19), channel_id=1, source_target_pairs={{0,2},{2,4},{4,6},{6,0},{1,3},{3,5},{5,7},{7,1},{8,10},{10,12},{12... | collective-permute-start | bytes 884744 | tf_op jit(solution)/shard_map/ppermute | solution.py:63
  84.5 12.6 %collective-permute-start.7 = (bf16[384,2,192]{0,2,1:T(8,128)(2,1)S(1)}, bf16[384,2,192]{0,2,1:T(8,128)(2,1)S(1)}, u32[]{:S(2)}, u32[]{:S(2)}) collective-permute-start(bf16[384,2,192]{0,2,1:T(8,128)(2,1)S(1)} %get-tuple-element.20), channel_id=1, source_target_pairs={{0,6},{2,0},{4,2},{6,4},{1,7},{3,1},{5,3},{7,5},{8,14},{10,8},{12,... | collective-permute-start | bytes 884744 | tf_op jit(solution)/shard_map/ppermute | solution.py:64
  93.7 16.4 %collective-permute-start.6 = (bf16[768,2,192]{0,2,1:T(8,128)(2,1)S(1)}, bf16[768,2,192]{0,2,1:T(8,128)(2,1)S(1)}, u32[]{:S(2)}, u32[]{:S(2)}) collective-permute-start(bf16[768,2,192]{0,2,1:T(8,128)(2,1)S(1)} %pad_maximum_fusion.2), channel_id=1, source_target_pairs={{0,2},{2,4},{4,6},{6,0},{1,3},{3,5},{5,7},{7,1},{8,10},{10,12},{12... | collective-permute-start | bytes 1769480 | tf_op jit(solution)/shard_map/ppermute | solution.py:69
  97.2 17.6 %collective-permute-start.8 = (bf16[768,2,192]{0,2,1:T(8,128)(2,1)S(1)}, bf16[768,2,192]{0,2,1:T(8,128)(2,1)S(1)}, u32[]{:S(2)}, u32[]{:S(2)}) collective-permute-start(bf16[768,2,192]{0,2,1:T(8,128)(2,1)S(1)} %pad_maximum_fusion.3), channel_id=1, source_target_pairs={{0,6},{2,0},{4,2},{6,4},{1,7},{3,1},{5,3},{7,5},{8,14},{10,8},{12,... | collective-permute-start | bytes 1769480 | tf_op jit(solution)/shard_map/ppermute | solution.py:70
  116.3 28.3 %collective-permute-start.9 = (bf16[768,192]{0,1:T(8,128)(2,1)S(1)}, bf16[768,192]{0,1:T(8,128)(2,1)S(1)}, u32[]{:S(2)}, u32[]{:S(2)}) collective-permute-start(bf16[768,192]{0,1:T(8,128)(2,1)S(1)} %fusion.18), channel_id=1, source_target_pairs={{0,8},{8,0},{1,9},{9,1},{2,10},{10,2},{3,11},{11,3},{4,12},{12,4},... | collective-permute-start | bytes 884744 | tf_op jit(solution)/shard_map/ppermute | solution.py:95

commit v4 on v3

--- a/solution.py
+++ b/solution.py
@@ -71,17 +71,14 @@
     return pick(block, 1, x) + got_left.astype(jnp.float32) + got_right.astype(jnp.float32)
 
 
-def reduce_scatter(parts):
-    c = lax.axis_index("c")
+def reduce_scatter(mine, other):
     zh = lax.axis_index("zh")
-    n_c, n_x, n_zh = parts.shape[3], parts.shape[2], parts.shape[1]
-    if n_c > 1:
-        got = lax.ppermute(
-            pick(parts, 3, 1 - c).astype(jnp.bfloat16), "c", [(0, 1), (1, 0)]
-        )
-        sums = pick(parts, 3, c) + got.astype(jnp.float32)
+    n_x, n_zh = mine.shape[2], mine.shape[1]
+    if other is not None:
+        got = lax.ppermute(other.astype(jnp.bfloat16), "c", [(0, 1), (1, 0)])
+        sums = mine + got.astype(jnp.float32)
     else:
-        sums = parts[:, :, :, 0]
+        sums = mine
     if n_x == 4:
         sums = four_scatter(jnp.swapaxes(sums, 1, 2))
     elif n_x > 1:
@@ -225,16 +222,29 @@
     owned = partials[:, rows_dev : 2 * rows_dev] + from_next + from_prev
     key_grads = owned[0].astype(jnp.bfloat16).reshape(rows_dev, heads_dev * HD)
     value_grads = owned[1].astype(jnp.bfloat16).reshape(rows_dev, heads_dev * HD)
-    grad_stack = jnp.stack(
-        [jnp.concatenate(query_grads, axis=1), key_grads, value_grads]
-    )
+    query_grads = jnp.concatenate(query_grads, axis=1)
+    return reduce_scatter(*project(query_grads, key_grads, value_grads, projection)).astype(
+        jnp.bfloat16
+    )
+
+
+def project(query_grads, key_grads, value_grads, projection):
     n_zh, n_x, n_c = (lax.axis_size(a) for a in HEAD_AXES)
+    c = lax.axis_index("c")
+    features = projection.shape[1]
     width = projection.shape[2] // (n_zh * n_x * n_c)
-    weight = projection.reshape(3, heads_dev * HD, n_zh, n_x, n_c, width)
-    parts = jnp.einsum(
-        "cik,ckzxym->izxym", grad_stack, weight, preferred_element_type=jnp.float32
-    )
-    return reduce_scatter(parts).astype(jnp.bfloat16)
+    weight = projection.reshape(3, features, n_zh, n_x, n_c, width)
+    grads = (query_grads, key_grads, value_grads)
+
+    def term(columns):
+        return sum(
+            jnp.einsum("ik,kzxm->izxm", g, columns[j], preferred_element_type=jnp.float32)
+            for j, g in enumerate(grads)
+        )
+
+    mine = term(pick(weight, 4, c))
+    other = term(pick(weight, 4, 1 - c)).astype(jnp.bfloat16) if n_c > 1 else None
+    return mine, other
 
 
 def head_shape(n_head):

time: 146 us -> 147 us (level)
  other arithmetic: 11 us -> 16.7 us
  waiting for transfers between devices: 75.8 us -> 71.2 us
  local copies, waits for them, and re-layouts: 12.1 us -> 9.58 us
  matrix products: 2.65 us -> 4.62 us
    unnamed x0 -> x6, matrix products: none -> 4.62 us
    unnamed x18 -> x20, local copies, waits for them, and re-layouts: 9.18 us -> 5.01 us
    dot_general x1 -> x0, matrix products: 2.65 us -> none  [local(): jnp.einsum('cik,ckzxym->izxym', grad_stack, weight, preferred_element_typ...]
    ppermute x1, waiting for transfers between devices: 2.53 us -> 0.01 us  [with_halo(): lax.ppermute(tail, axis, [(i, (i + 1) % count) for i in range(count)])]
    convert_element_type x1 -> x2, other arithmetic: 0.76 us -> 3.27 us  [the longest x1 2.5 us: project(): term(pick(weight, 4, 1 - c)).astype(jnp.bfloat16)]
    ppermute x1, waiting for transfers between devices: 4.58 us -> 2.24 us  [reduce_scatter(): got = lax.ppermute(other.astype(jnp.bfloat16), 'c', [(0, 1), (1, 0)])]
    ppermute x2, waiting for transfers between devices: 16.4 us -> 18.6 us  [passed_along(): return lax.ppermute(block, axis, route)]
    another operation x1, local copies, waits for them, and re-layouts: 0.13 us -> 1.74 us
  transfers between devices with their start and end apart: 10 -> 10, of which waited for: 9 -> 8; matrix products, arithmetic and copies ran while one was open for 6% -> 10% of each run, Pallas kernels for 0% -> 0%
where the time goes in v4:
time: 147 us; the launch traced here: 146 us
  waiting for transfers between devices  71.2 us (48%)
  starting transfers between devices  35.9 us (24%)
  other arithmetic  16.7 us (11%)
  local copies, waits for them, and re-layouts  9.58 us (7%)
  Pallas kernels  7.41 us (5%)
  matrix products  4.62 us (3%)
    ppermute x1, waiting for transfers between devices, reduce_scatter(): got = lax.ppermute(acc.astype(jnp.bfloat16), 'zh', route)  19.2 us
    ppermute x2, waiting for transfers between devices, passed_along(): return lax.ppermute(block, axis, route)  18.6 us
    ppermute x1, waiting for transfers between devices, with_halo(): lax.ppermute(head, axis, [((i + 1) % count, i) for i in range(count)])  12.4 us
    ppermute x1, waiting for transfers between devices, four_scatter(): got_left = lax.ppermute(to_right.astype(jnp.bfloat16), 'x', cw)  9.31 us
    ppermute x1, starting transfers between devices, reduce_scatter(): got = lax.ppermute(acc.astype(jnp.bfloat16), 'zh', route)  9.08 us
    pallas_call x1, Pallas kernels, attention(): pl.pallas_call(attention_kernel, grid=(tiles,), in_specs=[row_spec, row_s...  7.41 us
    ppermute x2, starting transfers between devices, passed_along(): return lax.ppermute(block, axis, route)  7.01 us
    ppermute x1, waiting for transfers between devices, four_scatter(): got_right = lax.ppermute(to_left.astype(jnp.bfloat16), 'x', ccw)  5.84 us
  transfers between devices with their start and end apart: 10, of which 8 were waited for; matrix products, arithmetic and copies ran while one was open for 10% of the time, Pallas kernels for 0%

profile of v4, /device:TPU:70, one launch (start us, length us, event | category | flops | bytes accessed | tf_op | source)
XLA Modules:
  0.0 145.9 jit_solution(16152245879475854842)
XLA Ops:
  0.0 1.8 %pad_maximum_fusion.4 = bf16[2,768,128]{2,1,0:T(8,128)(2,1)} fusion(bf16[1,768,128]{2,1,0:T(8,128)(2,1)} %bitcast.126, bf16[1,768,128]{2,1,0:T(8,128)(2,1)} %bitcast.128), kind=kLoop, calls=%fused_computation.31 | loop fusion | flops 196608 | bytes 786432 | tf_op jit(solution)/shard_map/stack | solution.py:185
  1.8 4.3 %collective-permute-start = (bf16[2,768,128]{2,1,0:T(8,128)(2,1)}, bf16[2,768,128]{2,1,0:T(8,128)(2,1)S(1)}, u32[]{:S(2)}, u32[]{:S(2)}) collective-permute-start(bf16[2,768,128]{2,1,0:T(8,128)(2,1)} %pad_maximum_fusion.4), channel_id=1, source_target_pairs={{0,16},{16,32},{32,48},{48,64},{64,80},{80,96},{96,112},{112,128},... | collective-permute-start | bytes 1179656 | tf_op jit(solution)/shard_map/ppermute | solution.py:21
  6.1 1.9 %collective-permute-start.1 = (bf16[2,768,128]{2,1,0:T(8,128)(2,1)}, bf16[2,768,128]{2,1,0:T(8,128)(2,1)}, u32[]{:S(2)}, u32[]{:S(2)}) collective-permute-start(bf16[2,768,128]{2,1,0:T(8,128)(2,1)} %pad_maximum_fusion.4), channel_id=1, source_target_pairs={{16,0},{32,16},{48,32},{64,48},{80,64},{96,80},{112,96},{128,112},... | collective-permute-start | bytes 1179656 | tf_op jit(solution)/shard_map/ppermute | solution.py:23
  12.2 3.2 %copy.18 = bf16[3,128,3072]{1,2,0:T(8,128)(2,1)S(1)} copy(bf16[3,128,3072]{2,1,0:T(8,128)(2,1)} %param.13) | data formatting | bytes 4718592 | tf_op args[5]
  15.5 12.4 %collective-permute-done.1 = bf16[2,768,128]{2,1,0:T(8,128)(2,1)} collective-permute-done((bf16[2,768,128]{2,1,0:T(8,128)(2,1)}, bf16[2,768,128]{2,1,0:T(8,128)(2,1)}, u32[]{:S(2)}, u32[]{:S(2)}) %collective-permute-start.1) | collective-permute-done | bytes 393248 | tf_op jit(solution)/shard_map/ppermute | solution.py:23
  29.1 7.4 %shard_map.82 = (bf16[768,128]{1,0:T(8,128)(2,1)S(1)}, f32[2304,128]{1,0:T(8,128)S(1)}, f32[2304,128]{1,0:T(8,128)S(1)}) custom-call(bf16[768,128]{1,0:T(8,128)(2,1)S(1)} %copy-done, bf16[768,128]{1,0:T(8,128)(2,1)S(1)} %copy-done.1, bf16[768,128]{1,0:T(8,128)(2,1)S(1)} %copy-done.2, bf16[2304,128]{1,0:T(8,128)(2,1)S(1)} %get-tuple-element.24.k_ref, ...), custom_call_target="tpu_custom_call" | custom-call | flops 2264924160 | bytes 4128768 | tf_op jit(solution)/shard_map/pallas_call | solution.py:145
  36.8 1.9 %collective-permute-start.2 = (bf16[2,768,1,128]{3,1,2,0:T(8,128)(2,1)S(1)}, bf16[2,768,1,128]{3,1,2,0:T(8,128)(2,1)S(1)}, u32[]{:S(2)}, u32[]{:S(2)}) collective-permute-start(bf16[2,768,1,128]{3,1,2,0:T(8,128)(2,1)S(1)} %get-tuple-element.21), channel_id=1, source_target_pairs={{16,0},{32,16},{48,32},{64,48},{80,64},{96,80},{112,96},{128,112},... | collective-permute-start | bytes 1179656 | tf_op jit(solution)/shard_map/ppermute | solution.py:32
  38.7 5.1 %collective-permute-start.3 = (bf16[2,768,1,128]{3,1,2,0:T(8,128)(2,1)S(1)}, bf16[2,768,1,128]{3,1,2,0:T(8,128)(2,1)S(1)}, u32[]{:S(2)}, u32[]{:S(2)}) collective-permute-start(bf16[2,768,1,128]{3,1,2,0:T(8,128)(2,1)S(1)} %get-tuple-element.22), channel_id=1, source_target_pairs={{752,0},{0,16},{16,32},{32,48},{48,64},{64,80},{80,96},{96,112},{1... | collective-permute-start | bytes 1179656 | tf_op jit(solution)/shard_map/ppermute | solution.py:32
  45.7 5.5 %collective-permute-done.2 = bf16[2,768,1,128]{3,1,2,0:T(8,128)(2,1)S(1)} collective-permute-done((bf16[2,768,1,128]{3,1,2,0:T(8,128)(2,1)S(1)}, bf16[2,768,1,128]{3,1,2,0:T(8,128)(2,1)S(1)}, u32[]{:S(2)}, u32[]{:S(2)}) %collective-permute-start.2) | collective-permute-done | bytes 393248 | tf_op jit(solution)/shard_map/ppermute | solution.py:32
  51.2 13.1 %collective-permute-done.3 = bf16[2,768,1,128]{3,1,2,0:T(8,128)(2,1)S(1)} collective-permute-done((bf16[2,768,1,128]{3,1,2,0:T(8,128)(2,1)S(1)}, bf16[2,768,1,128]{3,1,2,0:T(8,128)(2,1)S(1)}, u32[]{:S(2)}, u32[]{:S(2)}) %collective-permute-start.3) | collective-permute-done | bytes 393248 | tf_op jit(solution)/shard_map/ppermute | solution.py:32
  66.0 2.5 %add_convert_fusion = bf16[768,2,4,192]{0,3,2,1:T(8,128)(2,1)} fusion(f32[768,2,4,192]{0,3,2,1:T(8,128)S(1)} %bitcast.118, f32[768,2,4,192]{0,3,2,1:T(8,128)S(1)} %bitcast.113, f32[768,2,4,192]{0,3,2,1:T(8,128)S(1)} %bitcast.117), kind=kLoop, calls=%fused_computation.1 | loop fusion | flops 3538944 | bytes 16515072 | tf_op jit(solution)/shard_map/convert_element_type | solution.py:246
  68.5 1.9 %collective-permute-start.4 = (bf16[768,2,4,192]{0,3,2,1:T(8,128)(2,1)}, bf16[768,2,4,192]{0,3,2,1:T(8,128)(2,1)}, u32[]{:S(2)}, u32[]{:S(2)}) collective-permute-start(bf16[768,2,4,192]{0,3,2,1:T(8,128)(2,1)} %add_convert_fusion), channel_id=1, source_target_pairs={{0,1},{1,0},{2,3},{3,2},{4,5},{5,4},{6,7},{7,6},{8,9},{9,8},{10,11... | collective-permute-start | bytes 7077896 | tf_op jit(solution)/shard_map/ppermute | solution.py:78
  73.0 2.2 %collective-permute-done.4 = bf16[768,2,4,192]{0,3,2,1:T(8,128)(2,1)} collective-permute-done((bf16[768,2,4,192]{0,3,2,1:T(8,128)(2,1)}, bf16[768,2,4,192]{0,3,2,1:T(8,128)(2,1)}, u32[]{:S(2)}, u32[]{:S(2)}) %collective-permute-start.4) | collective-permute-done | bytes 2359328 | tf_op jit(solution)/shard_map/ppermute | solution.py:78
  75.2 5.0 %convert_add_fusion = f32[768,2,4,192]{0,3,2,1:T(8,128)} fusion(bf16[768,2,4,192]{0,3,2,1:T(8,128)(2,1)} %collective-permute-done.4, f32[768,2,4,192]{0,3,2,1:T(8,128)S(1)} %bitcast.116, f32[768,2,4,192]{0,3,2,1:T(8,128)S(1)} %bitcast.114, f32[768,2,4,192]{0,3,2,1:T(8,128)S(1)} %bitcast.115), kind=kLoop, calls=%fused_computation | loop fusion | flops 4718592 | bytes 21233664 | tf_op jit(solution)/shard_map/add | solution.py:79
  80.2 1.7 %dynamic-slice_bitcast_fusion = (bf16[768,2,1,192]{0,3,1,2:T(8,128)(2,1)S(1)}, bf16[768,2,1,192]{0,3,1,2:T(8,128)(2,1)S(1)}) fusion(f32[768,2,4,192]{0,3,2,1:T(8,128)} %convert_add_fusion, s32[]{:T(128)S(6)} %select_n.88, s32[]{:T(128)S(6)} %select_n.86), kind=kLoop, calls=%fused_computation.10 | loop fusion | bytes 2359304 | tf_op jit(solution)/shard_map/dynamic-slice.3
  82.1 1.9 %collective-permute-start.5 = (bf16[384,2,192]{0,2,1:T(8,128)(2,1)S(1)}, bf16[384,2,192]{0,2,1:T(8,128)(2,1)S(1)}, u32[]{:S(2)}, u32[]{:S(2)}) collective-permute-start(bf16[384,2,192]{0,2,1:T(8,128)(2,1)S(1)} %get-tuple-element.25), channel_id=1, source_target_pairs={{0,2},{2,4},{4,6},{6,0},{1,3},{3,5},{5,7},{7,1},{8,10},{10,12},{12... | collective-permute-start | bytes 884744 | tf_op jit(solution)/shard_map/ppermute | solution.py:63
  84.0 3.9 %collective-permute-start.7 = (bf16[384,2,192]{0,2,1:T(8,128)(2,1)S(1)}, bf16[384,2,192]{0,2,1:T(8,128)(2,1)S(1)}, u32[]{:S(2)}, u32[]{:S(2)}) collective-permute-start(bf16[384,2,192]{0,2,1:T(8,128)(2,1)S(1)} %get-tuple-element.26), channel_id=1, source_target_pairs={{0,6},{2,0},{4,2},{6,4},{1,7},{3,1},{5,3},{7,5},{8,14},{10,8},{12,... | collective-permute-start | bytes 884744 | tf_op jit(solution)/shard_map/ppermute | solution.py:64
  89.4 3.6 %collective-permute-done.5 = bf16[384,2,192]{0,2,1:T(8,128)(2,1)S(1)} collective-permute-done((bf16[384,2,192]{0,2,1:T(8,128)(2,1)S(1)}, bf16[384,2,192]{0,2,1:T(8,128)(2,1)S(1)}, u32[]{:S(2)}, u32[]{:S(2)}) %collective-permute-start.5) | collective-permute-done | bytes 294944 | tf_op jit(solution)/shard_map/ppermute | solution.py:63
  93.1 3.4 %collective-permute-start.6 = (bf16[768,2,192]{0,2,1:T(8,128)(2,1)S(1)}, bf16[768,2,192]{0,2,1:T(8,128)(2,1)S(1)}, u32[]{:S(2)}, u32[]{:S(2)}) collective-permute-start(bf16[768,2,192]{0,2,1:T(8,128)(2,1)S(1)} %pad_maximum_fusion.2), channel_id=1, source_target_pairs={{0,2},{2,4},{4,6},{6,0},{1,3},{3,5},{5,7},{7,1},{8,10},{10,12},{12... | collective-permute-start | bytes 1769480 | tf_op jit(solution)/shard_map/ppermute | solution.py:69
  97.8 2.4 %collective-permute-start.8 = (bf16[768,2,192]{0,2,1:T(8,128)(2,1)S(1)}, bf16[768,2,192]{0,2,1:T(8,128)(2,1)S(1)}, u32[]{:S(2)}, u32[]{:S(2)}) collective-permute-start(bf16[768,2,192]{0,2,1:T(8,128)(2,1)S(1)} %pad_maximum_fusion.3), channel_id=1, source_target_pairs={{0,6},{2,0},{4,2},{6,4},{1,7},{3,1},{5,3},{7,5},{8,14},{10,8},{12,... | collective-permute-start | bytes 1769480 | tf_op jit(solution)/shard_map/ppermute | solution.py:70
  100.2 9.3 %collective-permute-done.6 = bf16[768,2,192]{0,2,1:T(8,128)(2,1)S(1)} collective-permute-done((bf16[768,2,192]{0,2,1:T(8,128)(2,1)S(1)}, bf16[768,2,192]{0,2,1:T(8,128)(2,1)S(1)}, u32[]{:S(2)}, u32[]{:S(2)}) %collective-permute-start.6) | collective-permute-done | bytes 589856 | tf_op jit(solution)/shard_map/ppermute | solution.py:69
  109.5 5.8 %collective-permute-done.8 = bf16[768,2,192]{0,2,1:T(8,128)(2,1)S(1)} collective-permute-done((bf16[768,2,192]{0,2,1:T(8,128)(2,1)S(1)}, bf16[768,2,192]{0,2,1:T(8,128)(2,1)S(1)}, u32[]{:S(2)}, u32[]{:S(2)}) %collective-permute-start.8) | collective-permute-done | bytes 589856 | tf_op jit(solution)/shard_map/ppermute | solution.py:70
  116.9 9.1 %collective-permute-start.9 = (bf16[768,192]{0,1:T(8,128)(2,1)S(1)}, bf16[768,192]{0,1:T(8,128)(2,1)S(1)}, u32[]{:S(2)}, u32[]{:S(2)}) collective-permute-start(bf16[768,192]{0,1:T(8,128)(2,1)S(1)} %fusion.11), channel_id=1, source_target_pairs={{0,8},{8,0},{1,9},{9,1},{2,10},{10,2},{3,11},{11,3},{4,12},{12,4},... | collective-permute-start | bytes 884744 | tf_op jit(solution)/shard_map/ppermute | solution.py:92
  126.0 19.2 %collective-permute-done.9 = bf16[768,192]{0,1:T(8,128)(2,1)S(1)} collective-permute-done((bf16[768,192]{0,1:T(8,128)(2,1)S(1)}, bf16[768,192]{0,1:T(8,128)(2,1)S(1)}, u32[]{:S(2)}, u32[]{:S(2)}) %collective-permute-start.9) | collective-permute-done | bytes 294944 | tf_op jit(solution)/shard_map/ppermute | solution.py:92
  (54 shorter events, 16.7 us)
Async XLA Ops:
  1.8 13.7 %collective-permute-start = (bf16[2,768,128]{2,1,0:T(8,128)(2,1)}, bf16[2,768,128]{2,1,0:T(8,128)(2,1)S(1)}, u32[]{:S(2)}, u32[]{:S(2)}) collective-permute-start(bf16[2,768,128]{2,1,0:T(8,128)(2,1)} %pad_maximum_fusion.4), channel_id=1, source_target_pairs={{0,16},{16,32},{32,48},{48,64},{64,80},{80,96},{96,112},{112,128},... | collective-permute-start | bytes 1179656 | tf_op jit(solution)/shard_map/ppermute | solution.py:21
  6.1 21.9 %collective-permute-start.1 = (bf16[2,768,128]{2,1,0:T(8,128)(2,1)}, bf16[2,768,128]{2,1,0:T(8,128)(2,1)}, u32[]{:S(2)}, u32[]{:S(2)}) collective-permute-start(bf16[2,768,128]{2,1,0:T(8,128)(2,1)} %pad_maximum_fusion.4), channel_id=1, source_target_pairs={{16,0},{32,16},{48,32},{64,48},{80,64},{96,80},{112,96},{128,112},... | collective-permute-start | bytes 1179656 | tf_op jit(solution)/shard_map/ppermute | solution.py:23
  12.2 15.7 %copy-start.5 = (bf16[768,128]{1,0:T(8,128)(2,1)S(1)}, bf16[768,128]{1,0:T(8,128)(2,1)}, u32[]{:S(2)}) copy-start(bf16[768,128]{1,0:T(8,128)(2,1)} %param.10) | copy-start | bytes 589828
  12.2 15.7 %copy-start.6 = (bf16[768,128]{1,0:T(8,128)(2,1)S(1)}, bf16[768,128]{1,0:T(8,128)(2,1)}, u32[]{:S(2)}) copy-start(bf16[768,128]{1,0:T(8,128)(2,1)} %param.9) | copy-start | bytes 589828
  15.5 13.6 %copy-start = (bf16[768,128]{1,0:T(8,128)(2,1)S(1)}, bf16[768,128]{1,0:T(8,128)(2,1)}, u32[]{:S(2)}) copy-start(bf16[768,128]{1,0:T(8,128)(2,1)} %q_ref.1) | copy-start | bytes 589828
  15.5 13.6 %copy-start.1 = (bf16[768,128]{1,0:T(8,128)(2,1)S(1)}, bf16[768,128]{1,0:T(8,128)(2,1)}, u32[]{:S(2)}) copy-start(bf16[768,128]{1,0:T(8,128)(2,1)} %do_ref.1) | copy-start | bytes 589828
  15.5 13.6 %copy-start.2 = (bf16[768,128]{1,0:T(8,128)(2,1)S(1)}, bf16[768,128]{1,0:T(8,128)(2,1)}, u32[]{:S(2)}) copy-start(bf16[768,128]{1,0:T(8,128)(2,1)} %o_ref.1) | copy-start | bytes 589828
  36.8 14.4 %collective-permute-start.2 = (bf16[2,768,1,128]{3,1,2,0:T(8,128)(2,1)S(1)}, bf16[2,768,1,128]{3,1,2,0:T(8,128)(2,1)S(1)}, u32[]{:S(2)}, u32[]{:S(2)}) collective-permute-start(bf16[2,768,1,128]{3,1,2,0:T(8,128)(2,1)S(1)} %get-tuple-element.21), channel_id=1, source_target_pairs={{16,0},{32,16},{48,32},{64,48},{80,64},{96,80},{112,96},{128,112},... | collective-permute-start | bytes 1179656 | tf_op jit(solution)/shard_map/ppermute | solution.py:32
  38.7 25.6 %collective-permute-start.3 = (bf16[2,768,1,128]{3,1,2,0:T(8,128)(2,1)S(1)}, bf16[2,768,1,128]{3,1,2,0:T(8,128)(2,1)S(1)}, u32[]{:S(2)}, u32[]{:S(2)}) collective-permute-start(bf16[2,768,1,128]{3,1,2,0:T(8,128)(2,1)S(1)} %get-tuple-element.22), channel_id=1, source_target_pairs={{752,0},{0,16},{16,32},{32,48},{48,64},{64,80},{80,96},{96,112},{1... | collective-permute-start | bytes 1179656 | tf_op jit(solution)/shard_map/ppermute | solution.py:32
  66.0 4.5 %copy-start.4 = (bf16[1,128,2,4,1,192]{1,5,4,3,2,0:T(8,128)(2,1)S(1)}, bf16[1,128,2,4,1,192]{1,5,4,3,2,0:T(8,128)(2,1)}, u32[]{:S(2)}) copy-start(bf16[1,128,2,4,1,192]{1,5,4,3,2,0:T(8,128)(2,1)} %get-tuple-element.18) | copy-start | bytes 1179652
  68.5 6.8 %collective-permute-start.4 = (bf16[768,2,4,192]{0,3,2,1:T(8,128)(2,1)}, bf16[768,2,4,192]{0,3,2,1:T(8,128)(2,1)}, u32[]{:S(2)}, u32[]{:S(2)}) collective-permute-start(bf16[768,2,4,192]{0,3,2,1:T(8,128)(2,1)} %add_convert_fusion), channel_id=1, source_target_pairs={{0,1},{1,0},{2,3},{3,2},{4,5},{5,4},{6,7},{7,6},{8,9},{9,8},{10,11... | collective-permute-start | bytes 7077896 | tf_op jit(solution)/shard_map/ppermute | solution.py:78
  71.2 1.0 copy-start.3
  82.1 10.9 %collective-permute-start.5 = (bf16[384,2,192]{0,2,1:T(8,128)(2,1)S(1)}, bf16[384,2,192]{0,2,1:T(8,128)(2,1)S(1)}, u32[]{:S(2)}, u32[]{:S(2)}) collective-permute-start(bf16[384,2,192]{0,2,1:T(8,128)(2,1)S(1)} %get-tuple-element.25), channel_id=1, source_target_pairs={{0,2},{2,4},{4,6},{6,0},{1,3},{3,5},{5,7},{7,1},{8,10},{10,12},{12... | collective-permute-start | bytes 884744 | tf_op jit(solution)/shard_map/ppermute | solution.py:63
  84.0 12.6 %collective-permute-start.7 = (bf16[384,2,192]{0,2,1:T(8,128)(2,1)S(1)}, bf16[384,2,192]{0,2,1:T(8,128)(2,1)S(1)}, u32[]{:S(2)}, u32[]{:S(2)}) collective-permute-start(bf16[384,2,192]{0,2,1:T(8,128)(2,1)S(1)} %get-tuple-element.26), channel_id=1, source_target_pairs={{0,6},{2,0},{4,2},{6,4},{1,7},{3,1},{5,3},{7,5},{8,14},{10,8},{12,... | collective-permute-start | bytes 884744 | tf_op jit(solution)/shard_map/ppermute | solution.py:64
  93.1 16.4 %collective-permute-start.6 = (bf16[768,2,192]{0,2,1:T(8,128)(2,1)S(1)}, bf16[768,2,192]{0,2,1:T(8,128)(2,1)S(1)}, u32[]{:S(2)}, u32[]{:S(2)}) collective-permute-start(bf16[768,2,192]{0,2,1:T(8,128)(2,1)S(1)} %pad_maximum_fusion.2), channel_id=1, source_target_pairs={{0,2},{2,4},{4,6},{6,0},{1,3},{3,5},{5,7},{7,1},{8,10},{10,12},{12... | collective-permute-start | bytes 1769480 | tf_op jit(solution)/shard_map/ppermute | solution.py:69
  97.8 17.6 %collective-permute-start.8 = (bf16[768,2,192]{0,2,1:T(8,128)(2,1)S(1)}, bf16[768,2,192]{0,2,1:T(8,128)(2,1)S(1)}, u32[]{:S(2)}, u32[]{:S(2)}) collective-permute-start(bf16[768,2,192]{0,2,1:T(8,128)(2,1)S(1)} %pad_maximum_fusion.3), channel_id=1, source_target_pairs={{0,6},{2,0},{4,2},{6,4},{1,7},{3,1},{5,3},{7,5},{8,14},{10,8},{12,... | collective-permute-start | bytes 1769480 | tf_op jit(solution)/shard_map/ppermute | solution.py:70
  116.9 28.3 %collective-permute-start.9 = (bf16[768,192]{0,1:T(8,128)(2,1)S(1)}, bf16[768,192]{0,1:T(8,128)(2,1)S(1)}, u32[]{:S(2)}, u32[]{:S(2)}) collective-permute-start(bf16[768,192]{0,1:T(8,128)(2,1)S(1)} %fusion.11), channel_id=1, source_target_pairs={{0,8},{8,0},{1,9},{9,1},{2,10},{10,2},{3,11},{11,3},{4,12},{12,4},... | collective-permute-start | bytes 884744 | tf_op jit(solution)/shard_map/ppermute | solution.py:92

commit v5 on v4

--- a/solution.py
+++ b/solution.py
@@ -71,14 +71,9 @@
     return pick(block, 1, x) + got_left.astype(jnp.float32) + got_right.astype(jnp.float32)
 
 
-def reduce_scatter(mine, other):
+def reduce_scatter(sums):
     zh = lax.axis_index("zh")
-    n_x, n_zh = mine.shape[2], mine.shape[1]
-    if other is not None:
-        got = lax.ppermute(other.astype(jnp.bfloat16), "c", [(0, 1), (1, 0)])
-        sums = mine + got.astype(jnp.float32)
-    else:
-        sums = mine
+    n_x, n_zh = sums.shape[2], sums.shape[1]
     if n_x == 4:
         sums = four_scatter(jnp.swapaxes(sums, 1, 2))
     elif n_x > 1:
@@ -182,6 +177,7 @@
     win = 3 * tiles_dev
     score_scale = HD ** (-0.5)
     first_tile = (place - 1) * tiles_dev
+    weights = core_weights(projection)
     window = with_halo(jnp.stack([key_rows, value_rows]), "seq", rows_dev)
     key_window = window[0].reshape(win * TILE, heads_dev, HD)
     value_window = window[1].reshape(win * TILE, heads_dev, HD)
@@ -210,6 +206,7 @@
         query_grads.append(dq)
         key_accs.append(dk)
         value_accs.append(dv)
+    query_grads = jnp.concatenate(query_grads, axis=1)
     key_acc = jnp.stack(key_accs, axis=1)
     value_acc = jnp.stack(value_accs, axis=1)
     partials = jnp.stack([key_acc, value_acc])
@@ -222,29 +219,34 @@
     owned = partials[:, rows_dev : 2 * rows_dev] + from_next + from_prev
     key_grads = owned[0].astype(jnp.bfloat16).reshape(rows_dev, heads_dev * HD)
     value_grads = owned[1].astype(jnp.bfloat16).reshape(rows_dev, heads_dev * HD)
-    query_grads = jnp.concatenate(query_grads, axis=1)
-    return reduce_scatter(*project(query_grads, key_grads, value_grads, projection)).astype(
-        jnp.bfloat16
-    )
-
-
-def project(query_grads, key_grads, value_grads, projection):
+    sums = project((query_grads, key_grads, value_grads), weights)
+    return reduce_scatter(sums).astype(jnp.bfloat16)
+
+
+def core_weights(projection):
     n_zh, n_x, n_c = (lax.axis_size(a) for a in HEAD_AXES)
     c = lax.axis_index("c")
     features = projection.shape[1]
     width = projection.shape[2] // (n_zh * n_x * n_c)
     weight = projection.reshape(3, features, n_zh, n_x, n_c, width)
-    grads = (query_grads, key_grads, value_grads)
-
-    def term(columns):
-        return sum(
-            jnp.einsum("ik,kzxm->izxm", g, columns[j], preferred_element_type=jnp.float32)
-            for j, g in enumerate(grads)
-        )
-
-    mine = term(pick(weight, 4, c))
-    other = term(pick(weight, 4, 1 - c)).astype(jnp.bfloat16) if n_c > 1 else None
-    return mine, other
+    mine = pick(weight, 4, c)
+    if n_c == 1:
+        return mine, None
+    partner = lax.ppermute(pick(weight, 4, 1 - c), "c", [(0, 1), (1, 0)])
+    return mine, partner
+
+
+def project(grads, weights):
+    mine_w, partner_w = weights
+    total = 0.0
+    for j, g in enumerate(grads):
+        total = total + jnp.einsum("ik,kzxm->izxm", g, mine_w[j], preferred_element_type=jnp.float32)
+        if partner_w is not None:
+            got = lax.ppermute(g, "c", [(0, 1), (1, 0)])
+            total = total + jnp.einsum(
+                "ik,kzxm->izxm", got, partner_w[j], preferred_element_type=jnp.float32
+            )
+    return total
 
 
 def head_shape(n_head):

time: 147 us -> 153 us (1.041)
  starting transfers between devices: 35.9 us -> 42.1 us
  waiting for transfers between devices: 71.2 us -> 65.1 us
  matrix products: 4.62 us -> 10.2 us
  local copies, waits for them, and re-layouts: 9.58 us -> 12.3 us
  other arithmetic: 16.7 us -> 14.4 us
    ppermute x1 -> x4, starting transfers between devices: 1.91 us -> 8.14 us  [the longest x3 6.24 us: project(): got = lax.ppermute(g, 'c', [(0, 1), (1, 0)])]
    unnamed x6, matrix products: 4.62 us -> 10.2 us
    convert_element_type x2 -> x1, other arithmetic: 3.27 us -> 0.76 us  [local(): return reduce_scatter(sums).astype(jnp.bfloat16)]
    ppermute x2, waiting for transfers between devices: 18.6 us -> 16.2 us  [passed_along(): return lax.ppermute(block, axis, route)]
    ppermute x1 -> x4, waiting for transfers between devices: 2.24 us -> 0.01 us  [the longest x3 0.01 us: project(): got = lax.ppermute(g, 'c', [(0, 1), (1, 0)])]
    add x1 -> x2, other arithmetic: 5.01 us -> 6.2 us  [the longest x1 4.96 us: project(): total + jnp.einsum('ik,kzxm->izxm', got, partner_w[j], preferred_element_...]
    unnamed x20 -> x26, local copies, waits for them, and re-layouts: 5.01 us -> 5.38 us
  transfers between devices with their start and end apart: 10 -> 13, of which waited for: 8 -> 7; matrix products, arithmetic and copies ran while one was open for 10% -> 15% of each run, Pallas kernels for 0% -> 5%
where the time goes in v5:
time: 153 us; the launch traced here: 152 us
  waiting for transfers between devices  65.1 us (43%)
  starting transfers between devices  42.1 us (28%)
  other arithmetic  14.4 us (9%)
  local copies, waits for them, and re-layouts  12.3 us (8%)
  matrix products  10.2 us (7%)
  Pallas kernels  7.41 us (5%)
    ppermute x1, waiting for transfers between devices, reduce_scatter(): got = lax.ppermute(acc.astype(jnp.bfloat16), 'zh', route)  19.1 us
    ppermute x2, waiting for transfers between devices, passed_along(): return lax.ppermute(block, axis, route)  16.2 us
    ppermute x1, waiting for transfers between devices, with_halo(): lax.ppermute(head, axis, [((i + 1) % count, i) for i in range(count)])  11.2 us
    unnamed x6, matrix products  10.2 us
    ppermute x1, waiting for transfers between devices, four_scatter(): got_left = lax.ppermute(to_right.astype(jnp.bfloat16), 'x', cw)  9.22 us
    ppermute x1, starting transfers between devices, reduce_scatter(): got = lax.ppermute(acc.astype(jnp.bfloat16), 'zh', route)  9.05 us
    pallas_call x1, Pallas kernels, attention(): pl.pallas_call(attention_kernel, grid=(tiles,), in_specs=[row_spec, row_s...  7.41 us
    ppermute x2, starting transfers between devices, passed_along(): return lax.ppermute(block, axis, route)  7 us
  transfers between devices with their start and end apart: 13, of which 7 were waited for; matrix products, arithmetic and copies ran while one was open for 15% of the time, Pallas kernels for 5%

profile of v5, /device:TPU:70, one launch (start us, length us, event | category | flops | bytes accessed | tf_op | source)
XLA Modules:
  0.0 152.0 jit_solution(9084817847429219445)
XLA Ops:
  1.8 4.3 %collective-permute-start = (bf16[2,768,128]{2,1,0:T(8,128)(2,1)}, bf16[2,768,128]{2,1,0:T(8,128)(2,1)S(1)}, u32[]{:S(2)}, u32[]{:S(2)}) collective-permute-start(bf16[2,768,128]{2,1,0:T(8,128)(2,1)} %pad_maximum_fusion.4), channel_id=1, source_target_pairs={{0,16},{16,32},{32,48},{48,64},{64,80},{80,96},{96,112},{112,128},... | collective-permute-start | bytes 1179656 | tf_op jit(solution)/shard_map/ppermute | solution.py:21
  6.1 1.9 %collective-permute-start.1 = (bf16[2,768,128]{2,1,0:T(8,128)(2,1)}, bf16[2,768,128]{2,1,0:T(8,128)(2,1)}, u32[]{:S(2)}, u32[]{:S(2)}) collective-permute-start(bf16[2,768,128]{2,1,0:T(8,128)(2,1)} %pad_maximum_fusion.4), channel_id=1, source_target_pairs={{16,0},{32,16},{48,32},{64,48},{80,64},{96,80},{112,96},{128,112},... | collective-permute-start | bytes 1179656 | tf_op jit(solution)/shard_map/ppermute | solution.py:23
  8.0 3.0 %copy.17 = bf16[3,128,3072]{1,2,0:T(8,128)(2,1)S(1)} copy(bf16[3,128,3072]{2,1,0:T(8,128)(2,1)} %param.13) | data formatting | bytes 4718592 | tf_op args[5]
  12.3 1.9 %collective-permute-start.3 = (bf16[3,128,2,4,192]{1,4,3,2,0:T(8,128)(2,1)}, bf16[3,128,2,4,192]{1,4,3,2,0:T(8,128)(2,1)}, u32[]{:S(2)}, u32[]{:S(2)}) collective-permute-start(bf16[3,128,2,4,192]{1,4,3,2,0:T(8,128)(2,1)} %dynamic-slice_bitcast_fusion.2), channel_id=1, source_target_pairs={{0,1},{1,0},{2,3},{3,2},{4,5},{5,4},{6,7},{7,6},{8,9},{9,8},{10,11... | collective-permute-start | bytes 3538952 | tf_op jit(solution)/shard_map/ppermute | solution.py:235
  16.8 11.2 %collective-permute-done.1 = bf16[2,768,128]{2,1,0:T(8,128)(2,1)} collective-permute-done((bf16[2,768,128]{2,1,0:T(8,128)(2,1)}, bf16[2,768,128]{2,1,0:T(8,128)(2,1)}, u32[]{:S(2)}, u32[]{:S(2)}) %collective-permute-start.1) | collective-permute-done | bytes 393248 | tf_op jit(solution)/shard_map/ppermute | solution.py:23
  29.1 7.4 %shard_map.82 = (bf16[768,128]{1,0:T(8,128)(2,1)S(1)}, f32[2304,128]{1,0:T(8,128)S(1)}, f32[2304,128]{1,0:T(8,128)S(1)}) custom-call(bf16[768,128]{1,0:T(8,128)(2,1)S(1)} %copy-done, bf16[768,128]{1,0:T(8,128)(2,1)S(1)} %copy-done.1, bf16[768,128]{1,0:T(8,128)(2,1)S(1)} %copy-done.2, bf16[2304,128]{1,0:T(8,128)(2,1)S(1)} %get-tuple-element.24.k_ref, ...), custom_call_target="tpu_custom_call" | custom-call | flops 2264924160 | bytes 4128768 | tf_op jit(solution)/shard_map/pallas_call | solution.py:140
  37.7 1.9 %collective-permute-start.4 = (bf16[2,768,1,128]{3,1,2,0:T(8,128)(2,1)}, bf16[2,768,1,128]{3,1,2,0:T(8,128)(2,1)}, u32[]{:S(2)}, u32[]{:S(2)}) collective-permute-start(bf16[2,768,1,128]{3,1,2,0:T(8,128)(2,1)} %get-tuple-element.21), channel_id=1, source_target_pairs={{16,0},{32,16},{48,32},{64,48},{80,64},{96,80},{112,96},{128,112},... | collective-permute-start | bytes 1179656 | tf_op jit(solution)/shard_map/ppermute | solution.py:32
  39.6 5.1 %collective-permute-start.5 = (bf16[2,768,1,128]{3,1,2,0:T(8,128)(2,1)}, bf16[2,768,1,128]{3,1,2,0:T(8,128)(2,1)}, u32[]{:S(2)}, u32[]{:S(2)}) collective-permute-start(bf16[2,768,1,128]{3,1,2,0:T(8,128)(2,1)} %get-tuple-element.22), channel_id=1, source_target_pairs={{752,0},{0,16},{16,32},{32,48},{48,64},{64,80},{80,96},{96,112},{1... | collective-permute-start | bytes 1179656 | tf_op jit(solution)/shard_map/ppermute | solution.py:32
  49.3 3.1 %collective-permute-done.4 = bf16[2,768,1,128]{3,1,2,0:T(8,128)(2,1)} collective-permute-done((bf16[2,768,1,128]{3,1,2,0:T(8,128)(2,1)}, bf16[2,768,1,128]{3,1,2,0:T(8,128)(2,1)}, u32[]{:S(2)}, u32[]{:S(2)}) %collective-permute-start.4) | collective-permute-done | bytes 393248 | tf_op jit(solution)/shard_map/ppermute | solution.py:32
  52.4 13.1 %collective-permute-done.5 = bf16[2,768,1,128]{3,1,2,0:T(8,128)(2,1)} collective-permute-done((bf16[2,768,1,128]{3,1,2,0:T(8,128)(2,1)}, bf16[2,768,1,128]{3,1,2,0:T(8,128)(2,1)}, u32[]{:S(2)}, u32[]{:S(2)}) %collective-permute-start.5) | collective-permute-done | bytes 393248 | tf_op jit(solution)/shard_map/ppermute | solution.py:32
  66.8 1.9 %collective-permute-start.6 = (bf16[768,128]{1,0:T(8,128)(2,1)S(1)}, bf16[768,128]{1,0:T(8,128)(2,1)S(1)}, u32[]{:S(2)}, u32[]{:S(2)}) collective-permute-start(bf16[768,128]{1,0:T(8,128)(2,1)S(1)} %get-tuple-element.27), channel_id=1, source_target_pairs={{0,1},{1,0},{2,3},{3,2},{4,5},{5,4},{6,7},{7,6},{8,9},{9,8},{10,11... | collective-permute-start | bytes 589832 | tf_op jit(solution)/shard_map/ppermute | solution.py:245
  68.7 2.4 %collective-permute-start.7 = (bf16[768,128]{1,0:T(8,128)(2,1)S(1)}, bf16[768,128]{1,0:T(8,128)(2,1)S(1)}, u32[]{:S(2)}, u32[]{:S(2)}) collective-permute-start(bf16[768,128]{1,0:T(8,128)(2,1)S(1)} %get-tuple-element.28), channel_id=1, source_target_pairs={{0,1},{1,0},{2,3},{3,2},{4,5},{5,4},{6,7},{7,6},{8,9},{9,8},{10,11... | collective-permute-start | bytes 589832 | tf_op jit(solution)/shard_map/ppermute | solution.py:245
  74.8 3.0 %fusion.33 = f32[768,1536]{0,1} fusion(bf16[768,128]{1,0:T(8,128)(2,1)S(1)} %collective-permute-done.7, bf16[128,1536]{0,1:T(8,128)(2,1)S(1)} %bitcast.120), kind=kOutput, calls=%fused_computation.72 | convolution fusion | flops 301989888 | bytes 5308416
  77.8 3.1 %fusion.29 = f32[768,1536]{0,1} fusion(bf16[768,128]{1,0:T(8,128)(2,1)S(1)} %collective-permute-done.2, bf16[128,1536]{0,1:T(8,128)(2,1)S(1)} %bitcast.119), kind=kOutput, calls=%fused_computation.68 | convolution fusion | flops 301989888 | bytes 5308416
  81.7 5.0 %add_add_fusion = f32[768,2,4,192]{0,3,2,1:T(8,128)} fusion(f32[768,2,4,192]{0,3,2,1:T(8,128)S(1)} %bitcast.112, f32[768,2,4,192]{0,3,2,1:T(8,128)S(1)} %bitcast.110, f32[768,2,4,192]{0,3,2,1:T(8,128)S(1)} %bitcast.111, f32[768,2,4,192]{0,3,2,1:T(8,128)S(1)} %bitcast.109, f32[768,2,4,192]{0,3,2,1:T(8,128)S(1)} %bitcast.108, f32[768,2,4,192]{0,3,2,1:T(8,128)} %bitcast.113), kind=kLoop, calls=%fused_computation | loop fusion | flops 5898240 | bytes 33030144 | tf_op jit(solution)/shard_map/add | solution.py:246
  88.4 1.9 %collective-permute-start.8 = (bf16[384,2,192]{0,2,1:T(8,128)(2,1)S(1)}, bf16[384,2,192]{0,2,1:T(8,128)(2,1)S(1)}, u32[]{:S(2)}, u32[]{:S(2)}) collective-permute-start(bf16[384,2,192]{0,2,1:T(8,128)(2,1)S(1)} %get-tuple-element.25), channel_id=1, source_target_pairs={{0,2},{2,4},{4,6},{6,0},{1,3},{3,5},{5,7},{7,1},{8,10},{10,12},{12... | collective-permute-start | bytes 884744 | tf_op jit(solution)/shard_map/ppermute | solution.py:63
  90.4 3.9 %collective-permute-start.10 = (bf16[384,2,192]{0,2,1:T(8,128)(2,1)S(1)}, bf16[384,2,192]{0,2,1:T(8,128)(2,1)S(1)}, u32[]{:S(2)}, u32[]{:S(2)}) collective-permute-start(bf16[384,2,192]{0,2,1:T(8,128)(2,1)S(1)} %get-tuple-element.26), channel_id=1, source_target_pairs={{0,6},{2,0},{4,2},{6,4},{1,7},{3,1},{5,3},{7,5},{8,14},{10,8},{12,... | collective-permute-start | bytes 884744 | tf_op jit(solution)/shard_map/ppermute | solution.py:64
  95.7 3.5 %collective-permute-done.8 = bf16[384,2,192]{0,2,1:T(8,128)(2,1)S(1)} collective-permute-done((bf16[384,2,192]{0,2,1:T(8,128)(2,1)S(1)}, bf16[384,2,192]{0,2,1:T(8,128)(2,1)S(1)}, u32[]{:S(2)}, u32[]{:S(2)}) %collective-permute-start.8) | collective-permute-done | bytes 294944 | tf_op jit(solution)/shard_map/ppermute | solution.py:63
  99.4 3.4 %collective-permute-start.9 = (bf16[768,2,192]{0,2,1:T(8,128)(2,1)S(1)}, bf16[768,2,192]{0,2,1:T(8,128)(2,1)S(1)}, u32[]{:S(2)}, u32[]{:S(2)}) collective-permute-start(bf16[768,2,192]{0,2,1:T(8,128)(2,1)S(1)} %pad_maximum_fusion.2), channel_id=1, source_target_pairs={{0,2},{2,4},{4,6},{6,0},{1,3},{3,5},{5,7},{7,1},{8,10},{10,12},{12... | collective-permute-start | bytes 1769480 | tf_op jit(solution)/shard_map/ppermute | solution.py:69
  104.0 2.4 %collective-permute-start.11 = (bf16[768,2,192]{0,2,1:T(8,128)(2,1)S(1)}, bf16[768,2,192]{0,2,1:T(8,128)(2,1)S(1)}, u32[]{:S(2)}, u32[]{:S(2)}) collective-permute-start(bf16[768,2,192]{0,2,1:T(8,128)(2,1)S(1)} %pad_maximum_fusion.3), channel_id=1, source_target_pairs={{0,6},{2,0},{4,2},{6,4},{1,7},{3,1},{5,3},{7,5},{8,14},{10,8},{12,... | collective-permute-start | bytes 1769480 | tf_op jit(solution)/shard_map/ppermute | solution.py:70
  106.5 9.2 %collective-permute-done.9 = bf16[768,2,192]{0,2,1:T(8,128)(2,1)S(1)} collective-permute-done((bf16[768,2,192]{0,2,1:T(8,128)(2,1)S(1)}, bf16[768,2,192]{0,2,1:T(8,128)(2,1)S(1)}, u32[]{:S(2)}, u32[]{:S(2)}) %collective-permute-start.9) | collective-permute-done | bytes 589856 | tf_op jit(solution)/shard_map/ppermute | solution.py:69
  115.7 5.8 %collective-permute-done.11 = bf16[768,2,192]{0,2,1:T(8,128)(2,1)S(1)} collective-permute-done((bf16[768,2,192]{0,2,1:T(8,128)(2,1)S(1)}, bf16[768,2,192]{0,2,1:T(8,128)(2,1)S(1)}, u32[]{:S(2)}, u32[]{:S(2)}) %collective-permute-start.11) | collective-permute-done | bytes 589856 | tf_op jit(solution)/shard_map/ppermute | solution.py:70
  123.0 9.0 %collective-permute-start.12 = (bf16[768,192]{0,1:T(8,128)(2,1)S(1)}, bf16[768,192]{0,1:T(8,128)(2,1)S(1)}, u32[]{:S(2)}, u32[]{:S(2)}) collective-permute-start(bf16[768,192]{0,1:T(8,128)(2,1)S(1)} %fusion.10), channel_id=1, source_target_pairs={{0,8},{8,0},{1,9},{9,1},{2,10},{10,2},{3,11},{11,3},{4,12},{12,4},... | collective-permute-start | bytes 884744 | tf_op jit(solution)/shard_map/ppermute | solution.py:87
  132.1 19.1 %collective-permute-done.12 = bf16[768,192]{0,1:T(8,128)(2,1)S(1)} collective-permute-done((bf16[768,192]{0,1:T(8,128)(2,1)S(1)}, bf16[768,192]{0,1:T(8,128)(2,1)S(1)}, u32[]{:S(2)}, u32[]{:S(2)}) %collective-permute-start.12) | collective-permute-done | bytes 294944 | tf_op jit(solution)/shard_map/ppermute | solution.py:87
  (68 shorter events, 24.7 us)
Async XLA Ops:
  1.8 14.9 %collective-permute-start = (bf16[2,768,128]{2,1,0:T(8,128)(2,1)}, bf16[2,768,128]{2,1,0:T(8,128)(2,1)S(1)}, u32[]{:S(2)}, u32[]{:S(2)}) collective-permute-start(bf16[2,768,128]{2,1,0:T(8,128)(2,1)} %pad_maximum_fusion.4), channel_id=1, source_target_pairs={{0,16},{16,32},{32,48},{48,64},{64,80},{80,96},{96,112},{112,128},... | collective-permute-start | bytes 1179656 | tf_op jit(solution)/shard_map/ppermute | solution.py:21
  6.1 21.9 %collective-permute-start.1 = (bf16[2,768,128]{2,1,0:T(8,128)(2,1)}, bf16[2,768,128]{2,1,0:T(8,128)(2,1)}, u32[]{:S(2)}, u32[]{:S(2)}) collective-permute-start(bf16[2,768,128]{2,1,0:T(8,128)(2,1)} %pad_maximum_fusion.4), channel_id=1, source_target_pairs={{16,0},{32,16},{48,32},{64,48},{80,64},{96,80},{112,96},{128,112},... | collective-permute-start | bytes 1179656 | tf_op jit(solution)/shard_map/ppermute | solution.py:23
  11.1 18.0 %copy-start.4 = (bf16[3,128,3072]{1,2,0:T(8,128)(2,1)}, bf16[3,128,3072]{1,2,0:T(8,128)(2,1)S(1)}, u32[]{:S(2)}) copy-start(bf16[3,128,3072]{1,2,0:T(8,128)(2,1)S(1)} %copy.17) | copy-start | bytes 7077892
  11.1 3.1 %copy-start.9 = (s32[96]{0:T(128)S(1)}, s32[96]{0:T(128)}, u32[]{:S(2)}) copy-start(s32[96]{0:T(128)} %param.15) | copy-start | bytes 1156
  11.1 4.4 %copy-start.8 = (s32[96,4]{0,1:T(4,128)S(1)}, s32[96,4]{0,1:T(4,128)}, u32[]{:S(2)}) copy-start(s32[96,4]{0,1:T(4,128)} %param.14) | copy-start | bytes 4612
  11.1 16.8 %copy-start.6 = (bf16[768,128]{1,0:T(8,128)(2,1)S(1)}, bf16[768,128]{1,0:T(8,128)(2,1)}, u32[]{:S(2)}) copy-start(bf16[768,128]{1,0:T(8,128)(2,1)} %param.10) | copy-start | bytes 589828
  11.1 16.8 %copy-start.7 = (bf16[768,128]{1,0:T(8,128)(2,1)S(1)}, bf16[768,128]{1,0:T(8,128)(2,1)}, u32[]{:S(2)}) copy-start(bf16[768,128]{1,0:T(8,128)(2,1)} %param.9) | copy-start | bytes 589828
  12.3 60.4 %collective-permute-start.3 = (bf16[3,128,2,4,192]{1,4,3,2,0:T(8,128)(2,1)}, bf16[3,128,2,4,192]{1,4,3,2,0:T(8,128)(2,1)}, u32[]{:S(2)}, u32[]{:S(2)}) collective-permute-start(bf16[3,128,2,4,192]{1,4,3,2,0:T(8,128)(2,1)} %dynamic-slice_bitcast_fusion.2), channel_id=1, source_target_pairs={{0,1},{1,0},{2,3},{3,2},{4,5},{5,4},{6,7},{7,6},{8,9},{9,8},{10,11... | collective-permute-start | bytes 3538952 | tf_op jit(solution)/shard_map/ppermute | solution.py:235
  16.7 12.4 %copy-start = (bf16[768,128]{1,0:T(8,128)(2,1)S(1)}, bf16[768,128]{1,0:T(8,128)(2,1)}, u32[]{:S(2)}) copy-start(bf16[768,128]{1,0:T(8,128)(2,1)} %q_ref.1) | copy-start | bytes 589828
  16.7 12.4 %copy-start.1 = (bf16[768,128]{1,0:T(8,128)(2,1)S(1)}, bf16[768,128]{1,0:T(8,128)(2,1)}, u32[]{:S(2)}) copy-start(bf16[768,128]{1,0:T(8,128)(2,1)} %do_ref.1) | copy-start | bytes 589828
  16.7 12.4 %copy-start.2 = (bf16[768,128]{1,0:T(8,128)(2,1)S(1)}, bf16[768,128]{1,0:T(8,128)(2,1)}, u32[]{:S(2)}) copy-start(bf16[768,128]{1,0:T(8,128)(2,1)} %o_ref.1) | copy-start | bytes 589828
  36.6 8.2 %copy-start.5 = (bf16[3,128,3072]{1,2,0:T(8,128)(2,1)S(1)}, bf16[3,128,3072]{1,2,0:T(8,128)(2,1)}, u32[]{:S(2)}) copy-start(bf16[3,128,3072]{1,2,0:T(8,128)(2,1)} %copy-done.4) | copy-start | bytes 7077892
  37.7 14.7 %collective-permute-start.4 = (bf16[2,768,1,128]{3,1,2,0:T(8,128)(2,1)}, bf16[2,768,1,128]{3,1,2,0:T(8,128)(2,1)}, u32[]{:S(2)}, u32[]{:S(2)}) collective-permute-start(bf16[2,768,1,128]{3,1,2,0:T(8,128)(2,1)} %get-tuple-element.21), channel_id=1, source_target_pairs={{16,0},{32,16},{48,32},{64,48},{80,64},{96,80},{112,96},{128,112},... | collective-permute-start | bytes 1179656 | tf_op jit(solution)/shard_map/ppermute | solution.py:32
  39.6 25.9 %collective-permute-start.5 = (bf16[2,768,1,128]{3,1,2,0:T(8,128)(2,1)}, bf16[2,768,1,128]{3,1,2,0:T(8,128)(2,1)}, u32[]{:S(2)}, u32[]{:S(2)}) collective-permute-start(bf16[2,768,1,128]{3,1,2,0:T(8,128)(2,1)} %get-tuple-element.22), channel_id=1, source_target_pairs={{752,0},{0,16},{16,32},{32,48},{48,64},{64,80},{80,96},{96,112},{1... | collective-permute-start | bytes 1179656 | tf_op jit(solution)/shard_map/ppermute | solution.py:32
  45.6 32.2 %collective-permute-start.2 = (bf16[768,128]{1,0:T(8,128)(2,1)S(1)}, bf16[768,128]{1,0:T(8,128)(2,1)S(1)}, u32[]{:S(2)}, u32[]{:S(2)}) collective-permute-start(bf16[768,128]{1,0:T(8,128)(2,1)S(1)} %get-tuple-element.8), channel_id=1, source_target_pairs={{0,1},{1,0},{2,3},{3,2},{4,5},{5,4},{6,7},{7,6},{8,9},{9,8},{10,11... | collective-permute-start | bytes 589832 | tf_op jit(solution)/shard_map/ppermute | solution.py:245
  66.8 7.2 %collective-permute-start.6 = (bf16[768,128]{1,0:T(8,128)(2,1)S(1)}, bf16[768,128]{1,0:T(8,128)(2,1)S(1)}, u32[]{:S(2)}, u32[]{:S(2)}) collective-permute-start(bf16[768,128]{1,0:T(8,128)(2,1)S(1)} %get-tuple-element.27), channel_id=1, source_target_pairs={{0,1},{1,0},{2,3},{3,2},{4,5},{5,4},{6,7},{7,6},{8,9},{9,8},{10,11... | collective-permute-start | bytes 589832 | tf_op jit(solution)/shard_map/ppermute | solution.py:245
  68.7 6.1 %collective-permute-start.7 = (bf16[768,128]{1,0:T(8,128)(2,1)S(1)}, bf16[768,128]{1,0:T(8,128)(2,1)S(1)}, u32[]{:S(2)}, u32[]{:S(2)}) collective-permute-start(bf16[768,128]{1,0:T(8,128)(2,1)S(1)} %get-tuple-element.28), channel_id=1, source_target_pairs={{0,1},{1,0},{2,3},{3,2},{4,5},{5,4},{6,7},{7,6},{8,9},{9,8},{10,11... | collective-permute-start | bytes 589832 | tf_op jit(solution)/shard_map/ppermute | solution.py:245
  77.8 3.9 %copy-start.3 = (f32[768,1536]{0,1:S(1)}, f32[768,1536]{0,1}, u32[]{:S(2)}) copy-start(f32[768,1536]{0,1} %fusion.33) | copy-start | bytes 14155780
  88.4 10.8 %collective-permute-start.8 = (bf16[384,2,192]{0,2,1:T(8,128)(2,1)S(1)}, bf16[384,2,192]{0,2,1:T(8,128)(2,1)S(1)}, u32[]{:S(2)}, u32[]{:S(2)}) collective-permute-start(bf16[384,2,192]{0,2,1:T(8,128)(2,1)S(1)} %get-tuple-element.25), channel_id=1, source_target_pairs={{0,2},{2,4},{4,6},{6,0},{1,3},{3,5},{5,7},{7,1},{8,10},{10,12},{12... | collective-permute-start | bytes 884744 | tf_op jit(solution)/shard_map/ppermute | solution.py:63
  90.4 12.5 %collective-permute-start.10 = (bf16[384,2,192]{0,2,1:T(8,128)(2,1)S(1)}, bf16[384,2,192]{0,2,1:T(8,128)(2,1)S(1)}, u32[]{:S(2)}, u32[]{:S(2)}) collective-permute-start(bf16[384,2,192]{0,2,1:T(8,128)(2,1)S(1)} %get-tuple-element.26), channel_id=1, source_target_pairs={{0,6},{2,0},{4,2},{6,4},{1,7},{3,1},{5,3},{7,5},{8,14},{10,8},{12,... | collective-permute-start | bytes 884744 | tf_op jit(solution)/shard_map/ppermute | solution.py:64
  99.4 16.3 %collective-permute-start.9 = (bf16[768,2,192]{0,2,1:T(8,128)(2,1)S(1)}, bf16[768,2,192]{0,2,1:T(8,128)(2,1)S(1)}, u32[]{:S(2)}, u32[]{:S(2)}) collective-permute-start(bf16[768,2,192]{0,2,1:T(8,128)(2,1)S(1)} %pad_maximum_fusion.2), channel_id=1, source_target_pairs={{0,2},{2,4},{4,6},{6,0},{1,3},{3,5},{5,7},{7,1},{8,10},{10,12},{12... | collective-permute-start | bytes 1769480 | tf_op jit(solution)/shard_map/ppermute | solution.py:69
  104.0 17.5 %collective-permute-start.11 = (bf16[768,2,192]{0,2,1:T(8,128)(2,1)S(1)}, bf16[768,2,192]{0,2,1:T(8,128)(2,1)S(1)}, u32[]{:S(2)}, u32[]{:S(2)}) collective-permute-start(bf16[768,2,192]{0,2,1:T(8,128)(2,1)S(1)} %pad_maximum_fusion.3), channel_id=1, source_target_pairs={{0,6},{2,0},{4,2},{6,4},{1,7},{3,1},{5,3},{7,5},{8,14},{10,8},{12,... | collective-permute-start | bytes 1769480 | tf_op jit(solution)/shard_map/ppermute | solution.py:70
  123.0 28.2 %collective-permute-start.12 = (bf16[768,192]{0,1:T(8,128)(2,1)S(1)}, bf16[768,192]{0,1:T(8,128)(2,1)S(1)}, u32[]{:S(2)}, u32[]{:S(2)}) collective-permute-start(bf16[768,192]{0,1:T(8,128)(2,1)S(1)} %fusion.10), channel_id=1, source_target_pairs={{0,8},{8,0},{1,9},{9,1},{2,10},{10,2},{3,11},{11,3},{4,12},{12,4},... | collective-permute-start | bytes 884744 | tf_op jit(solution)/shard_map/ppermute | solution.py:87

commit v6 on v3

--- a/solution.py
+++ b/solution.py
@@ -76,12 +76,10 @@
     zh = lax.axis_index("zh")
     n_c, n_x, n_zh = parts.shape[3], parts.shape[2], parts.shape[1]
     if n_c > 1:
-        got = lax.ppermute(
-            pick(parts, 3, 1 - c).astype(jnp.bfloat16), "c", [(0, 1), (1, 0)]
-        )
-        sums = pick(parts, 3, c) + got.astype(jnp.float32)
+        got = lax.ppermute(pick(parts, 3, 1 - c), "c", [(0, 1), (1, 0)])
+        sums = pick(parts, 3, c).astype(jnp.float32) + got.astype(jnp.float32)
     else:
-        sums = parts[:, :, :, 0]
+        sums = parts[:, :, :, 0].astype(jnp.float32)
     if n_x == 4:
         sums = four_scatter(jnp.swapaxes(sums, 1, 2))
     elif n_x > 1:
@@ -233,7 +231,7 @@
     weight = projection.reshape(3, heads_dev * HD, n_zh, n_x, n_c, width)
     parts = jnp.einsum(
         "cik,ckzxym->izxym", grad_stack, weight, preferred_element_type=jnp.float32
-    )
+    ).astype(jnp.bfloat16)
     return reduce_scatter(parts).astype(jnp.bfloat16)
 
 

time: 146 us -> 144 us (0.986)
  local copies, waits for them, and re-layouts: 12.1 us -> 10.3 us
    unnamed x18, local copies, waits for them, and re-layouts: 9.18 us -> 7.48 us
where the time goes in v6:
time: 144 us; the launch traced here: 143 us
  waiting for transfers between devices  75.8 us (53%)
  starting transfers between devices  35.9 us (25%)
  local copies, waits for them, and re-layouts  10.3 us (7%)
  other arithmetic  10.2 us (7%)
  Pallas kernels  7.49 us (5%)
  matrix products  2.87 us (2%)
    ppermute x1, waiting for transfers between devices, reduce_scatter(): got = lax.ppermute(acc.astype(jnp.bfloat16), 'zh', route)  19.2 us
    ppermute x2, waiting for transfers between devices, passed_along(): return lax.ppermute(block, axis, route)  16.4 us
    ppermute x1, waiting for transfers between devices, with_halo(): lax.ppermute(head, axis, [((i + 1) % count, i) for i in range(count)])  13.1 us
    ppermute x1, waiting for transfers between devices, four_scatter(): got_left = lax.ppermute(to_right.astype(jnp.bfloat16), 'x', cw)  10.4 us
    ppermute x1, starting transfers between devices, reduce_scatter(): got = lax.ppermute(acc.astype(jnp.bfloat16), 'zh', route)  9.08 us
    pallas_call x1, Pallas kernels, attention(): pl.pallas_call(attention_kernel, grid=(tiles,), in_specs=[row_spec, row_s...  7.49 us
    unnamed x18, local copies, waits for them, and re-layouts  7.48 us
    ppermute x2, starting transfers between devices, passed_along(): return lax.ppermute(block, axis, route)  7 us
  transfers between devices with their start and end apart: 10, of which 9 were waited for; matrix products, arithmetic and copies ran while one was open for 6% of the time, Pallas kernels for 0%

profile of v6, /device:TPU:70, one launch (start us, length us, event | category | flops | bytes accessed | tf_op | source)
XLA Modules:
  0.0 143.1 jit_solution(17628878642098225461)
XLA Ops:
  1.1 4.3 %collective-permute-start = (bf16[2,768,128]{2,1,0:T(8,128)(2,1)S(1)}, bf16[2,768,128]{2,1,0:T(8,128)(2,1)S(1)}, u32[]{:S(2)}, u32[]{:S(2)}) collective-permute-start(bf16[2,768,128]{2,1,0:T(8,128)(2,1)S(1)} %pad_maximum_fusion.4), channel_id=1, source_target_pairs={{0,16},{16,32},{32,48},{48,64},{64,80},{80,96},{96,112},{112,128},... | collective-permute-start | bytes 1179656 | tf_op jit(solution)/shard_map/ppermute | solution.py:21
  5.3 1.9 %collective-permute-start.1 = (bf16[2,768,128]{2,1,0:T(8,128)(2,1)S(1)}, bf16[2,768,128]{2,1,0:T(8,128)(2,1)S(1)}, u32[]{:S(2)}, u32[]{:S(2)}) collective-permute-start(bf16[2,768,128]{2,1,0:T(8,128)(2,1)S(1)} %pad_maximum_fusion.4), channel_id=1, source_target_pairs={{16,0},{32,16},{48,32},{64,48},{80,64},{96,80},{112,96},{128,112},... | collective-permute-start | bytes 1179656 | tf_op jit(solution)/shard_map/ppermute | solution.py:23
  11.3 2.5 %collective-permute-done = bf16[2,768,128]{2,1,0:T(8,128)(2,1)S(1)} collective-permute-done((bf16[2,768,128]{2,1,0:T(8,128)(2,1)S(1)}, bf16[2,768,128]{2,1,0:T(8,128)(2,1)S(1)}, u32[]{:S(2)}, u32[]{:S(2)}) %collective-permute-start) | collective-permute-done | bytes 393248 | tf_op jit(solution)/shard_map/ppermute | solution.py:21
  13.8 13.1 %collective-permute-done.1 = bf16[2,768,128]{2,1,0:T(8,128)(2,1)S(1)} collective-permute-done((bf16[2,768,128]{2,1,0:T(8,128)(2,1)S(1)}, bf16[2,768,128]{2,1,0:T(8,128)(2,1)S(1)}, u32[]{:S(2)}, u32[]{:S(2)}) %collective-permute-start.1) | collective-permute-done | bytes 393248 | tf_op jit(solution)/shard_map/ppermute | solution.py:23
  29.1 7.5 %shard_map.82 = (bf16[768,128]{1,0:T(8,128)(2,1)S(1)}, f32[2304,128]{1,0:T(8,128)S(1)}, f32[2304,128]{1,0:T(8,128)S(1)}) custom-call(bf16[768,128]{1,0:T(8,128)(2,1)S(1)} %copy-done, bf16[768,128]{1,0:T(8,128)(2,1)S(1)} %copy-done.1, bf16[768,128]{1,0:T(8,128)(2,1)S(1)} %copy-done.2, bf16[2304,128]{1,0:T(8,128)(2,1)S(1)} %get-tuple-element.18.k_ref, ...), custom_call_target="tpu_custom_call" | custom-call | flops 2264924160 | bytes 4128768 | tf_op jit(solution)/shard_map/pallas_call | solution.py:146
  37.7 1.9 %collective-permute-start.2 = (bf16[2,768,1,128]{3,1,2,0:T(8,128)(2,1)}, bf16[2,768,1,128]{3,1,2,0:T(8,128)(2,1)S(1)}, u32[]{:S(2)}, u32[]{:S(2)}) collective-permute-start(bf16[2,768,1,128]{3,1,2,0:T(8,128)(2,1)} %get-tuple-element.15), channel_id=1, source_target_pairs={{16,0},{32,16},{48,32},{64,48},{80,64},{96,80},{112,96},{128,112},... | collective-permute-start | bytes 1179656 | tf_op jit(solution)/shard_map/ppermute | solution.py:32
  39.6 5.1 %collective-permute-start.3 = (bf16[2,768,1,128]{3,1,2,0:T(8,128)(2,1)}, bf16[2,768,1,128]{3,1,2,0:T(8,128)(2,1)S(1)}, u32[]{:S(2)}, u32[]{:S(2)}) collective-permute-start(bf16[2,768,1,128]{3,1,2,0:T(8,128)(2,1)} %get-tuple-element.16), channel_id=1, source_target_pairs={{752,0},{0,16},{16,32},{32,48},{48,64},{64,80},{80,96},{96,112},{1... | collective-permute-start | bytes 1179656 | tf_op jit(solution)/shard_map/ppermute | solution.py:32
  44.7 4.3 %copy.18 = bf16[3,128,3072]{1,2,0:T(8,128)(2,1)} copy(bf16[3,128,3072]{2,1,0:T(8,128)(2,1)} %param.13) | data formatting | bytes 4718592 | tf_op args[5]
  49.0 3.3 %collective-permute-done.2 = bf16[2,768,1,128]{3,1,2,0:T(8,128)(2,1)S(1)} collective-permute-done((bf16[2,768,1,128]{3,1,2,0:T(8,128)(2,1)}, bf16[2,768,1,128]{3,1,2,0:T(8,128)(2,1)S(1)}, u32[]{:S(2)}, u32[]{:S(2)}) %collective-permute-start.2) | collective-permute-done | bytes 393248 | tf_op jit(solution)/shard_map/ppermute | solution.py:32
  52.3 13.1 %collective-permute-done.3 = bf16[2,768,1,128]{3,1,2,0:T(8,128)(2,1)S(1)} collective-permute-done((bf16[2,768,1,128]{3,1,2,0:T(8,128)(2,1)}, bf16[2,768,1,128]{3,1,2,0:T(8,128)(2,1)S(1)}, u32[]{:S(2)}, u32[]{:S(2)}) %collective-permute-start.3) | collective-permute-done | bytes 393248 | tf_op jit(solution)/shard_map/ppermute | solution.py:32
  65.6 2.9 %bitcast_convert_fusion = bf16[768,2,4,2,192]{0,4,3,2,1:T(8,128)(2,1)S(1)} fusion(bf16[3,128,2,4,2,192]{1,5,4,3,2,0:T(8,128)(2,1)S(1)} %bitcast.83, bf16[1,768,128]{2,1,0:T(8,128)(2,1)S(1)} %get-tuple-element.22, bf16[1,768,128]{2,1,0:T(8,128)(2,1)S(1)} %get-tuple-element.21, bf16[1,768,128]{2,1,0:T(8,128)(2,1)S(1)} %bitcast.82), kind=kOutput, calls=%fused_computation | convolution fusion | flops 1816068096 | bytes 7667712 | tf_op jit(solution)/shard_map/cik,ckzxym->izxym/dot_general | solution.py:232
  68.7 1.9 %copy-done.4 = bf16[768,2,4,2,192]{0,4,3,2,1:T(8,128)(2,1)} copy-done((bf16[768,2,4,2,192]{0,4,3,2,1:T(8,128)(2,1)}, bf16[768,2,4,2,192]{0,4,3,2,1:T(8,128)(2,1)S(1)}, u32[]{:S(2)}) %copy-start.4) | copy-done | bytes 4718616
  70.6 1.9 %collective-permute-start.4 = (bf16[768,2,4,192]{0,3,2,1:T(8,128)(2,1)S(1)}, bf16[768,2,4,192]{0,3,2,1:T(8,128)(2,1)}, u32[]{:S(2)}, u32[]{:S(2)}) collective-permute-start(bf16[768,2,4,192]{0,3,2,1:T(8,128)(2,1)S(1)} %dynamic-slice_bitcast_fusion), channel_id=1, source_target_pairs={{0,1},{1,0},{2,3},{3,2},{4,5},{5,4},{6,7},{7,6},{8,9},{9,8},{10,11... | collective-permute-start | bytes 7077896 | tf_op jit(solution)/shard_map/ppermute | solution.py:79
  72.6 4.6 %collective-permute-done.4 = bf16[768,2,4,192]{0,3,2,1:T(8,128)(2,1)} collective-permute-done((bf16[768,2,4,192]{0,3,2,1:T(8,128)(2,1)S(1)}, bf16[768,2,4,192]{0,3,2,1:T(8,128)(2,1)}, u32[]{:S(2)}, u32[]{:S(2)}) %collective-permute-start.4) | collective-permute-done | bytes 2359328 | tf_op jit(solution)/shard_map/ppermute | solution.py:79
  77.2 2.9 %convert_add_fusion = f32[768,2,4,192]{0,3,2,1:T(8,128)S(1)} fusion(bf16[768,2,4,192]{0,3,2,1:T(8,128)(2,1)} %collective-permute-done.4, bf16[768,2,4,2,192]{0,4,3,2,1:T(8,128)(2,1)} %copy-done.4, s32[]{:T(128)S(6)} %select_n.80), kind=kLoop, calls=%fused_computation.1 | loop fusion | flops 3538944 | bytes 9437188 | tf_op jit(solution)/shard_map/add | solution.py:80
  80.3 1.9 %collective-permute-start.5 = (bf16[384,2,192]{0,2,1:T(8,128)(2,1)S(1)}, bf16[384,2,192]{0,2,1:T(8,128)(2,1)S(1)}, u32[]{:S(2)}, u32[]{:S(2)}) collective-permute-start(bf16[384,2,192]{0,2,1:T(8,128)(2,1)S(1)} %get-tuple-element.19), channel_id=1, source_target_pairs={{0,2},{2,4},{4,6},{6,0},{1,3},{3,5},{5,7},{7,1},{8,10},{10,12},{12... | collective-permute-start | bytes 884744 | tf_op jit(solution)/shard_map/ppermute | solution.py:63
  82.2 3.9 %collective-permute-start.7 = (bf16[384,2,192]{0,2,1:T(8,128)(2,1)S(1)}, bf16[384,2,192]{0,2,1:T(8,128)(2,1)S(1)}, u32[]{:S(2)}, u32[]{:S(2)}) collective-permute-start(bf16[384,2,192]{0,2,1:T(8,128)(2,1)S(1)} %get-tuple-element.20), channel_id=1, source_target_pairs={{0,6},{2,0},{4,2},{6,4},{1,7},{3,1},{5,3},{7,5},{8,14},{10,8},{12,... | collective-permute-start | bytes 884744 | tf_op jit(solution)/shard_map/ppermute | solution.py:64
  86.3 4.9 %collective-permute-done.5 = bf16[384,2,192]{0,2,1:T(8,128)(2,1)S(1)} collective-permute-done((bf16[384,2,192]{0,2,1:T(8,128)(2,1)S(1)}, bf16[384,2,192]{0,2,1:T(8,128)(2,1)S(1)}, u32[]{:S(2)}, u32[]{:S(2)}) %collective-permute-start.5) | collective-permute-done | bytes 294944 | tf_op jit(solution)/shard_map/ppermute | solution.py:63
  91.3 3.4 %collective-permute-start.6 = (bf16[768,2,192]{0,2,1:T(8,128)(2,1)S(1)}, bf16[768,2,192]{0,2,1:T(8,128)(2,1)S(1)}, u32[]{:S(2)}, u32[]{:S(2)}) collective-permute-start(bf16[768,2,192]{0,2,1:T(8,128)(2,1)S(1)} %pad_maximum_fusion.2), channel_id=1, source_target_pairs={{0,2},{2,4},{4,6},{6,0},{1,3},{3,5},{5,7},{7,1},{8,10},{10,12},{12... | collective-permute-start | bytes 1769480 | tf_op jit(solution)/shard_map/ppermute | solution.py:69
  94.9 2.4 %collective-permute-start.8 = (bf16[768,2,192]{0,2,1:T(8,128)(2,1)S(1)}, bf16[768,2,192]{0,2,1:T(8,128)(2,1)S(1)}, u32[]{:S(2)}, u32[]{:S(2)}) collective-permute-start(bf16[768,2,192]{0,2,1:T(8,128)(2,1)S(1)} %pad_maximum_fusion.3), channel_id=1, source_target_pairs={{0,6},{2,0},{4,2},{6,4},{1,7},{3,1},{5,3},{7,5},{8,14},{10,8},{12,... | collective-permute-start | bytes 1769480 | tf_op jit(solution)/shard_map/ppermute | solution.py:70
  97.4 10.4 %collective-permute-done.6 = bf16[768,2,192]{0,2,1:T(8,128)(2,1)S(1)} collective-permute-done((bf16[768,2,192]{0,2,1:T(8,128)(2,1)S(1)}, bf16[768,2,192]{0,2,1:T(8,128)(2,1)S(1)}, u32[]{:S(2)}, u32[]{:S(2)}) %collective-permute-start.6) | collective-permute-done | bytes 589856 | tf_op jit(solution)/shard_map/ppermute | solution.py:69
  107.8 4.8 %collective-permute-done.8 = bf16[768,2,192]{0,2,1:T(8,128)(2,1)S(1)} collective-permute-done((bf16[768,2,192]{0,2,1:T(8,128)(2,1)S(1)}, bf16[768,2,192]{0,2,1:T(8,128)(2,1)S(1)}, u32[]{:S(2)}, u32[]{:S(2)}) %collective-permute-start.8) | collective-permute-done | bytes 589856 | tf_op jit(solution)/shard_map/ppermute | solution.py:70
  114.0 9.1 %collective-permute-start.9 = (bf16[768,192]{0,1:T(8,128)(2,1)S(1)}, bf16[768,192]{0,1:T(8,128)(2,1)S(1)}, u32[]{:S(2)}, u32[]{:S(2)}) collective-permute-start(bf16[768,192]{0,1:T(8,128)(2,1)S(1)} %fusion.17), channel_id=1, source_target_pairs={{0,8},{8,0},{1,9},{9,1},{2,10},{10,2},{3,11},{11,3},{4,12},{12,4},... | collective-permute-start | bytes 884744 | tf_op jit(solution)/shard_map/ppermute | solution.py:93
  123.1 19.2 %collective-permute-done.9 = bf16[768,192]{0,1:T(8,128)(2,1)S(1)} collective-permute-done((bf16[768,192]{0,1:T(8,128)(2,1)S(1)}, bf16[768,192]{0,1:T(8,128)(2,1)S(1)}, u32[]{:S(2)}, u32[]{:S(2)}) %collective-permute-start.9) | collective-permute-done | bytes 294944 | tf_op jit(solution)/shard_map/ppermute | solution.py:93
  (47 shorter events, 11.5 us)
Async XLA Ops:
  1.1 12.7 %collective-permute-start = (bf16[2,768,128]{2,1,0:T(8,128)(2,1)S(1)}, bf16[2,768,128]{2,1,0:T(8,128)(2,1)S(1)}, u32[]{:S(2)}, u32[]{:S(2)}) collective-permute-start(bf16[2,768,128]{2,1,0:T(8,128)(2,1)S(1)} %pad_maximum_fusion.4), channel_id=1, source_target_pairs={{0,16},{16,32},{32,48},{48,64},{64,80},{80,96},{96,112},{112,128},... | collective-permute-start | bytes 1179656 | tf_op jit(solution)/shard_map/ppermute | solution.py:21
  5.3 21.5 %collective-permute-start.1 = (bf16[2,768,128]{2,1,0:T(8,128)(2,1)S(1)}, bf16[2,768,128]{2,1,0:T(8,128)(2,1)S(1)}, u32[]{:S(2)}, u32[]{:S(2)}) collective-permute-start(bf16[2,768,128]{2,1,0:T(8,128)(2,1)S(1)} %pad_maximum_fusion.4), channel_id=1, source_target_pairs={{16,0},{32,16},{48,32},{64,48},{80,64},{96,80},{112,96},{128,112},... | collective-permute-start | bytes 1179656 | tf_op jit(solution)/shard_map/ppermute | solution.py:23
  28.0 0.9 copy-start
  28.0 1.0 copy-start.1
  28.0 1.1 copy-start.2
  37.7 14.6 %collective-permute-start.2 = (bf16[2,768,1,128]{3,1,2,0:T(8,128)(2,1)}, bf16[2,768,1,128]{3,1,2,0:T(8,128)(2,1)S(1)}, u32[]{:S(2)}, u32[]{:S(2)}) collective-permute-start(bf16[2,768,1,128]{3,1,2,0:T(8,128)(2,1)} %get-tuple-element.15), channel_id=1, source_target_pairs={{16,0},{32,16},{48,32},{64,48},{80,64},{96,80},{112,96},{128,112},... | collective-permute-start | bytes 1179656 | tf_op jit(solution)/shard_map/ppermute | solution.py:32
  39.6 25.8 %collective-permute-start.3 = (bf16[2,768,1,128]{3,1,2,0:T(8,128)(2,1)}, bf16[2,768,1,128]{3,1,2,0:T(8,128)(2,1)S(1)}, u32[]{:S(2)}, u32[]{:S(2)}) collective-permute-start(bf16[2,768,1,128]{3,1,2,0:T(8,128)(2,1)} %get-tuple-element.16), channel_id=1, source_target_pairs={{752,0},{0,16},{16,32},{32,48},{48,64},{64,80},{80,96},{96,112},{1... | collective-permute-start | bytes 1179656 | tf_op jit(solution)/shard_map/ppermute | solution.py:32
  49.0 16.6 %copy-start.5 = (bf16[3,128,3072]{1,2,0:T(8,128)(2,1)S(1)}, bf16[3,128,3072]{1,2,0:T(8,128)(2,1)}, u32[]{:S(2)}) copy-start(bf16[3,128,3072]{1,2,0:T(8,128)(2,1)} %copy.18) | copy-start | bytes 7077892
  68.5 2.1 %copy-start.4 = (bf16[768,2,4,2,192]{0,4,3,2,1:T(8,128)(2,1)}, bf16[768,2,4,2,192]{0,4,3,2,1:T(8,128)(2,1)S(1)}, u32[]{:S(2)}) copy-start(bf16[768,2,4,2,192]{0,4,3,2,1:T(8,128)(2,1)S(1)} %bitcast_convert_fusion) | copy-start | bytes 14155780
  70.6 6.5 %collective-permute-start.4 = (bf16[768,2,4,192]{0,3,2,1:T(8,128)(2,1)S(1)}, bf16[768,2,4,192]{0,3,2,1:T(8,128)(2,1)}, u32[]{:S(2)}, u32[]{:S(2)}) collective-permute-start(bf16[768,2,4,192]{0,3,2,1:T(8,128)(2,1)S(1)} %dynamic-slice_bitcast_fusion), channel_id=1, source_target_pairs={{0,1},{1,0},{2,3},{3,2},{4,5},{5,4},{6,7},{7,6},{8,9},{9,8},{10,11... | collective-permute-start | bytes 7077896 | tf_op jit(solution)/shard_map/ppermute | solution.py:79
  80.1 14.7 %copy-start.3 = (f32[768,2,4,192]{0,3,2,1:T(8,128)}, f32[768,2,4,192]{0,3,2,1:T(8,128)S(1)}, u32[]{:S(2)}) copy-start(f32[768,2,4,192]{0,3,2,1:T(8,128)S(1)} %convert_add_fusion) | copy-start | bytes 14155780
  80.3 10.9 %collective-permute-start.5 = (bf16[384,2,192]{0,2,1:T(8,128)(2,1)S(1)}, bf16[384,2,192]{0,2,1:T(8,128)(2,1)S(1)}, u32[]{:S(2)}, u32[]{:S(2)}) collective-permute-start(bf16[384,2,192]{0,2,1:T(8,128)(2,1)S(1)} %get-tuple-element.19), channel_id=1, source_target_pairs={{0,2},{2,4},{4,6},{6,0},{1,3},{3,5},{5,7},{7,1},{8,10},{10,12},{12... | collective-permute-start | bytes 884744 | tf_op jit(solution)/shard_map/ppermute | solution.py:63
  82.2 12.6 %collective-permute-start.7 = (bf16[384,2,192]{0,2,1:T(8,128)(2,1)S(1)}, bf16[384,2,192]{0,2,1:T(8,128)(2,1)S(1)}, u32[]{:S(2)}, u32[]{:S(2)}) collective-permute-start(bf16[384,2,192]{0,2,1:T(8,128)(2,1)S(1)} %get-tuple-element.20), channel_id=1, source_target_pairs={{0,6},{2,0},{4,2},{6,4},{1,7},{3,1},{5,3},{7,5},{8,14},{10,8},{12,... | collective-permute-start | bytes 884744 | tf_op jit(solution)/shard_map/ppermute | solution.py:64
  91.3 16.4 %collective-permute-start.6 = (bf16[768,2,192]{0,2,1:T(8,128)(2,1)S(1)}, bf16[768,2,192]{0,2,1:T(8,128)(2,1)S(1)}, u32[]{:S(2)}, u32[]{:S(2)}) collective-permute-start(bf16[768,2,192]{0,2,1:T(8,128)(2,1)S(1)} %pad_maximum_fusion.2), channel_id=1, source_target_pairs={{0,2},{2,4},{4,6},{6,0},{1,3},{3,5},{5,7},{7,1},{8,10},{10,12},{12... | collective-permute-start | bytes 1769480 | tf_op jit(solution)/shard_map/ppermute | solution.py:69
  94.9 17.6 %collective-permute-start.8 = (bf16[768,2,192]{0,2,1:T(8,128)(2,1)S(1)}, bf16[768,2,192]{0,2,1:T(8,128)(2,1)S(1)}, u32[]{:S(2)}, u32[]{:S(2)}) collective-permute-start(bf16[768,2,192]{0,2,1:T(8,128)(2,1)S(1)} %pad_maximum_fusion.3), channel_id=1, source_target_pairs={{0,6},{2,0},{4,2},{6,4},{1,7},{3,1},{5,3},{7,5},{8,14},{10,8},{12,... | collective-permute-start | bytes 1769480 | tf_op jit(solution)/shard_map/ppermute | solution.py:70
  114.0 28.3 %collective-permute-start.9 = (bf16[768,192]{0,1:T(8,128)(2,1)S(1)}, bf16[768,192]{0,1:T(8,128)(2,1)S(1)}, u32[]{:S(2)}, u32[]{:S(2)}) collective-permute-start(bf16[768,192]{0,1:T(8,128)(2,1)S(1)} %fusion.17), channel_id=1, source_target_pairs={{0,8},{8,0},{1,9},{9,1},{2,10},{10,2},{3,11},{11,3},{4,12},{12,4},... | collective-permute-start | bytes 884744 | tf_op jit(solution)/shard_map/ppermute | solution.py:93

commit v7 on v6

--- a/solution.py
+++ b/solution.py
@@ -71,15 +71,9 @@
     return pick(block, 1, x) + got_left.astype(jnp.float32) + got_right.astype(jnp.float32)
 
 
-def reduce_scatter(parts):
-    c = lax.axis_index("c")
+def reduce_scatter(sums):
     zh = lax.axis_index("zh")
-    n_c, n_x, n_zh = parts.shape[3], parts.shape[2], parts.shape[1]
-    if n_c > 1:
-        got = lax.ppermute(pick(parts, 3, 1 - c), "c", [(0, 1), (1, 0)])
-        sums = pick(parts, 3, c).astype(jnp.float32) + got.astype(jnp.float32)
-    else:
-        sums = parts[:, :, :, 0].astype(jnp.float32)
+    n_x, n_zh = sums.shape[2], sums.shape[1]
     if n_x == 4:
         sums = four_scatter(jnp.swapaxes(sums, 1, 2))
     elif n_x > 1:
@@ -229,10 +223,19 @@
     n_zh, n_x, n_c = (lax.axis_size(a) for a in HEAD_AXES)
     width = projection.shape[2] // (n_zh * n_x * n_c)
     weight = projection.reshape(3, heads_dev * HD, n_zh, n_x, n_c, width)
-    parts = jnp.einsum(
-        "cik,ckzxym->izxym", grad_stack, weight, preferred_element_type=jnp.float32
-    ).astype(jnp.bfloat16)
-    return reduce_scatter(parts).astype(jnp.bfloat16)
+    c = lax.axis_index("c")
+
+    def term(columns):
+        return jnp.einsum("cik,ckzxm->izxm", grad_stack, columns, preferred_element_type=jnp.float32)
+
+    if n_c > 1:
+        other = term(pick(weight, 4, 1 - c)).astype(jnp.bfloat16)
+        got = lax.ppermute(other, "c", [(0, 1), (1, 0)])
+        mine = term(pick(weight, 4, c)).astype(jnp.bfloat16)
+        sums = mine.astype(jnp.float32) + got.astype(jnp.float32)
+    else:
+        sums = term(weight[:, :, :, :, 0]).astype(jnp.bfloat16).astype(jnp.float32)
+    return reduce_scatter(sums).astype(jnp.bfloat16)
 
 
 def head_shape(n_head):

time: 144 us -> 142 us (0.986)
  matrix products: 2.87 us -> 5.92 us
  other arithmetic: 10.2 us -> 7.34 us
  waiting for transfers between devices: 75.8 us -> 73.2 us
    dot_general x1 -> x2, matrix products: 2.87 us -> 5.92 us  [term(): jnp.einsum('cik,ckzxm->izxm', grad_stack, columns, preferred_element_type...]
    add x1 -> x0, other arithmetic: 2.9 us -> none  [reduce_scatter(): sums = pick(parts, 3, c).astype(jnp.float32) + got.astype(jnp.float32)]
    ppermute x2, waiting for transfers between devices: 16.4 us -> 13.6 us  [passed_along(): return lax.ppermute(block, axis, route)]
    dynamic_slice x0 -> x1, local copies, waits for them, and re-layouts: none -> 2.83 us  [pick(): return lax.dynamic_index_in_dim(array, index, axis, keepdims=False)]
    unnamed x18 -> x16, local copies, waits for them, and re-layouts: 7.48 us -> 5.54 us
  transfers between devices with their start and end apart: 10 -> 10, of which waited for: 9 -> 9; matrix products, arithmetic and copies ran while one was open for 6% -> 8% of each run, Pallas kernels for 0% -> 0%
where the time goes in v7:
time: 142 us; the launch traced here: 141 us
  waiting for transfers between devices  73.2 us (52%)
  starting transfers between devices  35.9 us (25%)
  local copies, waits for them, and re-layouts  11.1 us (8%)
  Pallas kernels  7.49 us (5%)
  other arithmetic  7.34 us (5%)
  matrix products  5.92 us (4%)
    ppermute x1, waiting for transfers between devices, reduce_scatter(): got = lax.ppermute(acc.astype(jnp.bfloat16), 'zh', route)  19.2 us
    ppermute x2, waiting for transfers between devices, passed_along(): return lax.ppermute(block, axis, route)  13.6 us
    ppermute x1, waiting for transfers between devices, with_halo(): lax.ppermute(head, axis, [((i + 1) % count, i) for i in range(count)])  13.1 us
    ppermute x1, waiting for transfers between devices, four_scatter(): got_left = lax.ppermute(to_right.astype(jnp.bfloat16), 'x', cw)  10.4 us
    ppermute x1, starting transfers between devices, reduce_scatter(): got = lax.ppermute(acc.astype(jnp.bfloat16), 'zh', route)  9.07 us
    pallas_call x1, Pallas kernels, attention(): pl.pallas_call(attention_kernel, grid=(tiles,), in_specs=[row_spec, row_s...  7.49 us
    ppermute x2, starting transfers between devices, passed_along(): return lax.ppermute(block, axis, route)  7 us
    dot_general x2, matrix products, term(): jnp.einsum('cik,ckzxm->izxm', grad_stack, columns, preferred_element_type...  5.92 us
  transfers between devices with their start and end apart: 10, of which 9 were waited for; matrix products, arithmetic and copies ran while one was open for 8% of the time, Pallas kernels for 0%

profile of v7, /device:TPU:70, one launch (start us, length us, event | category | flops | bytes accessed | tf_op | source)
XLA Modules:
  0.0 141.3 jit_solution(9056819405495149859)
XLA Ops:
  1.1 4.3 %collective-permute-start = (bf16[2,768,128]{2,1,0:T(8,128)(2,1)S(1)}, bf16[2,768,128]{2,1,0:T(8,128)(2,1)S(1)}, u32[]{:S(2)}, u32[]{:S(2)}) collective-permute-start(bf16[2,768,128]{2,1,0:T(8,128)(2,1)S(1)} %pad_maximum_fusion.4), channel_id=1, source_target_pairs={{0,16},{16,32},{32,48},{48,64},{64,80},{80,96},{96,112},{112,128},... | collective-permute-start | bytes 1179656 | tf_op jit(solution)/shard_map/ppermute | solution.py:21
  5.3 1.9 %collective-permute-start.1 = (bf16[2,768,128]{2,1,0:T(8,128)(2,1)S(1)}, bf16[2,768,128]{2,1,0:T(8,128)(2,1)S(1)}, u32[]{:S(2)}, u32[]{:S(2)}) collective-permute-start(bf16[2,768,128]{2,1,0:T(8,128)(2,1)S(1)} %pad_maximum_fusion.4), channel_id=1, source_target_pairs={{16,0},{32,16},{48,32},{64,48},{80,64},{96,80},{112,96},{128,112},... | collective-permute-start | bytes 1179656 | tf_op jit(solution)/shard_map/ppermute | solution.py:23
  11.3 2.5 %collective-permute-done = bf16[2,768,128]{2,1,0:T(8,128)(2,1)S(1)} collective-permute-done((bf16[2,768,128]{2,1,0:T(8,128)(2,1)S(1)}, bf16[2,768,128]{2,1,0:T(8,128)(2,1)S(1)}, u32[]{:S(2)}, u32[]{:S(2)}) %collective-permute-start) | collective-permute-done | bytes 393248 | tf_op jit(solution)/shard_map/ppermute | solution.py:21
  13.8 13.1 %collective-permute-done.1 = bf16[2,768,128]{2,1,0:T(8,128)(2,1)S(1)} collective-permute-done((bf16[2,768,128]{2,1,0:T(8,128)(2,1)S(1)}, bf16[2,768,128]{2,1,0:T(8,128)(2,1)S(1)}, u32[]{:S(2)}, u32[]{:S(2)}) %collective-permute-start.1) | collective-permute-done | bytes 393248 | tf_op jit(solution)/shard_map/ppermute | solution.py:23
  29.1 7.5 %shard_map.82 = (bf16[768,128]{1,0:T(8,128)(2,1)S(1)}, f32[2304,128]{1,0:T(8,128)S(1)}, f32[2304,128]{1,0:T(8,128)S(1)}) custom-call(bf16[768,128]{1,0:T(8,128)(2,1)S(1)} %copy-done, bf16[768,128]{1,0:T(8,128)(2,1)S(1)} %copy-done.1, bf16[768,128]{1,0:T(8,128)(2,1)S(1)} %copy-done.2, bf16[2304,128]{1,0:T(8,128)(2,1)S(1)} %get-tuple-element.20.k_ref, ...), custom_call_target="tpu_custom_call" | custom-call | flops 2264924160 | bytes 4128768 | tf_op jit(solution)/shard_map/pallas_call | solution.py:140
  37.7 1.9 %collective-permute-start.2 = (bf16[2,768,1,128]{3,1,2,0:T(8,128)(2,1)}, bf16[2,768,1,128]{3,1,2,0:T(8,128)(2,1)S(1)}, u32[]{:S(2)}, u32[]{:S(2)}) collective-permute-start(bf16[2,768,1,128]{3,1,2,0:T(8,128)(2,1)} %get-tuple-element.17), channel_id=1, source_target_pairs={{16,0},{32,16},{48,32},{64,48},{80,64},{96,80},{112,96},{128,112},... | collective-permute-start | bytes 1179656 | tf_op jit(solution)/shard_map/ppermute | solution.py:32
  39.6 5.1 %collective-permute-start.3 = (bf16[2,768,1,128]{3,1,2,0:T(8,128)(2,1)}, bf16[2,768,1,128]{3,1,2,0:T(8,128)(2,1)S(1)}, u32[]{:S(2)}, u32[]{:S(2)}) collective-permute-start(bf16[2,768,1,128]{3,1,2,0:T(8,128)(2,1)} %get-tuple-element.18), channel_id=1, source_target_pairs={{752,0},{0,16},{16,32},{32,48},{48,64},{64,80},{80,96},{96,112},{1... | collective-permute-start | bytes 1179656 | tf_op jit(solution)/shard_map/ppermute | solution.py:32
  44.8 4.3 %copy.20 = bf16[3,128,3072]{1,2,0:T(8,128)(2,1)} copy(bf16[3,128,3072]{2,1,0:T(8,128)(2,1)} %param.13) | data formatting | bytes 4718592 | tf_op args[5]
  49.0 2.8 %constant_dynamic-slice_fusion.1 = (bf16[3,128,2,4,1,192]{1,5,4,3,2,0:T(8,128)(2,1)}, bf16[3,128,2,4,1,192]{1,5,4,3,2,0:T(8,128)(2,1)S(1)}) fusion(bf16[3,128,2,4,2,192]{1,5,4,3,2,0:T(8,128)(2,1)} %bitcast.86, s32[]{:T(128)S(6)} %select_n.80, s32[]{:T(128)S(6)} %select_n.81), kind=kLoop, calls=%fused_computation.49 | loop fusion | bytes 4718600 | tf_op jit(solution)/shard_map/jit(dynamic_index_in_dim)/dynamic_slice | solution.py:36
  52.3 13.1 %collective-permute-done.3 = bf16[2,768,1,128]{3,1,2,0:T(8,128)(2,1)S(1)} collective-permute-done((bf16[2,768,1,128]{3,1,2,0:T(8,128)(2,1)}, bf16[2,768,1,128]{3,1,2,0:T(8,128)(2,1)S(1)}, u32[]{:S(2)}, u32[]{:S(2)}) %collective-permute-start.3) | collective-permute-done | bytes 393248 | tf_op jit(solution)/shard_map/ppermute | solution.py:32
  65.6 2.8 %bitcast_convert_fusion = bf16[768,2,4,192]{0,3,2,1:T(8,128)(2,1)} fusion(bf16[3,128,2,4,1,192]{1,5,4,3,2,0:T(8,128)(2,1)S(1)} %get-tuple-element.16, bf16[1,768,128]{2,1,0:T(8,128)(2,1)S(1)} %get-tuple-element.24, bf16[1,768,128]{2,1,0:T(8,128)(2,1)S(1)} %get-tuple-element.23, bf16[1,768,128]{2,1,0:T(8,128)(2,1)S(1)} %bitcast.84), kind=kOutput, calls=%fused_computation | convolution fusion | flops 908918784 | bytes 4128768 | tf_op jit(solution)/shard_map/cik,ckzxm->izxm/dot_general | solution.py:229
  68.4 1.9 %collective-permute-start.4 = (bf16[768,2,4,192]{0,3,2,1:T(8,128)(2,1)}, bf16[768,2,4,192]{0,3,2,1:T(8,128)(2,1)}, u32[]{:S(2)}, u32[]{:S(2)}) collective-permute-start(bf16[768,2,4,192]{0,3,2,1:T(8,128)(2,1)} %bitcast_convert_fusion), channel_id=1, source_target_pairs={{0,1},{1,0},{2,3},{3,2},{4,5},{5,4},{6,7},{7,6},{8,9},{9,8},{10,11... | collective-permute-start | bytes 7077896 | tf_op jit(solution)/shard_map/ppermute | solution.py:233
  70.4 4.8 %collective-permute-done.4 = bf16[768,2,4,192]{0,3,2,1:T(8,128)(2,1)} collective-permute-done((bf16[768,2,4,192]{0,3,2,1:T(8,128)(2,1)}, bf16[768,2,4,192]{0,3,2,1:T(8,128)(2,1)}, u32[]{:S(2)}, u32[]{:S(2)}) %collective-permute-start.4) | collective-permute-done | bytes 2359328 | tf_op jit(solution)/shard_map/ppermute | solution.py:233
  75.2 3.1 %convert_add_fusion = f32[768,2,4,192]{0,3,2,1:T(8,128)S(1)} fusion(bf16[768,2,4,192]{0,3,2,1:T(8,128)(2,1)} %collective-permute-done.4, bf16[3,128,2,4,1,192]{1,5,4,3,2,0:T(8,128)(2,1)S(1)} %copy-done.4, bf16[1,768,128]{2,1,0:T(8,128)(2,1)S(1)} %get-tuple-element.24, bf16[1,768,128]{2,1,0:T(8,128)(2,1)S(1)} %get-tuple-element.23, ...), kind=kOutput, calls=%fused_computation.2 | convolution fusion | flops 912457728 | bytes 8847360 | tf_op jit(solution)/shard_map/cik,ckzxm->izxm/dot_general | solution.py:229
  78.5 1.9 %collective-permute-start.5 = (bf16[384,2,192]{0,2,1:T(8,128)(2,1)S(1)}, bf16[384,2,192]{0,2,1:T(8,128)(2,1)S(1)}, u32[]{:S(2)}, u32[]{:S(2)}) collective-permute-start(bf16[384,2,192]{0,2,1:T(8,128)(2,1)S(1)} %get-tuple-element.21), channel_id=1, source_target_pairs={{0,2},{2,4},{4,6},{6,0},{1,3},{3,5},{5,7},{7,1},{8,10},{10,12},{12... | collective-permute-start | bytes 884744 | tf_op jit(solution)/shard_map/ppermute | solution.py:63
  80.4 3.9 %collective-permute-start.7 = (bf16[384,2,192]{0,2,1:T(8,128)(2,1)S(1)}, bf16[384,2,192]{0,2,1:T(8,128)(2,1)S(1)}, u32[]{:S(2)}, u32[]{:S(2)}) collective-permute-start(bf16[384,2,192]{0,2,1:T(8,128)(2,1)S(1)} %get-tuple-element.22), channel_id=1, source_target_pairs={{0,6},{2,0},{4,2},{6,4},{1,7},{3,1},{5,3},{7,5},{8,14},{10,8},{12,... | collective-permute-start | bytes 884744 | tf_op jit(solution)/shard_map/ppermute | solution.py:64
  84.5 4.9 %collective-permute-done.5 = bf16[384,2,192]{0,2,1:T(8,128)(2,1)S(1)} collective-permute-done((bf16[384,2,192]{0,2,1:T(8,128)(2,1)S(1)}, bf16[384,2,192]{0,2,1:T(8,128)(2,1)S(1)}, u32[]{:S(2)}, u32[]{:S(2)}) %collective-permute-start.5) | collective-permute-done | bytes 294944 | tf_op jit(solution)/shard_map/ppermute | solution.py:63
  89.6 3.4 %collective-permute-start.6 = (bf16[768,2,192]{0,2,1:T(8,128)(2,1)S(1)}, bf16[768,2,192]{0,2,1:T(8,128)(2,1)S(1)}, u32[]{:S(2)}, u32[]{:S(2)}) collective-permute-start(bf16[768,2,192]{0,2,1:T(8,128)(2,1)S(1)} %pad_maximum_fusion.2), channel_id=1, source_target_pairs={{0,2},{2,4},{4,6},{6,0},{1,3},{3,5},{5,7},{7,1},{8,10},{10,12},{12... | collective-permute-start | bytes 1769480 | tf_op jit(solution)/shard_map/ppermute | solution.py:69
  93.2 2.4 %collective-permute-start.8 = (bf16[768,2,192]{0,2,1:T(8,128)(2,1)S(1)}, bf16[768,2,192]{0,2,1:T(8,128)(2,1)S(1)}, u32[]{:S(2)}, u32[]{:S(2)}) collective-permute-start(bf16[768,2,192]{0,2,1:T(8,128)(2,1)S(1)} %pad_maximum_fusion.3), channel_id=1, source_target_pairs={{0,6},{2,0},{4,2},{6,4},{1,7},{3,1},{5,3},{7,5},{8,14},{10,8},{12,... | collective-permute-start | bytes 1769480 | tf_op jit(solution)/shard_map/ppermute | solution.py:70
  95.6 10.4 %collective-permute-done.6 = bf16[768,2,192]{0,2,1:T(8,128)(2,1)S(1)} collective-permute-done((bf16[768,2,192]{0,2,1:T(8,128)(2,1)S(1)}, bf16[768,2,192]{0,2,1:T(8,128)(2,1)S(1)}, u32[]{:S(2)}, u32[]{:S(2)}) %collective-permute-start.6) | collective-permute-done | bytes 589856 | tf_op jit(solution)/shard_map/ppermute | solution.py:69
  106.0 4.8 %collective-permute-done.8 = bf16[768,2,192]{0,2,1:T(8,128)(2,1)S(1)} collective-permute-done((bf16[768,2,192]{0,2,1:T(8,128)(2,1)S(1)}, bf16[768,2,192]{0,2,1:T(8,128)(2,1)S(1)}, u32[]{:S(2)}, u32[]{:S(2)}) %collective-permute-start.8) | collective-permute-done | bytes 589856 | tf_op jit(solution)/shard_map/ppermute | solution.py:70
  110.8 1.4 %fusion.1 = f32[768,2,192]{0,2,1:T(8,128)S(1)} fusion(bf16[768,2,192]{0,2,1:T(8,128)(2,1)S(1)} %collective-permute-done.8, bf16[768,2,192]{0,2,1:T(8,128)(2,1)S(1)} %collective-permute-done.6, f32[768,2,4,192]{0,3,2,1:T(8,128)} %copy-done.3, s32[]{:T(128)S(6)} %select_n.82), kind=kLoop, calls=%fused_computation.10 | loop fusion | flops 1179648 | bytes 3538948 | tf_op jit(solution)/shard_map/add | solution.py:71
  112.3 9.1 %collective-permute-start.9 = (bf16[768,192]{0,1:T(8,128)(2,1)S(1)}, bf16[768,192]{0,1:T(8,128)(2,1)S(1)}, u32[]{:S(2)}, u32[]{:S(2)}) collective-permute-start(bf16[768,192]{0,1:T(8,128)(2,1)S(1)} %fusion.15), channel_id=1, source_target_pairs={{0,8},{8,0},{1,9},{9,1},{2,10},{10,2},{3,11},{11,3},{4,12},{12,4},... | collective-permute-start | bytes 884744 | tf_op jit(solution)/shard_map/ppermute | solution.py:87
  121.4 19.2 %collective-permute-done.9 = bf16[768,192]{0,1:T(8,128)(2,1)S(1)} collective-permute-done((bf16[768,192]{0,1:T(8,128)(2,1)S(1)}, bf16[768,192]{0,1:T(8,128)(2,1)S(1)}, u32[]{:S(2)}, u32[]{:S(2)}) %collective-permute-start.9) | collective-permute-done | bytes 294944 | tf_op jit(solution)/shard_map/ppermute | solution.py:87
  (45 shorter events, 10.3 us)
Async XLA Ops:
  1.1 12.7 %collective-permute-start = (bf16[2,768,128]{2,1,0:T(8,128)(2,1)S(1)}, bf16[2,768,128]{2,1,0:T(8,128)(2,1)S(1)}, u32[]{:S(2)}, u32[]{:S(2)}) collective-permute-start(bf16[2,768,128]{2,1,0:T(8,128)(2,1)S(1)} %pad_maximum_fusion.4), channel_id=1, source_target_pairs={{0,16},{16,32},{32,48},{48,64},{64,80},{80,96},{96,112},{112,128},... | collective-permute-start | bytes 1179656 | tf_op jit(solution)/shard_map/ppermute | solution.py:21
  5.3 21.5 %collective-permute-start.1 = (bf16[2,768,128]{2,1,0:T(8,128)(2,1)S(1)}, bf16[2,768,128]{2,1,0:T(8,128)(2,1)S(1)}, u32[]{:S(2)}, u32[]{:S(2)}) collective-permute-start(bf16[2,768,128]{2,1,0:T(8,128)(2,1)S(1)} %pad_maximum_fusion.4), channel_id=1, source_target_pairs={{16,0},{32,16},{48,32},{64,48},{80,64},{96,80},{112,96},{128,112},... | collective-permute-start | bytes 1179656 | tf_op jit(solution)/shard_map/ppermute | solution.py:23
  28.0 0.9 copy-start
  28.0 1.0 copy-start.1
  28.0 1.1 copy-start.2
  37.7 14.6 %collective-permute-start.2 = (bf16[2,768,1,128]{3,1,2,0:T(8,128)(2,1)}, bf16[2,768,1,128]{3,1,2,0:T(8,128)(2,1)S(1)}, u32[]{:S(2)}, u32[]{:S(2)}) collective-permute-start(bf16[2,768,1,128]{3,1,2,0:T(8,128)(2,1)} %get-tuple-element.17), channel_id=1, source_target_pairs={{16,0},{32,16},{48,32},{64,48},{80,64},{96,80},{112,96},{128,112},... | collective-permute-start | bytes 1179656 | tf_op jit(solution)/shard_map/ppermute | solution.py:32
  39.6 25.8 %collective-permute-start.3 = (bf16[2,768,1,128]{3,1,2,0:T(8,128)(2,1)}, bf16[2,768,1,128]{3,1,2,0:T(8,128)(2,1)S(1)}, u32[]{:S(2)}, u32[]{:S(2)}) collective-permute-start(bf16[2,768,1,128]{3,1,2,0:T(8,128)(2,1)} %get-tuple-element.18), channel_id=1, source_target_pairs={{752,0},{0,16},{16,32},{32,48},{48,64},{64,80},{80,96},{96,112},{1... | collective-permute-start | bytes 1179656 | tf_op jit(solution)/shard_map/ppermute | solution.py:32
  65.6 9.6 %copy-start.4 = (bf16[3,128,2,4,1,192]{1,5,4,3,2,0:T(8,128)(2,1)S(1)}, bf16[3,128,2,4,1,192]{1,5,4,3,2,0:T(8,128)(2,1)}, u32[]{:S(2)}) copy-start(bf16[3,128,2,4,1,192]{1,5,4,3,2,0:T(8,128)(2,1)} %get-tuple-element.15) | copy-start | bytes 3538948
  68.4 6.8 %collective-permute-start.4 = (bf16[768,2,4,192]{0,3,2,1:T(8,128)(2,1)}, bf16[768,2,4,192]{0,3,2,1:T(8,128)(2,1)}, u32[]{:S(2)}, u32[]{:S(2)}) collective-permute-start(bf16[768,2,4,192]{0,3,2,1:T(8,128)(2,1)} %bitcast_convert_fusion), channel_id=1, source_target_pairs={{0,1},{1,0},{2,3},{3,2},{4,5},{5,4},{6,7},{7,6},{8,9},{9,8},{10,11... | collective-permute-start | bytes 7077896 | tf_op jit(solution)/shard_map/ppermute | solution.py:233
  78.3 14.7 %copy-start.3 = (f32[768,2,4,192]{0,3,2,1:T(8,128)}, f32[768,2,4,192]{0,3,2,1:T(8,128)S(1)}, u32[]{:S(2)}) copy-start(f32[768,2,4,192]{0,3,2,1:T(8,128)S(1)} %convert_add_fusion) | copy-start | bytes 14155780
  78.5 10.9 %collective-permute-start.5 = (bf16[384,2,192]{0,2,1:T(8,128)(2,1)S(1)}, bf16[384,2,192]{0,2,1:T(8,128)(2,1)S(1)}, u32[]{:S(2)}, u32[]{:S(2)}) collective-permute-start(bf16[384,2,192]{0,2,1:T(8,128)(2,1)S(1)} %get-tuple-element.21), channel_id=1, source_target_pairs={{0,2},{2,4},{4,6},{6,0},{1,3},{3,5},{5,7},{7,1},{8,10},{10,12},{12... | collective-permute-start | bytes 884744 | tf_op jit(solution)/shard_map/ppermute | solution.py:63
  80.4 12.6 %collective-permute-start.7 = (bf16[384,2,192]{0,2,1:T(8,128)(2,1)S(1)}, bf16[384,2,192]{0,2,1:T(8,128)(2,1)S(1)}, u32[]{:S(2)}, u32[]{:S(2)}) collective-permute-start(bf16[384,2,192]{0,2,1:T(8,128)(2,1)S(1)} %get-tuple-element.22), channel_id=1, source_target_pairs={{0,6},{2,0},{4,2},{6,4},{1,7},{3,1},{5,3},{7,5},{8,14},{10,8},{12,... | collective-permute-start | bytes 884744 | tf_op jit(solution)/shard_map/ppermute | solution.py:64
  89.6 16.4 %collective-permute-start.6 = (bf16[768,2,192]{0,2,1:T(8,128)(2,1)S(1)}, bf16[768,2,192]{0,2,1:T(8,128)(2,1)S(1)}, u32[]{:S(2)}, u32[]{:S(2)}) collective-permute-start(bf16[768,2,192]{0,2,1:T(8,128)(2,1)S(1)} %pad_maximum_fusion.2), channel_id=1, source_target_pairs={{0,2},{2,4},{4,6},{6,0},{1,3},{3,5},{5,7},{7,1},{8,10},{10,12},{12... | collective-permute-start | bytes 1769480 | tf_op jit(solution)/shard_map/ppermute | solution.py:69
  93.2 17.6 %collective-permute-start.8 = (bf16[768,2,192]{0,2,1:T(8,128)(2,1)S(1)}, bf16[768,2,192]{0,2,1:T(8,128)(2,1)S(1)}, u32[]{:S(2)}, u32[]{:S(2)}) collective-permute-start(bf16[768,2,192]{0,2,1:T(8,128)(2,1)S(1)} %pad_maximum_fusion.3), channel_id=1, source_target_pairs={{0,6},{2,0},{4,2},{6,4},{1,7},{3,1},{5,3},{7,5},{8,14},{10,8},{12,... | collective-permute-start | bytes 1769480 | tf_op jit(solution)/shard_map/ppermute | solution.py:70
  112.3 28.3 %collective-permute-start.9 = (bf16[768,192]{0,1:T(8,128)(2,1)S(1)}, bf16[768,192]{0,1:T(8,128)(2,1)S(1)}, u32[]{:S(2)}, u32[]{:S(2)}) collective-permute-start(bf16[768,192]{0,1:T(8,128)(2,1)S(1)} %fusion.15), channel_id=1, source_target_pairs={{0,8},{8,0},{1,9},{9,1},{2,10},{10,2},{3,11},{11,3},{4,12},{12,4},... | collective-permute-start | bytes 884744 | tf_op jit(solution)/shard_map/ppermute | solution.py:87

commit v8 on v7

--- a/solution.py
+++ b/solution.py
@@ -71,9 +71,45 @@
     return pick(block, 1, x) + got_left.astype(jnp.float32) + got_right.astype(jnp.float32)
 
 
+def four_then_pair(block):
+    x = lax.axis_index("x")
+    zh = lax.axis_index("zh")
+    rows = block.shape[0]
+    top = slice(0, rows // 2)
+    bottom = slice(rows // 2, rows)
+    cw = [(i, (i + 1) % 4) for i in range(4)]
+    ccw = [(i, (i - 1) % 4) for i in range(4)]
+    opposite = pick(block, 1, (x + 2) % 4)
+    from_left = lax.ppermute(opposite[top].astype(jnp.bfloat16), "x", cw).astype(jnp.float32)
+    from_right = lax.ppermute(opposite[bottom].astype(jnp.bfloat16), "x", ccw).astype(
+        jnp.float32
+    )
+    right = pick(block, 1, (x + 1) % 4)
+    left = pick(block, 1, (x - 1) % 4)
+    own = pick(block, 1, x)
+
+    def second_round(sub):
+        to_right = jnp.concatenate(
+            [pick(right, 1, sub)[top] + pick(from_left, 1, sub), pick(right, 1, sub)[bottom]]
+        )
+        to_left = jnp.concatenate(
+            [pick(left, 1, sub)[top], pick(left, 1, sub)[bottom] + pick(from_right, 1, sub)]
+        )
+        got_left = lax.ppermute(to_right.astype(jnp.bfloat16), "x", cw)
+        got_right = lax.ppermute(to_left.astype(jnp.bfloat16), "x", ccw)
+        return pick(own, 1, sub) + got_left.astype(jnp.float32) + got_right.astype(jnp.float32)
+
+    sent = second_round(1 - zh).astype(jnp.bfloat16)
+    got = lax.ppermute(sent, "zh", [(0, 1), (1, 0)])
+    kept = second_round(zh)
+    return kept + got.astype(jnp.float32)
+
+
 def reduce_scatter(sums):
     zh = lax.axis_index("zh")
     n_x, n_zh = sums.shape[2], sums.shape[1]
+    if n_x == 4 and n_zh == 2:
+        return four_then_pair(jnp.swapaxes(sums, 1, 2))
     if n_x == 4:
         sums = four_scatter(jnp.swapaxes(sums, 1, 2))
     elif n_x > 1:

time: 142 us -> 142 us (level)
  the two profiles are of different devices: /device:TPU:70 before, /device:TPU:64 now
where the time goes in v8:
time: 142 us; the launch traced here: 141 us
  starting transfers between devices  54.6 us (38%)
  waiting for transfers between devices  49 us (35%)
  local copies, waits for them, and re-layouts  14.3 us (10%)
  other arithmetic  9.58 us (7%)
  Pallas kernels  7.49 us (5%)
  matrix products  5.93 us (4%)
    ppermute x1, waiting for transfers between devices, four_then_pair(): got = lax.ppermute(sent, 'zh', [(0, 1), (1, 0)])  18.6 us
    ppermute x2, waiting for transfers between devices, passed_along(): return lax.ppermute(block, axis, route)  10.2 us
    ppermute x1, waiting for transfers between devices, with_halo(): lax.ppermute(head, axis, [((i + 1) % count, i) for i in range(count)])  9.23 us
    ppermute x1, starting transfers between devices, four_then_pair(): got = lax.ppermute(sent, 'zh', [(0, 1), (1, 0)])  9.18 us
    ppermute x2, starting transfers between devices, second_round(): got_right = lax.ppermute(to_left.astype(jnp.bfloat16), 'x', ccw)  8.48 us
    ppermute x1, starting transfers between devices, with_halo(): lax.ppermute(head, axis, [((i + 1) % count, i) for i in range(count)])  8.19 us
    unnamed x15, local copies, waits for them, and re-layouts  7.59 us
    pallas_call x1, Pallas kernels, attention(): pl.pallas_call(attention_kernel, grid=(tiles,), in_specs=[row_spec, row_s...  7.49 us
  transfers between devices with their start and end apart: 12, of which 7 were waited for; matrix products, arithmetic and copies ran while one was open for 10% of the time, Pallas kernels for 0%

profile of v8, /device:TPU:64, one launch (start us, length us, event | category | flops | bytes accessed | tf_op | source)
XLA Modules:
  0.0 141.3 jit_solution(14375013336411269142)
XLA Ops:
  1.1 4.3 %collective-permute-start = (bf16[2,768,128]{2,1,0:T(8,128)(2,1)S(1)}, bf16[2,768,128]{2,1,0:T(8,128)(2,1)S(1)}, u32[]{:S(2)}, u32[]{:S(2)}) collective-permute-start(bf16[2,768,128]{2,1,0:T(8,128)(2,1)S(1)} %pad_maximum_fusion.2), channel_id=1, source_target_pairs={{0,16},{16,32},{32,48},{48,64},{64,80},{80,96},{96,112},{112,128},... | collective-permute-start | bytes 1179656 | tf_op jit(solution)/shard_map/ppermute | solution.py:21
  5.3 8.2 %collective-permute-start.1 = (bf16[2,768,128]{2,1,0:T(8,128)(2,1)S(1)}, bf16[2,768,128]{2,1,0:T(8,128)(2,1)S(1)}, u32[]{:S(2)}, u32[]{:S(2)}) collective-permute-start(bf16[2,768,128]{2,1,0:T(8,128)(2,1)S(1)} %pad_maximum_fusion.2), channel_id=1, source_target_pairs={{16,0},{32,16},{48,32},{64,48},{80,64},{96,80},{112,96},{128,112},... | collective-permute-start | bytes 1179656 | tf_op jit(solution)/shard_map/ppermute | solution.py:23
  17.7 9.2 %collective-permute-done.1 = bf16[2,768,128]{2,1,0:T(8,128)(2,1)S(1)} collective-permute-done((bf16[2,768,128]{2,1,0:T(8,128)(2,1)S(1)}, bf16[2,768,128]{2,1,0:T(8,128)(2,1)S(1)}, u32[]{:S(2)}, u32[]{:S(2)}) %collective-permute-start.1) | collective-permute-done | bytes 393248 | tf_op jit(solution)/shard_map/ppermute | solution.py:23
  29.1 7.5 %shard_map.82 = (bf16[768,128]{1,0:T(8,128)(2,1)S(1)}, f32[2304,128]{1,0:T(8,128)S(1)}, f32[2304,128]{1,0:T(8,128)S(1)}) custom-call(bf16[768,128]{1,0:T(8,128)(2,1)S(1)} %copy-done, bf16[768,128]{1,0:T(8,128)(2,1)S(1)} %copy-done.1, bf16[768,128]{1,0:T(8,128)(2,1)S(1)} %copy-done.2, bf16[2304,128]{1,0:T(8,128)(2,1)S(1)} %get-tuple-element.28.k_ref, ...), custom_call_target="tpu_custom_call" | custom-call | flops 2264924160 | bytes 4128768 | tf_op jit(solution)/shard_map/pallas_call | solution.py:176
  37.7 4.8 %collective-permute-start.2 = (bf16[2,768,1,128]{3,1,2,0:T(8,128)(2,1)}, bf16[2,768,1,128]{3,1,2,0:T(8,128)(2,1)S(1)}, u32[]{:S(2)}, u32[]{:S(2)}) collective-permute-start(bf16[2,768,1,128]{3,1,2,0:T(8,128)(2,1)} %get-tuple-element.25), channel_id=1, source_target_pairs={{16,0},{32,16},{48,32},{64,48},{80,64},{96,80},{112,96},{128,112},... | collective-permute-start | bytes 1179656 | tf_op jit(solution)/shard_map/ppermute | solution.py:32
  42.5 2.2 %collective-permute-start.3 = (bf16[2,768,1,128]{3,1,2,0:T(8,128)(2,1)}, bf16[2,768,1,128]{3,1,2,0:T(8,128)(2,1)S(1)}, u32[]{:S(2)}, u32[]{:S(2)}) collective-permute-start(bf16[2,768,1,128]{3,1,2,0:T(8,128)(2,1)} %get-tuple-element.26), channel_id=1, source_target_pairs={{752,0},{0,16},{16,32},{32,48},{48,64},{64,80},{80,96},{96,112},{1... | collective-permute-start | bytes 1179656 | tf_op jit(solution)/shard_map/ppermute | solution.py:32
  44.8 4.3 %copy.14 = bf16[3,128,3072]{1,2,0:T(8,128)(2,1)} copy(bf16[3,128,3072]{2,1,0:T(8,128)(2,1)} %param.13) | data formatting | bytes 4718592 | tf_op args[5]
  49.0 2.8 %constant_dynamic-slice_fusion.1 = (bf16[3,128,2,4,1,192]{1,5,4,3,2,0:T(8,128)(2,1)}, bf16[3,128,2,4,1,192]{1,5,4,3,2,0:T(8,128)(2,1)S(1)}) fusion(bf16[3,128,2,4,2,192]{1,5,4,3,2,0:T(8,128)(2,1)} %bitcast.108, s32[]{:T(128)S(6)} %select_n.95, s32[]{:T(128)S(6)} %select_n.96), kind=kLoop, calls=%fused_computation.60 | loop fusion | bytes 4718600 | tf_op jit(solution)/shard_map/jit(dynamic_index_in_dim)/dynamic_slice | solution.py:36
  52.3 9.8 %collective-permute-done.3 = bf16[2,768,1,128]{3,1,2,0:T(8,128)(2,1)S(1)} collective-permute-done((bf16[2,768,1,128]{3,1,2,0:T(8,128)(2,1)}, bf16[2,768,1,128]{3,1,2,0:T(8,128)(2,1)S(1)}, u32[]{:S(2)}, u32[]{:S(2)}) %collective-permute-start.3) | collective-permute-done | bytes 393248 | tf_op jit(solution)/shard_map/ppermute | solution.py:32
  62.3 2.8 %bitcast_convert_fusion = bf16[768,2,4,192]{0,3,2,1:T(8,128)(2,1)} fusion(bf16[3,128,2,4,1,192]{1,5,4,3,2,0:T(8,128)(2,1)S(1)} %get-tuple-element.24, bf16[1,768,128]{2,1,0:T(8,128)(2,1)S(1)} %get-tuple-element.32, bf16[1,768,128]{2,1,0:T(8,128)(2,1)S(1)} %get-tuple-element.31, bf16[1,768,128]{2,1,0:T(8,128)(2,1)S(1)} %bitcast.106), kind=kOutput, calls=%fused_computation | convolution fusion | flops 908918784 | bytes 4128768 | tf_op jit(solution)/shard_map/cik,ckzxm->izxm/dot_general | solution.py:265
  65.1 1.9 %collective-permute-start.4 = (bf16[768,2,4,192]{0,3,2,1:T(8,128)(2,1)}, bf16[768,2,4,192]{0,3,2,1:T(8,128)(2,1)}, u32[]{:S(2)}, u32[]{:S(2)}) collective-permute-start(bf16[768,2,4,192]{0,3,2,1:T(8,128)(2,1)} %bitcast_convert_fusion), channel_id=1, source_target_pairs={{0,1},{1,0},{2,3},{3,2},{4,5},{5,4},{6,7},{7,6},{8,9},{9,8},{10,11... | collective-permute-start | bytes 7077896 | tf_op jit(solution)/shard_map/ppermute | solution.py:269
  67.0 4.8 %collective-permute-done.4 = bf16[768,2,4,192]{0,3,2,1:T(8,128)(2,1)} collective-permute-done((bf16[768,2,4,192]{0,3,2,1:T(8,128)(2,1)}, bf16[768,2,4,192]{0,3,2,1:T(8,128)(2,1)}, u32[]{:S(2)}, u32[]{:S(2)}) %collective-permute-start.4) | collective-permute-done | bytes 2359328 | tf_op jit(solution)/shard_map/ppermute | solution.py:269
  71.9 3.1 %convert_add_fusion = f32[768,2,4,192]{0,3,2,1:T(8,128)S(1)} fusion(bf16[768,2,4,192]{0,3,2,1:T(8,128)(2,1)} %collective-permute-done.4, bf16[3,128,2,4,1,192]{1,5,4,3,2,0:T(8,128)(2,1)S(1)} %copy-done.4, bf16[1,768,128]{2,1,0:T(8,128)(2,1)S(1)} %get-tuple-element.32, bf16[1,768,128]{2,1,0:T(8,128)(2,1)S(1)} %get-tuple-element.31, ...), kind=kOutput, calls=%fused_computation.2 | convolution fusion | flops 912457728 | bytes 8847360 | tf_op jit(solution)/shard_map/cik,ckzxm->izxm/dot_general | solution.py:265
  75.0 2.1 %copy-done.3 = f32[768,2,4,192]{0,3,2,1:T(8,128)} copy-done((f32[768,2,4,192]{0,3,2,1:T(8,128)}, f32[768,2,4,192]{0,3,2,1:T(8,128)S(1)}, u32[]{:S(2)}) %copy-start.3) | copy-done | bytes 4718616
  77.2 6.7 %collective-permute-start.5 = (bf16[384,2,192]{0,2,1:T(8,128)(2,1)S(1)}, bf16[384,2,192]{0,2,1:T(8,128)(2,1)S(1)}, u32[]{:S(2)}, u32[]{:S(2)}) collective-permute-start(bf16[384,2,192]{0,2,1:T(8,128)(2,1)S(1)} %get-tuple-element.29), channel_id=1, source_target_pairs={{0,2},{2,4},{4,6},{6,0},{1,3},{3,5},{5,7},{7,1},{8,10},{10,12},{12... | collective-permute-start | bytes 884744 | tf_op jit(solution)/shard_map/ppermute | solution.py:83
  84.0 3.2 %collective-permute-start.7 = (bf16[384,2,192]{0,2,1:T(8,128)(2,1)S(1)}, bf16[384,2,192]{0,2,1:T(8,128)(2,1)S(1)}, u32[]{:S(2)}, u32[]{:S(2)}) collective-permute-start(bf16[384,2,192]{0,2,1:T(8,128)(2,1)S(1)} %get-tuple-element.30), channel_id=1, source_target_pairs={{0,6},{2,0},{4,2},{6,4},{1,7},{3,1},{5,3},{7,5},{8,14},{10,8},{12,... | collective-permute-start | bytes 884744 | tf_op jit(solution)/shard_map/ppermute | solution.py:84
  88.5 4.0 %collective-permute-done.5 = bf16[384,2,192]{0,2,1:T(8,128)(2,1)S(1)} collective-permute-done((bf16[384,2,192]{0,2,1:T(8,128)(2,1)S(1)}, bf16[384,2,192]{0,2,1:T(8,128)(2,1)S(1)}, u32[]{:S(2)}, u32[]{:S(2)}) %collective-permute-start.5) | collective-permute-done | bytes 294944 | tf_op jit(solution)/shard_map/ppermute | solution.py:83
  92.6 2.0 %collective-permute-done.7 = bf16[384,2,192]{0,2,1:T(8,128)(2,1)S(1)} collective-permute-done((bf16[384,2,192]{0,2,1:T(8,128)(2,1)S(1)}, bf16[384,2,192]{0,2,1:T(8,128)(2,1)S(1)}, u32[]{:S(2)}, u32[]{:S(2)}) %collective-permute-start.7) | collective-permute-done | bytes 294944 | tf_op jit(solution)/shard_map/ppermute | solution.py:84
  96.1 3.4 %collective-permute-start.9 = (bf16[768,192]{0,1:T(8,128)(2,1)S(1)}, bf16[768,192]{0,1:T(8,128)(2,1)S(1)}, u32[]{:S(2)}, u32[]{:S(2)}) collective-permute-start(bf16[768,192]{0,1:T(8,128)(2,1)S(1)} %pad_maximum_fusion.5), channel_id=1, source_target_pairs={{0,2},{2,4},{4,6},{6,0},{1,3},{3,5},{5,7},{7,1},{8,10},{10,12},{12... | collective-permute-start | bytes 884744 | tf_op jit(solution)/shard_map/ppermute | solution.py:98
  99.5 3.6 %collective-permute-start.10 = (bf16[768,192]{0,1:T(8,128)(2,1)S(1)}, bf16[768,192]{0,1:T(8,128)(2,1)S(1)}, u32[]{:S(2)}, u32[]{:S(2)}) collective-permute-start(bf16[768,192]{0,1:T(8,128)(2,1)S(1)} %pad_maximum_fusion.6), channel_id=1, source_target_pairs={{0,6},{2,0},{4,2},{6,4},{1,7},{3,1},{5,3},{7,5},{8,14},{10,8},{12,... | collective-permute-start | bytes 884744 | tf_op jit(solution)/shard_map/ppermute | solution.py:99
  103.2 2.2 %collective-permute-start.6 = (bf16[768,192]{0,1:T(8,128)(2,1)S(1)}, bf16[768,192]{0,1:T(8,128)(2,1)S(1)}, u32[]{:S(2)}, u32[]{:S(2)}) collective-permute-start(bf16[768,192]{0,1:T(8,128)(2,1)S(1)} %pad_maximum_fusion.3), channel_id=1, source_target_pairs={{0,2},{2,4},{4,6},{6,0},{1,3},{3,5},{5,7},{7,1},{8,10},{10,12},{12... | collective-permute-start | bytes 884744 | tf_op jit(solution)/shard_map/ppermute | solution.py:98
  105.5 4.8 %collective-permute-start.8 = (bf16[768,192]{0,1:T(8,128)(2,1)S(1)}, bf16[768,192]{0,1:T(8,128)(2,1)S(1)}, u32[]{:S(2)}, u32[]{:S(2)}) collective-permute-start(bf16[768,192]{0,1:T(8,128)(2,1)S(1)} %pad_maximum_fusion.4), channel_id=1, source_target_pairs={{0,6},{2,0},{4,2},{6,4},{1,7},{3,1},{5,3},{7,5},{8,14},{10,8},{12,... | collective-permute-start | bytes 884744 | tf_op jit(solution)/shard_map/ppermute | solution.py:99
  111.5 9.2 %collective-permute-start.11 = (bf16[768,192]{0,1:T(8,128)(2,1)S(1)}, bf16[768,192]{0,1:T(8,128)(2,1)S(1)}, u32[]{:S(2)}, u32[]{:S(2)}) collective-permute-start(bf16[768,192]{0,1:T(8,128)(2,1)S(1)} %fusion.10), channel_id=1, source_target_pairs={{0,8},{8,0},{1,9},{9,1},{2,10},{10,2},{3,11},{11,3},{4,12},{12,4},... | collective-permute-start | bytes 884744 | tf_op jit(solution)/shard_map/ppermute | solution.py:103
  120.7 18.6 %collective-permute-done.11 = bf16[768,192]{0,1:T(8,128)(2,1)S(1)} collective-permute-done((bf16[768,192]{0,1:T(8,128)(2,1)S(1)}, bf16[768,192]{0,1:T(8,128)(2,1)S(1)}, u32[]{:S(2)}, u32[]{:S(2)}) %collective-permute-start.11) | collective-permute-done | bytes 294944 | tf_op jit(solution)/shard_map/ppermute | solution.py:103
  (49 shorter events, 15.1 us)
Async XLA Ops:
  1.1 16.6 %collective-permute-start = (bf16[2,768,128]{2,1,0:T(8,128)(2,1)S(1)}, bf16[2,768,128]{2,1,0:T(8,128)(2,1)S(1)}, u32[]{:S(2)}, u32[]{:S(2)}) collective-permute-start(bf16[2,768,128]{2,1,0:T(8,128)(2,1)S(1)} %pad_maximum_fusion.2), channel_id=1, source_target_pairs={{0,16},{16,32},{32,48},{48,64},{64,80},{80,96},{96,112},{112,128},... | collective-permute-start | bytes 1179656 | tf_op jit(solution)/shard_map/ppermute | solution.py:21
  5.3 21.5 %collective-permute-start.1 = (bf16[2,768,128]{2,1,0:T(8,128)(2,1)S(1)}, bf16[2,768,128]{2,1,0:T(8,128)(2,1)S(1)}, u32[]{:S(2)}, u32[]{:S(2)}) collective-permute-start(bf16[2,768,128]{2,1,0:T(8,128)(2,1)S(1)} %pad_maximum_fusion.2), channel_id=1, source_target_pairs={{16,0},{32,16},{48,32},{64,48},{80,64},{96,80},{112,96},{128,112},... | collective-permute-start | bytes 1179656 | tf_op jit(solution)/shard_map/ppermute | solution.py:23
  28.0 0.9 copy-start
  28.0 1.0 copy-start.1
  28.0 1.1 copy-start.2
  37.7 14.6 %collective-permute-start.2 = (bf16[2,768,1,128]{3,1,2,0:T(8,128)(2,1)}, bf16[2,768,1,128]{3,1,2,0:T(8,128)(2,1)S(1)}, u32[]{:S(2)}, u32[]{:S(2)}) collective-permute-start(bf16[2,768,1,128]{3,1,2,0:T(8,128)(2,1)} %get-tuple-element.25), channel_id=1, source_target_pairs={{16,0},{32,16},{48,32},{64,48},{80,64},{96,80},{112,96},{128,112},... | collective-permute-start | bytes 1179656 | tf_op jit(solution)/shard_map/ppermute | solution.py:32
  42.5 19.6 %collective-permute-start.3 = (bf16[2,768,1,128]{3,1,2,0:T(8,128)(2,1)}, bf16[2,768,1,128]{3,1,2,0:T(8,128)(2,1)S(1)}, u32[]{:S(2)}, u32[]{:S(2)}) collective-permute-start(bf16[2,768,1,128]{3,1,2,0:T(8,128)(2,1)} %get-tuple-element.26), channel_id=1, source_target_pairs={{752,0},{0,16},{16,32},{32,48},{48,64},{64,80},{80,96},{96,112},{1... | collective-permute-start | bytes 1179656 | tf_op jit(solution)/shard_map/ppermute | solution.py:32
  62.3 9.6 %copy-start.4 = (bf16[3,128,2,4,1,192]{1,5,4,3,2,0:T(8,128)(2,1)S(1)}, bf16[3,128,2,4,1,192]{1,5,4,3,2,0:T(8,128)(2,1)}, u32[]{:S(2)}) copy-start(bf16[3,128,2,4,1,192]{1,5,4,3,2,0:T(8,128)(2,1)} %get-tuple-element.23) | copy-start | bytes 3538948
  65.1 6.8 %collective-permute-start.4 = (bf16[768,2,4,192]{0,3,2,1:T(8,128)(2,1)}, bf16[768,2,4,192]{0,3,2,1:T(8,128)(2,1)}, u32[]{:S(2)}, u32[]{:S(2)}) collective-permute-start(bf16[768,2,4,192]{0,3,2,1:T(8,128)(2,1)} %bitcast_convert_fusion), channel_id=1, source_target_pairs={{0,1},{1,0},{2,3},{3,2},{4,5},{5,4},{6,7},{7,6},{8,9},{9,8},{10,11... | collective-permute-start | bytes 7077896 | tf_op jit(solution)/shard_map/ppermute | solution.py:269
  75.0 2.1 %copy-start.3 = (f32[768,2,4,192]{0,3,2,1:T(8,128)}, f32[768,2,4,192]{0,3,2,1:T(8,128)S(1)}, u32[]{:S(2)}) copy-start(f32[768,2,4,192]{0,3,2,1:T(8,128)S(1)} %convert_add_fusion) | copy-start | bytes 14155780
  77.2 15.3 %collective-permute-start.5 = (bf16[384,2,192]{0,2,1:T(8,128)(2,1)S(1)}, bf16[384,2,192]{0,2,1:T(8,128)(2,1)S(1)}, u32[]{:S(2)}, u32[]{:S(2)}) collective-permute-start(bf16[384,2,192]{0,2,1:T(8,128)(2,1)S(1)} %get-tuple-element.29), channel_id=1, source_target_pairs={{0,2},{2,4},{4,6},{6,0},{1,3},{3,5},{5,7},{7,1},{8,10},{10,12},{12... | collective-permute-start | bytes 884744 | tf_op jit(solution)/shard_map/ppermute | solution.py:83
  84.0 10.7 %collective-permute-start.7 = (bf16[384,2,192]{0,2,1:T(8,128)(2,1)S(1)}, bf16[384,2,192]{0,2,1:T(8,128)(2,1)S(1)}, u32[]{:S(2)}, u32[]{:S(2)}) collective-permute-start(bf16[384,2,192]{0,2,1:T(8,128)(2,1)S(1)} %get-tuple-element.30), channel_id=1, source_target_pairs={{0,6},{2,0},{4,2},{6,4},{1,7},{3,1},{5,3},{7,5},{8,14},{10,8},{12,... | collective-permute-start | bytes 884744 | tf_op jit(solution)/shard_map/ppermute | solution.py:84
  96.1 14.3 %collective-permute-start.9 = (bf16[768,192]{0,1:T(8,128)(2,1)S(1)}, bf16[768,192]{0,1:T(8,128)(2,1)S(1)}, u32[]{:S(2)}, u32[]{:S(2)}) collective-permute-start(bf16[768,192]{0,1:T(8,128)(2,1)S(1)} %pad_maximum_fusion.5), channel_id=1, source_target_pairs={{0,2},{2,4},{4,6},{6,0},{1,3},{3,5},{5,7},{7,1},{8,10},{10,12},{12... | collective-permute-start | bytes 884744 | tf_op jit(solution)/shard_map/ppermute | solution.py:98
  99.5 10.8 %collective-permute-start.10 = (bf16[768,192]{0,1:T(8,128)(2,1)S(1)}, bf16[768,192]{0,1:T(8,128)(2,1)S(1)}, u32[]{:S(2)}, u32[]{:S(2)}) collective-permute-start(bf16[768,192]{0,1:T(8,128)(2,1)S(1)} %pad_maximum_fusion.6), channel_id=1, source_target_pairs={{0,6},{2,0},{4,2},{6,4},{1,7},{3,1},{5,3},{7,5},{8,14},{10,8},{12,... | collective-permute-start | bytes 884744 | tf_op jit(solution)/shard_map/ppermute | solution.py:99
  103.2 17.5 %collective-permute-start.6 = (bf16[768,192]{0,1:T(8,128)(2,1)S(1)}, bf16[768,192]{0,1:T(8,128)(2,1)S(1)}, u32[]{:S(2)}, u32[]{:S(2)}) collective-permute-start(bf16[768,192]{0,1:T(8,128)(2,1)S(1)} %pad_maximum_fusion.3), channel_id=1, source_target_pairs={{0,2},{2,4},{4,6},{6,0},{1,3},{3,5},{5,7},{7,1},{8,10},{10,12},{12... | collective-permute-start | bytes 884744 | tf_op jit(solution)/shard_map/ppermute | solution.py:98
  105.5 15.2 %collective-permute-start.8 = (bf16[768,192]{0,1:T(8,128)(2,1)S(1)}, bf16[768,192]{0,1:T(8,128)(2,1)S(1)}, u32[]{:S(2)}, u32[]{:S(2)}) collective-permute-start(bf16[768,192]{0,1:T(8,128)(2,1)S(1)} %pad_maximum_fusion.4), channel_id=1, source_target_pairs={{0,6},{2,0},{4,2},{6,4},{1,7},{3,1},{5,3},{7,5},{8,14},{10,8},{12,... | collective-permute-start | bytes 884744 | tf_op jit(solution)/shard_map/ppermute | solution.py:99
  111.5 27.9 %collective-permute-start.11 = (bf16[768,192]{0,1:T(8,128)(2,1)S(1)}, bf16[768,192]{0,1:T(8,128)(2,1)S(1)}, u32[]{:S(2)}, u32[]{:S(2)}) collective-permute-start(bf16[768,192]{0,1:T(8,128)(2,1)S(1)} %fusion.10), channel_id=1, source_target_pairs={{0,8},{8,0},{1,9},{9,1},{2,10},{10,2},{3,11},{11,3},{4,12},{12,4},... | collective-permute-start | bytes 884744 | tf_op jit(solution)/shard_map/ppermute | solution.py:103

commit v9 on v7

--- a/solution.py
+++ b/solution.py
@@ -232,6 +232,7 @@
         other = term(pick(weight, 4, 1 - c)).astype(jnp.bfloat16)
         got = lax.ppermute(other, "c", [(0, 1), (1, 0)])
         mine = term(pick(weight, 4, c)).astype(jnp.bfloat16)
+        mine, got = lax.optimization_barrier((mine, got))
         sums = mine.astype(jnp.float32) + got.astype(jnp.float32)
     else:
         sums = term(weight[:, :, :, :, 0]).astype(jnp.bfloat16).astype(jnp.float32)

time: 142 us -> 139 us (0.979)
  waiting for transfers between devices: 73.2 us -> 70.3 us
    ppermute x1, waiting for transfers between devices: 4.79 us -> 1.97 us  [local(): got = lax.ppermute(other, 'c', [(0, 1), (1, 0)])]
    unnamed x16 -> x14, local copies, waits for them, and re-layouts: 5.54 us -> 5.54 us
  transfers between devices with their start and end apart: 10 -> 10, of which waited for: 9 -> 9; matrix products, arithmetic and copies ran while one was open for 8% -> 10% of each run, Pallas kernels for 0% -> 0%
where the time goes in v9:
time: 139 us
  waiting for transfers between devices  70.3 us (51%)
  starting transfers between devices  35.9 us (26%)
  local copies, waits for them, and re-layouts  11 us (8%)
  other arithmetic  7.9 us (6%)
  Pallas kernels  7.49 us (5%)
  matrix products  5.53 us (4%)
    ppermute x1, waiting for transfers between devices, reduce_scatter(): got = lax.ppermute(acc.astype(jnp.bfloat16), 'zh', route)  19.2 us
    ppermute x2, waiting for transfers between devices, passed_along(): return lax.ppermute(block, axis, route)  13.6 us
    ppermute x1, waiting for transfers between devices, with_halo(): lax.ppermute(head, axis, [((i + 1) % count, i) for i in range(count)])  13.1 us
    ppermute x1, waiting for transfers between devices, four_scatter(): got_left = lax.ppermute(to_right.astype(jnp.bfloat16), 'x', cw)  10.4 us
    ppermute x1, starting transfers between devices, reduce_scatter(): got = lax.ppermute(acc.astype(jnp.bfloat16), 'zh', route)  9.08 us
    pallas_call x1, Pallas kernels, attention(): pl.pallas_call(attention_kernel, grid=(tiles,), in_specs=[row_spec, row_s...  7.49 us
    ppermute x2, starting transfers between devices, passed_along(): return lax.ppermute(block, axis, route)  7 us
    unnamed x14, local copies, waits for them, and re-layouts  5.54 us
  transfers between devices with their start and end apart: 10, of which 9 were waited for; matrix products, arithmetic and copies ran while one was open for 10% of the time, Pallas kernels for 0%

profile of v9, /device:TPU:70, one launch (start us, length us, event | category | flops | bytes accessed | tf_op | source)
XLA Modules:
  0.0 138.6 jit_solution(16553276114856768188)
XLA Ops:
  1.1 4.3 %collective-permute-start = (bf16[2,768,128]{2,1,0:T(8,128)(2,1)S(1)}, bf16[2,768,128]{2,1,0:T(8,128)(2,1)S(1)}, u32[]{:S(2)}, u32[]{:S(2)}) collective-permute-start(bf16[2,768,128]{2,1,0:T(8,128)(2,1)S(1)} %pad_maximum_fusion.4), channel_id=1, source_target_pairs={{0,16},{16,32},{32,48},{48,64},{64,80},{80,96},{96,112},{112,128},... | collective-permute-start | bytes 1179656 | tf_op jit(solution)/shard_map/ppermute | solution.py:21
  5.3 1.9 %collective-permute-start.1 = (bf16[2,768,128]{2,1,0:T(8,128)(2,1)S(1)}, bf16[2,768,128]{2,1,0:T(8,128)(2,1)S(1)}, u32[]{:S(2)}, u32[]{:S(2)}) collective-permute-start(bf16[2,768,128]{2,1,0:T(8,128)(2,1)S(1)} %pad_maximum_fusion.4), channel_id=1, source_target_pairs={{16,0},{32,16},{48,32},{64,48},{80,64},{96,80},{112,96},{128,112},... | collective-permute-start | bytes 1179656 | tf_op jit(solution)/shard_map/ppermute | solution.py:23
  11.4 2.4 %collective-permute-done = bf16[2,768,128]{2,1,0:T(8,128)(2,1)S(1)} collective-permute-done((bf16[2,768,128]{2,1,0:T(8,128)(2,1)S(1)}, bf16[2,768,128]{2,1,0:T(8,128)(2,1)S(1)}, u32[]{:S(2)}, u32[]{:S(2)}) %collective-permute-start) | collective-permute-done | bytes 393248 | tf_op jit(solution)/shard_map/ppermute | solution.py:21
  13.8 13.1 %collective-permute-done.1 = bf16[2,768,128]{2,1,0:T(8,128)(2,1)S(1)} collective-permute-done((bf16[2,768,128]{2,1,0:T(8,128)(2,1)S(1)}, bf16[2,768,128]{2,1,0:T(8,128)(2,1)S(1)}, u32[]{:S(2)}, u32[]{:S(2)}) %collective-permute-start.1) | collective-permute-done | bytes 393248 | tf_op jit(solution)/shard_map/ppermute | solution.py:23
  29.1 7.5 %shard_map.82 = (bf16[768,128]{1,0:T(8,128)(2,1)S(1)}, f32[2304,128]{1,0:T(8,128)S(1)}, f32[2304,128]{1,0:T(8,128)S(1)}) custom-call(bf16[768,128]{1,0:T(8,128)(2,1)S(1)} %copy-done, bf16[768,128]{1,0:T(8,128)(2,1)S(1)} %copy-done.1, bf16[768,128]{1,0:T(8,128)(2,1)S(1)} %copy-done.2, bf16[2304,128]{1,0:T(8,128)(2,1)S(1)} %get-tuple-element.24.k_ref, ...), custom_call_target="tpu_custom_call" | custom-call | flops 2264924160 | bytes 4128768 | tf_op jit(solution)/shard_map/pallas_call | solution.py:140
  37.7 1.9 %collective-permute-start.2 = (bf16[2,768,1,128]{3,1,2,0:T(8,128)(2,1)}, bf16[2,768,1,128]{3,1,2,0:T(8,128)(2,1)S(1)}, u32[]{:S(2)}, u32[]{:S(2)}) collective-permute-start(bf16[2,768,1,128]{3,1,2,0:T(8,128)(2,1)} %get-tuple-element.21), channel_id=1, source_target_pairs={{16,0},{32,16},{48,32},{64,48},{80,64},{96,80},{112,96},{128,112},... | collective-permute-start | bytes 1179656 | tf_op jit(solution)/shard_map/ppermute | solution.py:32
  39.6 5.1 %collective-permute-start.3 = (bf16[2,768,1,128]{3,1,2,0:T(8,128)(2,1)}, bf16[2,768,1,128]{3,1,2,0:T(8,128)(2,1)S(1)}, u32[]{:S(2)}, u32[]{:S(2)}) collective-permute-start(bf16[2,768,1,128]{3,1,2,0:T(8,128)(2,1)} %get-tuple-element.22), channel_id=1, source_target_pairs={{752,0},{0,16},{16,32},{32,48},{48,64},{64,80},{80,96},{96,112},{1... | collective-permute-start | bytes 1179656 | tf_op jit(solution)/shard_map/ppermute | solution.py:32
  44.7 4.3 %copy.20 = bf16[3,128,3072]{1,2,0:T(8,128)(2,1)} copy(bf16[3,128,3072]{2,1,0:T(8,128)(2,1)} %param.13) | data formatting | bytes 4718592 | tf_op args[5]
  49.0 2.8 %constant_dynamic-slice_fusion = (bf16[3,128,2,4,1,192]{1,5,4,3,2,0:T(8,128)(2,1)S(1)}, bf16[3,128,2,4,1,192]{1,5,4,3,2,0:T(8,128)(2,1)}) fusion(bf16[3,128,2,4,2,192]{1,5,4,3,2,0:T(8,128)(2,1)} %bitcast.84, s32[]{:T(128)S(6)} %select_n.81, s32[]{:T(128)S(6)} %select_n.80), kind=kLoop, calls=%fused_computation.48 | loop fusion | bytes 4718600 | tf_op jit(solution)/shard_map/jit(dynamic_index_in_dim)/dynamic_slice | solution.py:36
  52.3 13.1 %collective-permute-done.3 = bf16[2,768,1,128]{3,1,2,0:T(8,128)(2,1)S(1)} collective-permute-done((bf16[2,768,1,128]{3,1,2,0:T(8,128)(2,1)}, bf16[2,768,1,128]{3,1,2,0:T(8,128)(2,1)S(1)}, u32[]{:S(2)}, u32[]{:S(2)}) %collective-permute-start.3) | collective-permute-done | bytes 393248 | tf_op jit(solution)/shard_map/ppermute | solution.py:32
  65.6 2.8 %bitcast_convert_fusion = bf16[768,2,4,192]{0,3,2,1:T(8,128)(2,1)} fusion(bf16[3,128,2,4,1,192]{1,5,4,3,2,0:T(8,128)(2,1)S(1)} %get-tuple-element.19, bf16[1,768,128]{2,1,0:T(8,128)(2,1)S(1)} %get-tuple-element.28, bf16[1,768,128]{2,1,0:T(8,128)(2,1)S(1)} %get-tuple-element.27, bf16[1,768,128]{2,1,0:T(8,128)(2,1)S(1)} %bitcast.82), kind=kOutput, calls=%fused_computation | convolution fusion | flops 908918784 | bytes 4128768 | tf_op jit(solution)/shard_map/cik,ckzxm->izxm/dot_general | solution.py:229
  68.4 1.9 %collective-permute-start.4 = (bf16[768,2,4,192]{0,3,2,1:T(8,128)(2,1)}, bf16[768,2,4,192]{0,3,2,1:T(8,128)(2,1)S(1)}, u32[]{:S(2)}, u32[]{:S(2)}) collective-permute-start(bf16[768,2,4,192]{0,3,2,1:T(8,128)(2,1)} %bitcast_convert_fusion), channel_id=1, source_target_pairs={{0,1},{1,0},{2,3},{3,2},{4,5},{5,4},{6,7},{7,6},{8,9},{9,8},{10,11... | collective-permute-start | bytes 7077896 | tf_op jit(solution)/shard_map/ppermute | solution.py:233
  70.4 2.7 %bitcast_convert_fusion.1 = bf16[768,2,4,192]{0,3,2,1:T(8,128)(2,1)S(1)} fusion(bf16[3,128,2,4,1,192]{1,5,4,3,2,0:T(8,128)(2,1)} %get-tuple-element.20, bf16[1,768,128]{2,1,0:T(8,128)(2,1)S(1)} %get-tuple-element.28, bf16[1,768,128]{2,1,0:T(8,128)(2,1)S(1)} %get-tuple-element.27, bf16[1,768,128]{2,1,0:T(8,128)(2,1)S(1)} %bitcast.83), kind=kOutput, calls=%fused_computation.1 | convolution fusion | flops 908918784 | bytes 4128768 | tf_op jit(solution)/shard_map/cik,ckzxm->izxm/dot_general | solution.py:229
  73.1 2.0 %collective-permute-done.4 = bf16[768,2,4,192]{0,3,2,1:T(8,128)(2,1)S(1)} collective-permute-done((bf16[768,2,4,192]{0,3,2,1:T(8,128)(2,1)}, bf16[768,2,4,192]{0,3,2,1:T(8,128)(2,1)S(1)}, u32[]{:S(2)}, u32[]{:S(2)}) %collective-permute-start.4) | collective-permute-done | bytes 2359328 | tf_op jit(solution)/shard_map/ppermute | solution.py:233
  75.8 1.9 %collective-permute-start.5 = (bf16[384,2,192]{0,2,1:T(8,128)(2,1)S(1)}, bf16[384,2,192]{0,2,1:T(8,128)(2,1)S(1)}, u32[]{:S(2)}, u32[]{:S(2)}) collective-permute-start(bf16[384,2,192]{0,2,1:T(8,128)(2,1)S(1)} %get-tuple-element.25), channel_id=1, source_target_pairs={{0,2},{2,4},{4,6},{6,0},{1,3},{3,5},{5,7},{7,1},{8,10},{10,12},{12... | collective-permute-start | bytes 884744 | tf_op jit(solution)/shard_map/ppermute | solution.py:63
  77.7 3.9 %collective-permute-start.7 = (bf16[384,2,192]{0,2,1:T(8,128)(2,1)S(1)}, bf16[384,2,192]{0,2,1:T(8,128)(2,1)S(1)}, u32[]{:S(2)}, u32[]{:S(2)}) collective-permute-start(bf16[384,2,192]{0,2,1:T(8,128)(2,1)S(1)} %get-tuple-element.26), channel_id=1, source_target_pairs={{0,6},{2,0},{4,2},{6,4},{1,7},{3,1},{5,3},{7,5},{8,14},{10,8},{12,... | collective-permute-start | bytes 884744 | tf_op jit(solution)/shard_map/ppermute | solution.py:64
  81.8 4.9 %collective-permute-done.5 = bf16[384,2,192]{0,2,1:T(8,128)(2,1)S(1)} collective-permute-done((bf16[384,2,192]{0,2,1:T(8,128)(2,1)S(1)}, bf16[384,2,192]{0,2,1:T(8,128)(2,1)S(1)}, u32[]{:S(2)}, u32[]{:S(2)}) %collective-permute-start.5) | collective-permute-done | bytes 294944 | tf_op jit(solution)/shard_map/ppermute | solution.py:63
  86.8 3.4 %collective-permute-start.6 = (bf16[768,2,192]{0,2,1:T(8,128)(2,1)S(1)}, bf16[768,2,192]{0,2,1:T(8,128)(2,1)S(1)}, u32[]{:S(2)}, u32[]{:S(2)}) collective-permute-start(bf16[768,2,192]{0,2,1:T(8,128)(2,1)S(1)} %pad_maximum_fusion.2), channel_id=1, source_target_pairs={{0,2},{2,4},{4,6},{6,0},{1,3},{3,5},{5,7},{7,1},{8,10},{10,12},{12... | collective-permute-start | bytes 1769480 | tf_op jit(solution)/shard_map/ppermute | solution.py:69
  90.4 2.4 %collective-permute-start.8 = (bf16[768,2,192]{0,2,1:T(8,128)(2,1)S(1)}, bf16[768,2,192]{0,2,1:T(8,128)(2,1)S(1)}, u32[]{:S(2)}, u32[]{:S(2)}) collective-permute-start(bf16[768,2,192]{0,2,1:T(8,128)(2,1)S(1)} %pad_maximum_fusion.3), channel_id=1, source_target_pairs={{0,6},{2,0},{4,2},{6,4},{1,7},{3,1},{5,3},{7,5},{8,14},{10,8},{12,... | collective-permute-start | bytes 1769480 | tf_op jit(solution)/shard_map/ppermute | solution.py:70
  92.9 10.4 %collective-permute-done.6 = bf16[768,2,192]{0,2,1:T(8,128)(2,1)S(1)} collective-permute-done((bf16[768,2,192]{0,2,1:T(8,128)(2,1)S(1)}, bf16[768,2,192]{0,2,1:T(8,128)(2,1)S(1)}, u32[]{:S(2)}, u32[]{:S(2)}) %collective-permute-start.6) | collective-permute-done | bytes 589856 | tf_op jit(solution)/shard_map/ppermute | solution.py:69
  103.2 4.8 %collective-permute-done.8 = bf16[768,2,192]{0,2,1:T(8,128)(2,1)S(1)} collective-permute-done((bf16[768,2,192]{0,2,1:T(8,128)(2,1)S(1)}, bf16[768,2,192]{0,2,1:T(8,128)(2,1)S(1)}, u32[]{:S(2)}, u32[]{:S(2)}) %collective-permute-start.8) | collective-permute-done | bytes 589856 | tf_op jit(solution)/shard_map/ppermute | solution.py:70
  108.0 1.4 %fusion.1 = f32[768,2,192]{0,2,1:T(8,128)S(1)} fusion(bf16[768,2,192]{0,2,1:T(8,128)(2,1)S(1)} %collective-permute-done.8, bf16[768,2,192]{0,2,1:T(8,128)(2,1)S(1)} %collective-permute-done.6, f32[768,2,4,192]{0,3,2,1:T(8,128)} %copy-done.3, s32[]{:T(128)S(6)} %select_n.82), kind=kLoop, calls=%fused_computation.10 | loop fusion | flops 1179648 | bytes 3538948 | tf_op jit(solution)/shard_map/add | solution.py:71
  109.5 9.1 %collective-permute-start.9 = (bf16[768,192]{0,1:T(8,128)(2,1)S(1)}, bf16[768,192]{0,1:T(8,128)(2,1)S(1)}, u32[]{:S(2)}, u32[]{:S(2)}) collective-permute-start(bf16[768,192]{0,1:T(8,128)(2,1)S(1)} %fusion.15), channel_id=1, source_target_pairs={{0,8},{8,0},{1,9},{9,1},{2,10},{10,2},{3,11},{11,3},{4,12},{12,4},... | collective-permute-start | bytes 884744 | tf_op jit(solution)/shard_map/ppermute | solution.py:87
  118.6 19.2 %collective-permute-done.9 = bf16[768,192]{0,1:T(8,128)(2,1)S(1)} collective-permute-done((bf16[768,192]{0,1:T(8,128)(2,1)S(1)}, bf16[768,192]{0,1:T(8,128)(2,1)S(1)}, u32[]{:S(2)}, u32[]{:S(2)}) %collective-permute-start.9) | collective-permute-done | bytes 294944 | tf_op jit(solution)/shard_map/ppermute | solution.py:87
  (44 shorter events, 10.9 us)
Async XLA Ops:
  1.1 12.7 %collective-permute-start = (bf16[2,768,128]{2,1,0:T(8,128)(2,1)S(1)}, bf16[2,768,128]{2,1,0:T(8,128)(2,1)S(1)}, u32[]{:S(2)}, u32[]{:S(2)}) collective-permute-start(bf16[2,768,128]{2,1,0:T(8,128)(2,1)S(1)} %pad_maximum_fusion.4), channel_id=1, source_target_pairs={{0,16},{16,32},{32,48},{48,64},{64,80},{80,96},{96,112},{112,128},... | collective-permute-start | bytes 1179656 | tf_op jit(solution)/shard_map/ppermute | solution.py:21
  5.3 21.5 %collective-permute-start.1 = (bf16[2,768,128]{2,1,0:T(8,128)(2,1)S(1)}, bf16[2,768,128]{2,1,0:T(8,128)(2,1)S(1)}, u32[]{:S(2)}, u32[]{:S(2)}) collective-permute-start(bf16[2,768,128]{2,1,0:T(8,128)(2,1)S(1)} %pad_maximum_fusion.4), channel_id=1, source_target_pairs={{16,0},{32,16},{48,32},{64,48},{80,64},{96,80},{112,96},{128,112},... | collective-permute-start | bytes 1179656 | tf_op jit(solution)/shard_map/ppermute | solution.py:23
  28.0 0.9 copy-start
  28.0 1.0 copy-start.1
  28.0 1.1 copy-start.2
  37.7 14.6 %collective-permute-start.2 = (bf16[2,768,1,128]{3,1,2,0:T(8,128)(2,1)}, bf16[2,768,1,128]{3,1,2,0:T(8,128)(2,1)S(1)}, u32[]{:S(2)}, u32[]{:S(2)}) collective-permute-start(bf16[2,768,1,128]{3,1,2,0:T(8,128)(2,1)} %get-tuple-element.21), channel_id=1, source_target_pairs={{16,0},{32,16},{48,32},{64,48},{80,64},{96,80},{112,96},{128,112},... | collective-permute-start | bytes 1179656 | tf_op jit(solution)/shard_map/ppermute | solution.py:32
  39.6 25.8 %collective-permute-start.3 = (bf16[2,768,1,128]{3,1,2,0:T(8,128)(2,1)}, bf16[2,768,1,128]{3,1,2,0:T(8,128)(2,1)S(1)}, u32[]{:S(2)}, u32[]{:S(2)}) collective-permute-start(bf16[2,768,1,128]{3,1,2,0:T(8,128)(2,1)} %get-tuple-element.22), channel_id=1, source_target_pairs={{752,0},{0,16},{16,32},{32,48},{48,64},{64,80},{80,96},{96,112},{1... | collective-permute-start | bytes 1179656 | tf_op jit(solution)/shard_map/ppermute | solution.py:32
  68.4 6.6 %collective-permute-start.4 = (bf16[768,2,4,192]{0,3,2,1:T(8,128)(2,1)}, bf16[768,2,4,192]{0,3,2,1:T(8,128)(2,1)S(1)}, u32[]{:S(2)}, u32[]{:S(2)}) collective-permute-start(bf16[768,2,4,192]{0,3,2,1:T(8,128)(2,1)} %bitcast_convert_fusion), channel_id=1, source_target_pairs={{0,1},{1,0},{2,3},{3,2},{4,5},{5,4},{6,7},{7,6},{8,9},{9,8},{10,11... | collective-permute-start | bytes 7077896 | tf_op jit(solution)/shard_map/ppermute | solution.py:233
  75.6 14.7 %copy-start.3 = (f32[768,2,4,192]{0,3,2,1:T(8,128)}, f32[768,2,4,192]{0,3,2,1:T(8,128)S(1)}, u32[]{:S(2)}) copy-start(f32[768,2,4,192]{0,3,2,1:T(8,128)S(1)} %convert_add_fusion) | copy-start | bytes 14155780
  75.8 10.9 %collective-permute-start.5 = (bf16[384,2,192]{0,2,1:T(8,128)(2,1)S(1)}, bf16[384,2,192]{0,2,1:T(8,128)(2,1)S(1)}, u32[]{:S(2)}, u32[]{:S(2)}) collective-permute-start(bf16[384,2,192]{0,2,1:T(8,128)(2,1)S(1)} %get-tuple-element.25), channel_id=1, source_target_pairs={{0,2},{2,4},{4,6},{6,0},{1,3},{3,5},{5,7},{7,1},{8,10},{10,12},{12... | collective-permute-start | bytes 884744 | tf_op jit(solution)/shard_map/ppermute | solution.py:63
  77.7 12.6 %collective-permute-start.7 = (bf16[384,2,192]{0,2,1:T(8,128)(2,1)S(1)}, bf16[384,2,192]{0,2,1:T(8,128)(2,1)S(1)}, u32[]{:S(2)}, u32[]{:S(2)}) collective-permute-start(bf16[384,2,192]{0,2,1:T(8,128)(2,1)S(1)} %get-tuple-element.26), channel_id=1, source_target_pairs={{0,6},{2,0},{4,2},{6,4},{1,7},{3,1},{5,3},{7,5},{8,14},{10,8},{12,... | collective-permute-start | bytes 884744 | tf_op jit(solution)/shard_map/ppermute | solution.py:64
  86.8 16.4 %collective-permute-start.6 = (bf16[768,2,192]{0,2,1:T(8,128)(2,1)S(1)}, bf16[768,2,192]{0,2,1:T(8,128)(2,1)S(1)}, u32[]{:S(2)}, u32[]{:S(2)}) collective-permute-start(bf16[768,2,192]{0,2,1:T(8,128)(2,1)S(1)} %pad_maximum_fusion.2), channel_id=1, source_target_pairs={{0,2},{2,4},{4,6},{6,0},{1,3},{3,5},{5,7},{7,1},{8,10},{10,12},{12... | collective-permute-start | bytes 1769480 | tf_op jit(solution)/shard_map/ppermute | solution.py:69
  90.4 17.6 %collective-permute-start.8 = (bf16[768,2,192]{0,2,1:T(8,128)(2,1)S(1)}, bf16[768,2,192]{0,2,1:T(8,128)(2,1)S(1)}, u32[]{:S(2)}, u32[]{:S(2)}) collective-permute-start(bf16[768,2,192]{0,2,1:T(8,128)(2,1)S(1)} %pad_maximum_fusion.3), channel_id=1, source_target_pairs={{0,6},{2,0},{4,2},{6,4},{1,7},{3,1},{5,3},{7,5},{8,14},{10,8},{12,... | collective-permute-start | bytes 1769480 | tf_op jit(solution)/shard_map/ppermute | solution.py:70
  109.5 28.3 %collective-permute-start.9 = (bf16[768,192]{0,1:T(8,128)(2,1)S(1)}, bf16[768,192]{0,1:T(8,128)(2,1)S(1)}, u32[]{:S(2)}, u32[]{:S(2)}) collective-permute-start(bf16[768,192]{0,1:T(8,128)(2,1)S(1)} %fusion.15), channel_id=1, source_target_pairs={{0,8},{8,0},{1,9},{9,1},{2,10},{10,2},{3,11},{11,3},{4,12},{12,4},... | collective-permute-start | bytes 884744 | tf_op jit(solution)/shard_map/ppermute | solution.py:87
